TPU v7x, 32 devices: a whole 2x2x4 slice. The times are simulated.
32 devices in a mesh: gy: 4 (over x, core), gx: 8 (over z, y).
Axes of the slice: x: 2, y: 2, z: 4, core: 2. Of those that a mesh axis runs over, the one named last changes fastest.
Arguments:
- tokens: bfloat16 [32, 128, 384], P('gy', 'gx'), may hold values from -6 to 6
- w_qkv: bfloat16 [384, 1152], replicated, may hold values from -1 to 1
- w_out: bfloat16 [384, 384], replicated, may hold values from -0.3125 to 0.3125
- block_mask: int32 [4, 16], P('gy', 'gx'), may hold values from 0 to 1, as said below
- grad_out: bfloat16 [32, 128, 384], P('gy', 'gx'), may hold values from -6 to 6
Outputs:
- mixed: bfloat16 [32, 128, 384], P('gy', 'gx')
- d_tokens: bfloat16 [32, 128, 384], P('gy', 'gx')
Inputs may be any that keep to these rules, and one draw needn't show every extreme that they name: `block_mask`: 1 marks a tissue block, 0 background.
All inputs are finite; a program needn't handle non-finite values.
Results may differ from a plain program's by a relative error of at most 0.017.
Values may be sent and summed in bfloat16 or wider, within the bound.
No kernel may reach another device: no remote copies, remote signals or barrier semaphores. Data moves between devices by JAX's collectives and lax.ppermute only.
A program may use at most 64 MiB of HBM per device.

v0:
```python
import jax
import jax.numpy as jnp
from jax import lax
from jax.sharding import PartitionSpec as P

NH = 6
HEAD_SIZE = 64
KS = 7
TISSUE_BLOCK = 8


NEG_FILL = -1e30


def with_halo(x, sides, width):
    for axis, dim in sides:
        size, length = (lax.axis_size(axis), x.shape[dim])
        up = [(i, (i + 1) % size) for i in range(size - 1)]
        down = [(j, i) for i, j in up]
        last = lax.slice_in_dim(x, length - width, length, axis=dim)
        first = lax.slice_in_dim(x, 0, width, axis=dim)
        before = lax.ppermute(last, axis, up)
        after = lax.ppermute(first, axis, down)
        x = jnp.concatenate([before, x, after], axis=dim)
    return x


def from_behind(value, axis, steps):
    count = lax.axis_size(axis)
    first, last = (max(0, -steps), min(count, count - steps))
    return lax.ppermute(value, axis, [(source, source + steps) for source in range(first, last)])


def block_means(field):
    tile_rows, tile_cols, width = field.shape
    grouped = field.astype(jnp.float32).reshape(
        tile_rows // TISSUE_BLOCK, TISSUE_BLOCK, tile_cols // TISSUE_BLOCK, TISSUE_BLOCK, width
    )
    return (jnp.sum(grouped, axis=(1, 3)) / TISSUE_BLOCK).reshape(-1, width)


def spread_blocks(blocks, tile_rows, tile_cols):
    shaped = blocks.reshape(tile_rows // TISSUE_BLOCK, tile_cols // TISSUE_BLOCK, -1)
    return jnp.repeat(jnp.repeat(shaped, TISSUE_BLOCK, 0), TISSUE_BLOCK, 1).reshape(
        tile_rows * tile_cols, -1
    )


def moving_window(extended, row_start, col_start, tile_rows, tile_cols):
    starts = (row_start, col_start) + tuple((0 for _ in extended.shape[2:]))
    extent = (tile_rows, tile_cols) + tuple(extended.shape[2:])
    return lax.dynamic_slice(extended, starts, extent)


def local(tokens, w_qkv, w_out, block_mask, grad_out):
    tile_rows, tile_cols, width = tokens.shape
    reachable_cells = KS // 2
    position_total = KS * KS
    token_count = tile_rows * tile_cols
    score_scale = HEAD_SIZE ** (-0.5)
    flat_tokens = tokens.reshape(token_count, width)
    qkv = jnp.dot(flat_tokens, w_qkv, preferred_element_type=jnp.float32).astype(jnp.bfloat16)
    query = qkv[:, :width].reshape(tile_rows, tile_cols, width)
    keys = qkv[:, width : 2 * width].reshape(tile_rows, tile_cols, width)
    values = qkv[:, 2 * width :].reshape(tile_rows, tile_cols, width)
    token_flag = spread_blocks(block_mask.astype(jnp.float32), tile_rows, tile_cols)
    row_place = (
        lax.axis_index("gy") * tile_rows
        + jnp.arange(tile_rows + 2 * reachable_cells)
        - reachable_cells
    )
    col_place = (
        lax.axis_index("gx") * tile_cols
        + jnp.arange(tile_cols + 2 * reachable_cells)
        - reachable_cells
    )
    row_inside = (row_place >= 0) & (row_place < tile_rows * lax.axis_size("gy"))
    col_inside = (col_place >= 0) & (col_place < tile_cols * lax.axis_size("gx"))
    inside = row_inside[:, None] & col_inside[None, :]

    def window(extended, position):
        return moving_window(extended, position // KS, position % KS, tile_rows, tile_cols)

    pooled_keys = block_means(keys).astype(jnp.bfloat16)
    pooled_vals = block_means(values).astype(jnp.bfloat16)
    pool_flag = block_mask.reshape(-1).astype(jnp.bfloat16)
    kv_ext = with_halo(
        jnp.concatenate([keys, values], axis=2), (("gy", 0), ("gx", 1)), reachable_cells
    )
    row_keys, row_vals, row_flag = (
        lax.all_gather(pooled_keys, "gx", axis=0, tiled=True),
        lax.all_gather(pooled_vals, "gx", axis=0, tiled=True),
        lax.all_gather(pool_flag, "gx", axis=0, tiled=True),
    )
    col_keys, col_vals, col_flag = (
        lax.all_gather(pooled_keys, "gy", axis=0, tiled=True),
        lax.all_gather(pooled_vals, "gy", axis=0, tiled=True),
        lax.all_gather(pool_flag, "gy", axis=0, tiled=True),
    )
    query_heads = query.reshape(token_count, NH, HEAD_SIZE)

    def score_step(position, collected):
        key_win = window(kv_ext, position)[:, :, :width].reshape(token_count, NH, HEAD_SIZE)
        scores = (
            jnp.einsum("tnd,tnd->nt", query_heads, key_win, preferred_element_type=jnp.float32)
            * score_scale
        )
        valid = window(inside, position).reshape(token_count)
        masked = jnp.where(valid[None, :], scores, NEG_FILL)
        return lax.dynamic_update_index_in_dim(collected, masked, position, 0)

    local_s = lax.fori_loop(
        0, position_total, score_step, jnp.zeros((position_total, NH, token_count), jnp.float32)
    )

    def pool_scores(pool_keys, flags):
        scores = (
            jnp.einsum(
                "tnd,pnd->ntp",
                query_heads,
                pool_keys.reshape(-1, NH, HEAD_SIZE),
                preferred_element_type=jnp.float32,
            )
            * score_scale
        )
        return jnp.where(flags[None, None, :] > 0, scores, NEG_FILL)

    row_s = pool_scores(row_keys, row_flag)
    col_s = pool_scores(col_keys, col_flag)
    top = jnp.maximum(jnp.maximum(jnp.max(local_s, 0), jnp.max(row_s, -1)), jnp.max(col_s, -1))
    total = (
        jnp.sum(jnp.exp(local_s - top), 0)
        + jnp.sum(jnp.exp(row_s - top[:, :, None]), -1)
        + jnp.sum(jnp.exp(col_s - top[:, :, None]), -1)
    )
    lse = top + jnp.log(total)
    local_probs = jnp.exp(local_s - lse)
    row_pf = jnp.exp(row_s - lse[:, :, None])
    col_pf = jnp.exp(col_s - lse[:, :, None])
    row_ph = row_pf.astype(jnp.bfloat16)
    col_ph = col_pf.astype(jnp.bfloat16)

    def value_step(position, output):
        value_win = window(kv_ext, position)[:, :, width:].reshape(token_count, NH, HEAD_SIZE)
        probs = lax.dynamic_index_in_dim(local_probs, position, 0, keepdims=False)
        return output + probs.T[:, :, None] * value_win

    output = lax.fori_loop(
        0, position_total, value_step, jnp.zeros((token_count, NH, HEAD_SIZE), jnp.float32)
    )
    output = output + jnp.einsum(
        "ntp,pnd->tnd",
        row_ph,
        row_vals.reshape(-1, NH, HEAD_SIZE),
        preferred_element_type=jnp.float32,
    )
    output = output + jnp.einsum(
        "ntp,pnd->tnd",
        col_ph,
        col_vals.reshape(-1, NH, HEAD_SIZE),
        preferred_element_type=jnp.float32,
    )
    attended = output.reshape(token_count, width).astype(jnp.bfloat16)
    gated = attended * token_flag.astype(jnp.bfloat16)
    mixed = (
        flat_tokens.astype(jnp.float32) + jnp.dot(gated, w_out, preferred_element_type=jnp.float32)
    ).astype(jnp.bfloat16)
    grad_flat = grad_out.reshape(token_count, width)
    d_att = (
        jnp.einsum("tc,ec->te", grad_flat, w_out, preferred_element_type=jnp.float32) * token_flag
    ).astype(jnp.bfloat16)
    datt_heads = d_att.reshape(token_count, NH, HEAD_SIZE)
    delta = jnp.einsum(
        "tnd,tnd->nt",
        datt_heads,
        attended.reshape(token_count, NH, HEAD_SIZE),
        preferred_element_type=jnp.float32,
    )

    def pool_backward(prob_full, prob_half, pool_keys, pool_vals):
        key_heads = pool_keys.reshape(-1, NH, HEAD_SIZE)
        value_heads = pool_vals.reshape(-1, NH, HEAD_SIZE)
        prob_grad = jnp.einsum(
            "tnd,pnd->ntp", datt_heads, value_heads, preferred_element_type=jnp.float32
        )
        score_grad = (prob_full * (prob_grad - delta[:, :, None])).astype(jnp.bfloat16)
        query_part = (
            jnp.einsum("ntp,pnd->tnd", score_grad, key_heads, preferred_element_type=jnp.float32)
            * score_scale
        )
        key_part = (
            jnp.einsum("ntp,tnd->pnd", score_grad, query_heads, preferred_element_type=jnp.float32)
            * score_scale
        )
        value_part = jnp.einsum(
            "ntp,tnd->pnd", prob_half, datt_heads, preferred_element_type=jnp.float32
        )
        return (query_part, key_part.reshape(-1, width), value_part.reshape(-1, width))

    row_dq, row_dk, row_dv = pool_backward(row_pf, row_ph, row_keys, row_vals)
    col_dq, col_dk, col_dv = pool_backward(col_pf, col_ph, col_keys, col_vals)
    block_count = pooled_keys.shape[0]
    whole_row_dk, whole_row_dv = (
        lax.psum(row_dk.astype(jnp.bfloat16), "gx").astype(jnp.float32),
        lax.psum(row_dv.astype(jnp.bfloat16), "gx").astype(jnp.float32),
    )
    whole_col_dk, whole_col_dv = (
        lax.psum(col_dk.astype(jnp.bfloat16), "gy").astype(jnp.float32),
        lax.psum(col_dv.astype(jnp.bfloat16), "gy").astype(jnp.float32),
    )
    row_start = lax.axis_index("gx") * block_count
    col_start = lax.axis_index("gy") * block_count
    own_row_dk = lax.dynamic_slice_in_dim(whole_row_dk, row_start, block_count, 0)
    own_row_dv = lax.dynamic_slice_in_dim(whole_row_dv, row_start, block_count, 0)
    own_col_dk = lax.dynamic_slice_in_dim(whole_col_dk, col_start, block_count, 0)
    own_col_dv = lax.dynamic_slice_in_dim(whole_col_dv, col_start, block_count, 0)

    def query_step(position, grad_query):
        both_win = window(kv_ext, position)
        key_win = both_win[:, :, :width].reshape(token_count, NH, HEAD_SIZE)
        value_win = both_win[:, :, width:].reshape(token_count, NH, HEAD_SIZE)
        prob_grad = jnp.einsum(
            "tnd,tnd->nt", datt_heads, value_win, preferred_element_type=jnp.float32
        )
        probs = lax.dynamic_index_in_dim(local_probs, position, 0, keepdims=False)
        score_grad = probs * (prob_grad - delta)
        return grad_query + (score_grad.T[:, :, None] * key_win * score_scale).reshape(
            token_count, width
        )

    grad_query = lax.fori_loop(
        0, position_total, query_step, (row_dq + col_dq).reshape(token_count, width)
    )

    def return_step(position, ext_grad):
        both_win = window(kv_ext, position)
        value_win = both_win[:, :, width:].reshape(token_count, NH, HEAD_SIZE)
        prob_grad = jnp.einsum(
            "tnd,tnd->nt", datt_heads, value_win, preferred_element_type=jnp.float32
        )
        probs = lax.dynamic_index_in_dim(local_probs, position, 0, keepdims=False)
        score_grad = probs * (prob_grad - delta)
        key_term = (score_grad.T[:, :, None] * query_heads * score_scale).reshape(
            tile_rows, tile_cols, width
        )
        value_term = (probs.T[:, :, None] * datt_heads).reshape(tile_rows, tile_cols, width)
        updated = window(ext_grad, position) + jnp.concatenate([key_term, value_term], axis=2)
        return lax.dynamic_update_slice(ext_grad, updated, (position // KS, position % KS, 0))

    ext_grad = lax.fori_loop(
        0,
        position_total,
        return_step,
        jnp.zeros(
            (tile_rows + 2 * reachable_cells, tile_cols + 2 * reachable_cells, 2 * width),
            jnp.float32,
        ),
    )
    col_moves = (
        (-1, slice(0, reachable_cells), slice(tile_cols, tile_cols + reachable_cells)),
        (
            1,
            slice(tile_cols + reachable_cells, tile_cols + 2 * reachable_cells),
            slice(reachable_cells, 2 * reachable_cells),
        ),
    )
    for step_by, source_span, target_span in col_moves:
        arrived = from_behind(ext_grad[:, source_span].astype(jnp.bfloat16), "gx", step_by).astype(
            jnp.float32
        )
        ext_grad = ext_grad.at[:, target_span].add(arrived)
    ext_grad = ext_grad[:, reachable_cells : reachable_cells + tile_cols]
    row_moves = (
        (-1, slice(0, reachable_cells), slice(tile_rows, tile_rows + reachable_cells)),
        (
            1,
            slice(tile_rows + reachable_cells, tile_rows + 2 * reachable_cells),
            slice(reachable_cells, 2 * reachable_cells),
        ),
    )
    for step_by, source_span, target_span in row_moves:
        arrived = from_behind(ext_grad[source_span].astype(jnp.bfloat16), "gy", step_by).astype(
            jnp.float32
        )
        ext_grad = ext_grad.at[target_span].add(arrived)
    own_grad = ext_grad[reachable_cells : reachable_cells + tile_rows].reshape(
        token_count, 2 * width
    )
    grad_keys = own_grad[:, :width]
    grad_vals = own_grad[:, width:]
    grad_keys = grad_keys + spread_blocks(
        (own_row_dk + own_col_dk) / TISSUE_BLOCK, tile_rows, tile_cols
    )
    grad_vals = grad_vals + spread_blocks(
        (own_row_dv + own_col_dv) / TISSUE_BLOCK, tile_rows, tile_cols
    )
    d_qkv = jnp.concatenate([grad_query, grad_keys, grad_vals], axis=1).astype(jnp.bfloat16)
    d_tokens = (
        grad_flat.astype(jnp.float32)
        + jnp.einsum("tf,cf->tc", d_qkv, w_qkv, preferred_element_type=jnp.float32)
    ).astype(jnp.bfloat16)
    return (
        mixed.reshape(tile_rows, tile_cols, width),
        d_tokens.reshape(tile_rows, tile_cols, width),
    )


def solution(mesh):
    placed = (P("gy", "gx", None), P(), P(), P("gy", "gx"), P("gy", "gx", None))
    return jax.shard_map(
        local,
        mesh=mesh,
        in_specs=placed,
        out_specs=(P("gy", "gx", None), P("gy", "gx", None)),
        check_vma=False,
    )
```

profile of v0, /device:TPU:1, one launch (start us, length us, event | category | flops | bytes accessed | tf_op | source)
XLA Modules:
  0.0 717.1 jit_solution(2901687024737776675)
XLA Ops:
  3.1 4.5 collective-permute-start
  9.6 21.7 %all-gather.2 = bf16[8,2,384]{2,1,0:T(2,128)(2,1)S(1)} all-gather(bf16[1,2,384]{2,1,0:T(2,128)(2,1)S(1)} %fusion.49), channel_id=1, replica_groups=mesh['gy'=4,'gx'=8] {'gx'}, dimensions={0}, use_global_device_ids=true | all-gather | bytes 13824 | tf_op jit(solution)/shard_map/all_gather | solution.py:91
  31.3 9.7 %all-gather.3 = bf16[4,2,384]{2,1,0:T(2,128)(2,1)S(1)} all-gather(bf16[1,2,384]{2,1,0:T(2,128)(2,1)S(1)} %fusion.49), channel_id=1, replica_groups=mesh['gy'=4,'gx'=8] {'gy'}, dimensions={0}, use_global_device_ids=true | all-gather | bytes 7680 | tf_op jit(solution)/shard_map/all_gather | solution.py:96
  44.1 16.2 %all-reduce = bf16[16]{0:T(256)(128)(2,1)S(1)} all-reduce(bf16[16]{0:T(256)(128)(2,1)S(1)} %dynamic-update-slice.12), channel_id=2, replica_groups=mesh['gy'=4,'gx'=8] {'gx'}, use_global_device_ids=true, to_apply=%add | all-reduce | flops 16 | bytes 64
  62.5 9.3 %all-reduce.1 = bf16[8]{0:T(256)(128)(2,1)S(1)} all-reduce(bf16[8]{0:T(256)(128)(2,1)S(1)} %dynamic-update-slice.13), channel_id=3, replica_groups=mesh['gy'=4,'gx'=8] {'gy'}, use_global_device_ids=true, to_apply=%add.1 | all-reduce | flops 8 | bytes 32
  77.0 21.3 %all-gather.4 = bf16[8,2,384]{2,1,0:T(2,128)(2,1)S(1)} all-gather(bf16[1,2,384]{2,1,0:T(2,128)(2,1)S(1)} %fusion.50), channel_id=1, replica_groups=mesh['gy'=4,'gx'=8] {'gx'}, dimensions={0}, use_global_device_ids=true | all-gather | bytes 13824 | tf_op jit(solution)/shard_map/all_gather | solution.py:92
  98.4 9.9 %all-gather.5 = bf16[4,2,384]{2,1,0:T(2,128)(2,1)S(1)} all-gather(bf16[1,2,384]{2,1,0:T(2,128)(2,1)S(1)} %fusion.50), channel_id=1, replica_groups=mesh['gy'=4,'gx'=8] {'gy'}, dimensions={0}, use_global_device_ids=true | all-gather | bytes 7680 | tf_op jit(solution)/shard_map/all_gather | solution.py:97
  110.5 37.0 %while.65 = (s32[]{:T(128)}, f32[49,6,128]{2,1,0:T(8,128)S(1)}, pred[14,22]{1,0:T(8,128)(4,1)S(1)}, bf16[14,22,768]{2,1,0:T(8,128)(2,1)S(1)}, bf16[128,6,64]{2,1...) while((s32[]{:T(128)}, f32[49,6,128]{2,1,0:T(8,128)S(1)}, ...), condition=%wide.region_1.0_spmd, body=%wide.region_0.0_spmd.sunk | while | flops 197396 | bytes 608564 | solution.py:112
  150.2 4.1 exp.21
  154.3 68.9 %while.68 = (s32[]{:T(128)}, f32[128,6,64]{2,1,0:T(8,128)S(1)}, f32[49,6,128]{1,2,0:T(8,128)}, bf16[14,22,768]{2,1,0:T(8,128)(2,1)S(1)}, s32[]{:T(128)}, /*index...) while((s32[]{:T(128)}, f32[128,6,64]{2,1,0:T(8,128)S(1)}, ...), condition=%wide.region_10.11_spmd.clone, body=%wide.region_9.10_spmd.clone.sunk | while | flops 196630 | bytes 1287498 | solution.py:148
  228.7 43.8 %while.66 = (s32[]{:T(128)}, f32[128,384]{0,1:T(8,128)S(1)}, f32[49,6,128]{2,1,0:T(8,128)S(1)}, bf16[14,22,768]{2,1,0:T(8,128)(2,1)S(1)}, bf16[128,6,64]{2,1,0:T...) while((s32[]{:T(128)}, f32[128,384]{0,1:T(8,128)S(1)}, ...), condition=%wide.region_13.14_spmd, body=%wide.region_12.13_spmd.sunk | while | flops 394005 | bytes 2089296 | solution.py:231
  273.5 362.1 %while.67 = (s32[]{:T(128)}, f32[14,22,768]{2,1,0:T(8,128)}, f32[49,6,128]{1,2,0:T(8,128)}, bf16[14,22,768]{2,1,0:T(8,128)(2,1)S(1)}, bf16[128,6,64]{2,1,0:T(8,1...) while((s32[]{:T(128)}, f32[14,22,768]{2,1,0:T(8,128)}, ...), condition=%wide.region_15.16_spmd, body=%wide.region_14.15_spmd.sunk | while | flops 639765 | bytes 3960160 | solution.py:250
  277.5 3.5 dynamic_update_slice.25
  284.9 3.5 dynamic_update_slice.25
  292.3 3.5 dynamic_update_slice.25
  299.8 3.5 dynamic_update_slice.25
  307.2 3.5 dynamic_update_slice.25
  314.6 3.5 dynamic_update_slice.25
  322.1 3.5 dynamic_update_slice.25
  329.5 3.5 dynamic_update_slice.25
  336.9 3.5 dynamic_update_slice.25
  344.4 3.5 dynamic_update_slice.25
  351.8 3.5 dynamic_update_slice.25
  359.2 3.5 dynamic_update_slice.25
  366.7 3.5 dynamic_update_slice.25
  374.1 3.5 dynamic_update_slice.25
  381.5 3.5 dynamic_update_slice.25
  389.0 3.5 dynamic_update_slice.25
  396.4 3.5 dynamic_update_slice.25
  403.8 3.5 dynamic_update_slice.25
  411.3 3.5 dynamic_update_slice.25
  418.7 3.5 dynamic_update_slice.25
  426.1 3.5 dynamic_update_slice.25
  433.5 3.5 dynamic_update_slice.25
  441.0 3.5 dynamic_update_slice.25
  448.4 3.5 dynamic_update_slice.25
  455.8 3.5 dynamic_update_slice.25
  463.3 3.5 dynamic_update_slice.25
  470.7 3.5 dynamic_update_slice.25
  478.1 3.5 dynamic_update_slice.25
  485.6 3.4 dynamic_update_slice.25
  492.9 3.4 dynamic_update_slice.25
  647.5 3.4 collective-permute-start.5
  653.5 3.5 scatter-add.15
  657.9 3.8 collective-permute-start.6
  663.3 28.1 %all-reduce.2 = (bf16[16,384]{1,0:T(8,128)(2,1)S(1)}, bf16[16,384]{1,0:T(8,128)(2,1)S(1)}) all-reduce(bf16[16,384]{1,0:T(8,128)(2,1)S(1)} %convert_element_type.237, bf16[16,384]{1,0:T(8,128)(2,1)S(1)} %convert_element_type.229), channel_id=1, replica_groups=mesh['gy'=4,'gx'=8] {'gx'}, use_global_device_ids=true, to_apply=%region_18.19 | all-reduce | flops 12288 | bytes 49152 | tf_op jit(solution)/shard_map/psum | solution.py:205
  691.5 16.6 %all-reduce.3 = (bf16[8,384]{1,0:T(8,128)(2,1)S(1)}, bf16[8,384]{1,0:T(8,128)(2,1)S(1)}) all-reduce(bf16[8,384]{1,0:T(8,128)(2,1)S(1)} %convert_element_type.241, bf16[8,384]{1,0:T(8,128)(2,1)S(1)} %convert_element_type.233), channel_id=1, replica_groups=mesh['gy'=4,'gx'=8] {'gy'}, use_global_device_ids=true, to_apply=%region_19.20 | all-reduce | flops 6144 | bytes 24576 | tf_op jit(solution)/shard_map/psum | solution.py:209
  710.3 4.2 collective-permute-start.7
  (1505 shorter events, 440.8 us)
Async XLA Ops:
  0.6 1.2 copy-start
  0.6 71.7 %copy-start.2 = (bf16[384,384]{1,0:T(8,128)(2,1)S(1)}, bf16[384,384]{1,0:T(8,128)(2,1)}, u32[]{:S(2)}) copy-start(bf16[384,384]{1,0:T(8,128)(2,1)} %param.23) | copy-start | bytes 884740
  3.1 70.4 %collective-permute-start = (bf16[3,16,768]{2,1,0:T(8,128)(2,1)S(1)}, bf16[3,16,768]{2,1,0:T(8,128)(2,1)S(1)}, u32[]{:S(2)}, u32[]{:S(2)}) collective-permute-start(bf16[3,16,768]{2,1,0:T(8,128)(2,1)S(1)} %get-tuple-element.772), channel_id=1, source_target_pairs={{0,8},{8,16},{16,24},{1,9},{9,17},{17,25},{2,10},{10,18},{18,26},{... | collective-permute-start | bytes 221192 | tf_op jit(solution)/shard_map/ppermute | solution.py:22
  7.6 65.9 %collective-permute-start.1 = (bf16[3,16,768]{2,1,0:T(8,128)(2,1)S(1)}, bf16[3,16,768]{2,1,0:T(8,128)(2,1)S(1)}, u32[]{:S(2)}, u32[]{:S(2)}) collective-permute-start(bf16[3,16,768]{2,1,0:T(8,128)(2,1)S(1)} %get-tuple-element.773), channel_id=1, source_target_pairs={{8,0},{16,8},{24,16},{9,1},{17,9},{25,17},{10,2},{18,10},{26,18},{... | collective-permute-start | bytes 221192 | tf_op jit(solution)/shard_map/ppermute | solution.py:23
  41.0 67.2 %copy-start.1 = (bf16[128,384]{0,1:T(8,128)(2,1)}, bf16[128,384]{0,1:T(8,128)(2,1)S(1)}, u32[]{:S(2)}) copy-start(bf16[128,384]{0,1:T(8,128)(2,1)S(1)} %copy.82) | copy-start | bytes 294916
  73.6 35.1 %collective-permute-start.2 = (bf16[14,3,768]{2,1,0:T(4,128)(2,1)S(1)}, bf16[14,3,768]{2,1,0:T(4,128)(2,1)S(1)}, u32[]{:S(2)}, u32[]{:S(2)}) collective-permute-start(bf16[14,3,768]{2,1,0:T(4,128)(2,1)S(1)} %get-tuple-element.767), channel_id=1, source_target_pairs={{0,1},{1,2},{2,3},{3,4},{4,5},{5,6},{6,7},{8,9},{9,10},{10,11},{11... | collective-permute-start | bytes 193544 | tf_op jit(solution)/shard_map/ppermute | solution.py:22
  74.9 34.5 %collective-permute-start.3 = (bf16[14,3,768]{2,1,0:T(4,128)(2,1)S(1)}, bf16[14,3,768]{2,1,0:T(4,128)(2,1)}, u32[]{:S(2)}, u32[]{:S(2)}) collective-permute-start(bf16[14,3,768]{2,1,0:T(4,128)(2,1)S(1)} %get-tuple-element.768), channel_id=1, source_target_pairs={{1,0},{2,1},{3,2},{4,3},{5,4},{6,5},{7,6},{9,8},{10,9},{11,10},{12... | collective-permute-start | bytes 193544 | tf_op jit(solution)/shard_map/ppermute | solution.py:23
  108.7 0.6 copy-start.8
  147.7 79.6 %copy-start.3 = (f32[6,128]{1,0:T(8,128)}, f32[6,128]{1,0:T(8,128)S(1)}, u32[]{:S(2)}) copy-start(f32[6,128]{1,0:T(8,128)S(1)} %log_add_fusion) | copy-start | bytes 9220
  224.6 4.1 copy-start.4
  224.8 4.0 copy-start.5
  635.7 27.3 %copy-start.7 = (bf16[16,6,64]{2,0,1:T(8,128)(2,1)S(1)}, bf16[16,6,64]{2,0,1:T(8,128)(2,1)}, u32[]{:S(2)}) copy-start(bf16[16,6,64]{2,0,1:T(8,128)(2,1)} %fusion.18) | copy-start | bytes 36868
  636.7 5.8 collective-permute-start.4
  641.8 74.2 %copy-start.6 = (bf16[8,16,384]{2,1,0:T(8,128)(2,1)S(1)}, bf16[8,16,384]{2,1,0:T(8,128)(2,1)}, u32[]{:S(2)}) copy-start(bf16[8,16,384]{2,1,0:T(8,128)(2,1)} %param.25) | copy-start | bytes 294916
  647.5 5.0 collective-permute-start.5
  657.9 51.4 %collective-permute-start.6 = (bf16[3,16,768]{2,1,0:T(8,128)(2,1)S(1)}, bf16[3,16,768]{2,1,0:T(8,128)(2,1)S(1)}, u32[]{:S(2)}, u32[]{:S(2)}) collective-permute-start(bf16[3,16,768]{2,1,0:T(8,128)(2,1)S(1)} %slice.252), channel_id=1, source_target_pairs={{8,0},{16,8},{24,16},{9,1},{17,9},{25,17},{10,2},{18,10},{26,18},{... | collective-permute-start | bytes 221192 | tf_op jit(solution)/shard_map/ppermute | solution.py:31
  710.3 5.6 collective-permute-start.7
where the time goes:
time: 731 us; the launch traced here: 717 us
  local copies, waits for them, and re-layouts  356 us (49%)
  other arithmetic  177 us (24%)
  blocking collectives  133 us (18%)
  starting transfers between devices  21.7 us (3%)
  loops' own time  13.3 us (2%)
  matrix products  11.1 us (2%)
    dynamic_update_slice x49, local copies, waits for them, and re-layouts, return_step(): lax.dynamic_update_slice(ext_grad, updated, (position // KS, position % K...  169 us
    add x49, other arithmetic, return_step(): window(ext_grad, position) + jnp.concatenate([key_term, value_term], axis=2)  55.9 us
    transpose x49, other arithmetic, return_step(): score_grad.T[:, :, None] * query_heads * score_scale  42.1 us
    transpose x49, local copies, waits for them, and re-layouts, value_step(): return output + probs.T[:, :, None] * value_win  41.7 us
    transpose x49, local copies, waits for them, and re-layouts, return_step(): probs.T[:, :, None] * datt_heads  41.7 us
    psum x1, blocking collectives, local(): lax.psum(row_dv.astype(jnp.bfloat16), 'gx').astype(jnp.float32)  28.1 us
    unnamed x2, blocking collectives  25.5 us
    all_gather x1, blocking collectives, local(): lax.all_gather(pooled_keys, 'gx', axis=0, tiled=True)  21.7 us
  transfers between devices with their start and end apart: 8, of which 3 were waited for; matrix products, arithmetic and copies ran while one was open for 2% of the time, Pallas kernels for 0%

commit v1 on v0

v1 whole, which is shorter than its diff:
```python
import functools

import jax
import jax.numpy as jnp
import numpy as np
from jax import lax
from jax.experimental import pallas as pl
from jax.experimental.pallas import tpu as pltpu
from jax.sharding import PartitionSpec as P

NH = 6
HEAD_SIZE = 64
KS = 7
TISSUE_BLOCK = 8
REACH = KS // 2
NEG_FILL = -1e30
LANES = 128


def pairs_low(count):
    return [(i, i ^ 1) for i in range(count)]


def pairs_odd(count, wrap):
    moves = []
    for i in range(count):
        j = (i + 1) % count if i % 2 else (i - 1) % count
        if wrap or abs(i - j) == 1:
            moves.append((i, j))
    return moves


def pairs_far(count, step):
    return [(i, i ^ step) for i in range(count)]


def window_pairs(count, step):
    moves = []
    for i in range(count):
        group, side = divmod((i - 1) % count, 2)
        moves.append((i, (2 * (group ^ step) + 1 + side) % count))
    return moves


def steps_above(count, first):
    steps = []
    while first < count:
        steps.append(first)
        first *= 2
    return steps


class Rows:
    def __init__(self, tile_rows, tile_cols, pooled):
        wide = tile_cols + 2 * REACH
        self.own = tile_rows * tile_cols
        self.side = tile_rows * REACH
        self.edge = REACH * wide
        self.left = self.own
        self.right = self.left + self.side
        self.up = self.right + self.side
        self.down = self.up + self.edge
        self.local = self.down + self.edge
        self.pool = -(-self.local // 16) * 16
        self.used = self.pool + pooled
        self.total = -(-self.used // LANES) * LANES


def band_table(rows, tile_rows, tile_cols):
    wide = tile_cols + 2 * REACH
    place = np.full((rows.total, 2), -1000, np.int64)
    own = np.stack(np.meshgrid(np.arange(tile_rows), np.arange(tile_cols), indexing="ij"), -1).reshape(-1, 2)
    side = np.stack(np.meshgrid(np.arange(tile_rows), np.arange(REACH), indexing="ij"), -1).reshape(-1, 2)
    edge = np.stack(np.meshgrid(np.arange(REACH), np.arange(wide), indexing="ij"), -1).reshape(-1, 2)
    place[: rows.own] = own
    place[rows.left : rows.right] = side + [0, -REACH]
    place[rows.right : rows.up] = side + [0, tile_cols]
    place[rows.up : rows.down] = edge + [-REACH, -REACH]
    place[rows.down : rows.local] = edge + [tile_rows, -REACH]
    near = (np.abs(place[:, None, :] - own[None, :, :]) <= REACH).all(-1)
    band = np.where(near, 0.0, NEG_FILL).astype(np.float32)
    cols = np.broadcast_to(place[:, 1:2], band.shape).astype(np.int32)
    return band, cols


def attention_kernel(
    rows, tile_cols, sizes,
    mask_ref, x_ref, flags_ref, band_ref, cols_ref, grad_ref, wqkv_ref, wout_ref,
    mixed_ref, back_ref, dkv_ref, att_ref, dq_ref,
):
    width = NH * HEAD_SIZE
    own = rows.own
    count_y, count_x = sizes
    iy, ix = lax.axis_index("gy"), lax.axis_index("gx")
    dot = functools.partial(lax.dot_general, preferred_element_type=jnp.float32)
    nn = (((1,), (0,)), ((), ()))
    nt = (((1,), (1,)), ((), ()))

    row_id = lax.broadcasted_iota(jnp.int32, (rows.total, own), 0)
    cols = cols_ref[...]
    local_row = row_id < rows.pool
    outside = (
        ((cols < 0) & (ix == 0) & local_row)
        | ((cols >= tile_cols) & (ix == count_x - 1))
        | ((row_id >= rows.up) & (row_id < rows.down) & (iy == 0))
        | ((row_id >= rows.down) & (row_id < rows.local) & (iy == count_y - 1))
    )
    bias = jnp.where(outside, NEG_FILL, band_ref[...])
    pooled = jnp.where(flags_ref[...] > 0, 0.0, NEG_FILL)
    bias = jnp.concatenate([bias[: rows.pool], pooled], axis=0)
    bias2 = jnp.concatenate([bias, bias], axis=1)

    token = lax.broadcasted_iota(jnp.int32, (own, width), 0)
    block_cols = tile_cols // TISSUE_BLOCK
    block = token // (tile_cols * TISSUE_BLOCK) * block_cols + token % tile_cols // TISSUE_BLOCK
    flag = jnp.zeros((own, width), jnp.float32)
    for b in range(mask_ref.shape[0] * mask_ref.shape[1]):
        value = mask_ref[b // block_cols, b % block_cols].astype(jnp.float32)
        flag = jnp.where(block == b, value, flag)

    x = x_ref[...]
    tokens = x[:own]
    kv = dot(x, wqkv_ref[:, width:], nn).astype(jnp.bfloat16)
    keys, values = kv[:, :width], kv[:, width:]
    scale = HEAD_SIZE**-0.5
    query = (dot(tokens, wqkv_ref[:, :width], nn).astype(jnp.bfloat16).astype(jnp.float32) * scale).astype(jnp.bfloat16)
    d_att = (dot(grad_ref[...], wout_ref[...], nt) * flag).astype(jnp.bfloat16)
    keys_t, values_t, d_att_t = keys.T, values.T, d_att.T
    low = lax.broadcasted_iota(jnp.int32, (own, LANES), 1) < HEAD_SIZE
    none = jnp.zeros((own, LANES), jnp.bfloat16)

    for pair in range(width // LANES):
        lanes = slice(pair * LANES, (pair + 1) * LANES)
        heads = [slice(pair * LANES + h * HEAD_SIZE, pair * LANES + (h + 1) * HEAD_SIZE) for h in range(2)]
        k_pair, v_pair = keys[:, lanes], values[:, lanes]
        q_pair, d_pair = query[:, lanes], d_att[:, lanes]
        q_two = jnp.concatenate([jnp.where(low, q_pair, none), jnp.where(low, none, q_pair)], axis=0)
        d_two = jnp.concatenate([jnp.where(low, d_pair, none), jnp.where(low, none, d_pair)], axis=0)
        scores = dot(k_pair, q_two, nt) + bias2
        top = jnp.max(scores, axis=0, keepdims=True)
        raised = jnp.exp(scores - top)
        prob = raised * (1.0 / jnp.sum(raised, axis=0, keepdims=True))
        prob_half = prob.astype(jnp.bfloat16)
        deltas = []
        for h, head in enumerate(heads):
            part = dot(values_t[head], prob_half[:, h * own : (h + 1) * own], nn).astype(jnp.bfloat16)
            att_ref[head] = part
            deltas.append(
                jnp.sum(d_att_t[head].astype(jnp.float32) * part.astype(jnp.float32), axis=0, keepdims=True)
            )
        delta = jnp.concatenate(deltas, axis=1)
        prob_grad = dot(v_pair, d_two, nt)
        score_grad = (prob * (prob_grad - delta)).astype(jnp.bfloat16)
        dkv_ref[:, lanes] = dot(score_grad, q_two, nn).astype(jnp.bfloat16)
        dkv_ref[:, width + pair * LANES : width + (pair + 1) * LANES] = dot(prob_half, d_two, nn).astype(jnp.bfloat16)
        for h, head in enumerate(heads):
            part = dot(keys_t[head], score_grad[:, h * own : (h + 1) * own], nn) * scale
            dq_ref[head] = part.astype(jnp.bfloat16)

    attended = (att_ref[...].T.astype(jnp.float32) * flag).astype(jnp.bfloat16)
    mixed_ref[...] = (tokens.astype(jnp.float32) + dot(attended, wout_ref[...], nn)).astype(jnp.bfloat16)
    back = dot(dkv_ref[...], wqkv_ref[:, width:], nt)
    d_query = dq_ref[...].T
    back_ref[:own] = back[:own] + grad_ref[...].astype(jnp.float32) + dot(d_query, wqkv_ref[:, :width], nt)
    back_ref[own:] = back[own:]


def attend(rows, tile_cols, sizes, block_mask, x_all, flags, grad_flat, w_qkv, w_out):
    width = x_all.shape[1]
    band, cols = band_table(rows, rows.own // tile_cols, tile_cols)
    vmem = pl.BlockSpec(memory_space=pltpu.VMEM)
    return pl.pallas_call(
        functools.partial(attention_kernel, rows, tile_cols, sizes),
        out_shape=(
            jax.ShapeDtypeStruct((rows.own, width), jnp.bfloat16),
            jax.ShapeDtypeStruct((rows.total, width), jnp.float32),
        ),
        in_specs=[pl.BlockSpec(memory_space=pltpu.SMEM)] + [vmem] * 7,
        out_specs=(vmem, vmem),
        scratch_shapes=[
            pltpu.VMEM((rows.total, 2 * width), jnp.bfloat16),
            pltpu.VMEM((width, rows.own), jnp.bfloat16),
            pltpu.VMEM((width, rows.own), jnp.bfloat16),
        ],
        compiler_params=pltpu.CompilerParams(vmem_limit_bytes=48 << 20),
        name="attention",
    )(block_mask, x_all, flags, jnp.asarray(band), jnp.asarray(cols), grad_flat, w_qkv, w_out)


def local(tokens, w_qkv, w_out, block_mask, grad_out):
    tile_rows, tile_cols, width = tokens.shape
    count_y, count_x = lax.axis_size("gy"), lax.axis_size("gx")
    blocks = block_mask.shape[0] * block_mask.shape[1]
    rows = Rows(tile_rows, tile_cols, blocks * (count_y + count_x))
    side, edge, wide = rows.side, rows.edge, tile_cols + 2 * REACH
    even_y, even_x = lax.axis_index("gy") % 2 == 0, lax.axis_index("gx") % 2 == 0
    flat_tokens = tokens.reshape(rows.own, width)
    grad_flat = grad_out.reshape(rows.own, width)

    grouped = tokens.astype(jnp.float32).reshape(
        tile_rows // TISSUE_BLOCK, TISSUE_BLOCK, tile_cols // TISSUE_BLOCK, TISSUE_BLOCK, width
    )
    sums = (jnp.sum(grouped, axis=(1, 3)) / TISSUE_BLOCK).reshape(blocks, width).astype(jnp.bfloat16)
    marks = jnp.broadcast_to(block_mask.reshape(blocks, 1), (blocks, width)).astype(jnp.bfloat16)
    mine = jnp.concatenate([sums, marks], axis=0)
    first = tokens[:, :REACH].reshape(side, width)
    last = tokens[:, tile_cols - REACH :].reshape(side, width)
    low_x = lax.ppermute(
        jnp.concatenate([jnp.where(even_x, last, first), mine], axis=0), "gx", pairs_low(count_x)
    )
    odd_x = lax.ppermute(jnp.where(even_x, first, last), "gx", pairs_odd(count_x, False))
    left = jnp.where(even_x, odd_x, low_x[:side])
    right = jnp.where(even_x, low_x[:side], odd_x)
    row_pool = jnp.concatenate([mine, low_x[side:]], axis=0)
    for step in steps_above(count_x, 2):
        row_pool = jnp.concatenate([row_pool, lax.ppermute(row_pool, "gx", pairs_far(count_x, step))], axis=0)
    spread = jnp.concatenate(
        [left.reshape(tile_rows, REACH, width), tokens, right.reshape(tile_rows, REACH, width)], axis=1
    )
    top, bottom = spread[:REACH].reshape(edge, width), spread[tile_rows - REACH :].reshape(edge, width)
    low_y = lax.ppermute(
        jnp.concatenate([jnp.where(even_y, bottom, top), mine], axis=0), "gy", pairs_low(count_y)
    )
    odd_y = lax.ppermute(
        jnp.concatenate([jnp.where(even_y, top, bottom), mine, low_y[edge:]], axis=0), "gy", pairs_odd(count_y, True)
    )
    up = jnp.where(even_y, odd_y[:edge], low_y[:edge])
    down = jnp.where(even_y, low_y[:edge], odd_y[:edge])
    col_pool = jnp.concatenate([mine, low_y[edge:], odd_y[edge:]], axis=0)
    for step in steps_above(count_y // 2, 2):
        col_pool = jnp.concatenate([col_pool, lax.ppermute(col_pool, "gy", window_pairs(count_y, step))], axis=0)
    pool = jnp.concatenate([row_pool, col_pool], axis=0).reshape(count_x + count_y, 2, blocks, width)
    x_all = jnp.concatenate(
        [
            flat_tokens,
            left,
            right,
            up,
            down,
            jnp.zeros((rows.pool - rows.local, width), jnp.bfloat16),
            pool[:, 0].reshape(-1, width),
            jnp.zeros((rows.total - rows.used, width), jnp.bfloat16),
        ],
        axis=0,
    )
    flags = pool[:, 1, :, : rows.own].reshape(-1, rows.own).astype(jnp.float32)
    flags = jnp.concatenate([flags, jnp.zeros((rows.total - rows.used, rows.own), jnp.float32)], axis=0)

    mixed, back = attend(rows, tile_cols, (count_y, count_x), block_mask, x_all, flags, grad_flat, w_qkv, w_out)

    half = jnp.bfloat16
    row_grad = back[rows.pool : rows.pool + count_x * blocks]
    col_grad = back[rows.pool + count_x * blocks : rows.used]

    def fold(grads, axis, moves):
        middle = grads.shape[0] // 2
        return grads[:middle] + lax.ppermute(grads[middle:].astype(half), axis, moves).astype(jnp.float32)

    for step in reversed(steps_above(count_x, 2)):
        row_grad = fold(row_grad, "gx", pairs_far(count_x, step))
    for step in reversed(steps_above(count_y // 2, 2)):
        col_grad = fold(col_grad, "gy", window_pairs(count_y, step))
    up_back, down_back = back[rows.up : rows.down], back[rows.down : rows.local]
    got = lax.ppermute(
        jnp.concatenate([jnp.where(even_y, up_back, down_back), col_grad[2 * blocks :]], axis=0).astype(half),
        "gy",
        pairs_odd(count_y, True),
    ).astype(jnp.float32)
    odd_back = got[:edge].reshape(REACH, wide, width)
    col_grad = col_grad[: 2 * blocks] + got[edge:]
    got = lax.ppermute(
        jnp.concatenate([jnp.where(even_y, down_back, up_back), col_grad[blocks:]], axis=0).astype(half),
        "gy",
        pairs_low(count_y),
    ).astype(jnp.float32)
    low_back = got[:edge].reshape(REACH, wide, width)
    block_grad = col_grad[:blocks] + got[edge:]
    spread_back = jnp.concatenate(
        [
            back[rows.left : rows.right].reshape(tile_rows, REACH, width),
            back[: rows.own].reshape(tile_rows, tile_cols, width),
            back[rows.right : rows.up].reshape(tile_rows, REACH, width),
        ],
        axis=1,
    )
    top_back = jnp.where(even_y, odd_back, low_back)
    bottom_back = jnp.where(even_y, low_back, odd_back)
    spread_back = spread_back + jnp.pad(top_back, ((0, tile_rows - REACH), (0, 0), (0, 0)))
    spread_back = spread_back + jnp.pad(bottom_back, ((tile_rows - REACH, 0), (0, 0), (0, 0)))
    left_back = spread_back[:, :REACH].reshape(side, width)
    right_back = spread_back[:, REACH + tile_cols :].reshape(side, width)
    odd_got = lax.ppermute(
        jnp.where(even_x, left_back, right_back).astype(half), "gx", pairs_odd(count_x, False)
    ).astype(jnp.float32)
    low_got = lax.ppermute(
        jnp.concatenate([jnp.where(even_x, right_back, left_back), row_grad[blocks:]], axis=0).astype(half),
        "gx",
        pairs_low(count_x),
    ).astype(jnp.float32)
    block_grad = block_grad + row_grad[:blocks] + low_got[side:]
    first_back = jnp.where(even_x, odd_got, low_got[:side]).reshape(tile_rows, REACH, width)
    last_back = jnp.where(even_x, low_got[:side], odd_got).reshape(tile_rows, REACH, width)
    d_tokens = spread_back[:, REACH : REACH + tile_cols]
    d_tokens = d_tokens + jnp.pad(first_back, ((0, 0), (0, tile_cols - REACH), (0, 0)))
    d_tokens = d_tokens + jnp.pad(last_back, ((0, 0), (tile_cols - REACH, 0), (0, 0)))
    shaped = (block_grad / TISSUE_BLOCK).reshape(tile_rows // TISSUE_BLOCK, tile_cols // TISSUE_BLOCK, width)
    d_tokens = d_tokens + jnp.repeat(jnp.repeat(shaped, TISSUE_BLOCK, 0), TISSUE_BLOCK, 1)
    return mixed.reshape(tile_rows, tile_cols, width), d_tokens.astype(jnp.bfloat16)


def solution(mesh):
    placed = (P("gy", "gx", None), P(), P(), P("gy", "gx"), P("gy", "gx", None))
    return jax.shard_map(
        local,
        mesh=mesh,
        in_specs=placed,
        out_specs=(P("gy", "gx", None), P("gy", "gx", None)),
        check_vma=False,
    )
```

time: 731 us -> 41.6 us (0.06)
  the two profiles are of different devices: /device:TPU:1 before, /device:TPU:22 now
where the time goes in v1:
time: 41.6 us; the launch traced here: 41.4 us
  waiting for transfers between devices  20.6 us (50%)
  starting transfers between devices  11.1 us (27%)
  Pallas kernels  4.05 us (10%)
  local copies, waits for them, and re-layouts  2.37 us (6%)
  other arithmetic  2.19 us (5%)
  between operations  1.11 us (3%)
    ppermute x2, waiting for transfers between devices, fold(): lax.ppermute(grads[middle:].astype(half), axis, moves).astype(jnp.float32)  7.46 us
    ppermute x2, waiting for transfers between devices, local(): lax.ppermute(row_pool, 'gx', pairs_far(count_x, step))  5.27 us
    ppermute x1, starting transfers between devices, local(): lax.ppermute(jnp.where(even_x, first, last), 'gx', pairs_odd(count_x, Fal...  4.44 us
    pallas_call x1, Pallas kernels, attend(): pl.pallas_call(functools.partial(attention_kernel, rows, tile_cols, sizes...  4.05 us
    ppermute x1, waiting for transfers between devices, local(): lax.ppermute(jnp.where(even_x, left_back, right_back).astype(half), 'gx',...  3.54 us
    ppermute x1, starting transfers between devices, local(): lax.ppermute(jnp.where(even_x, left_back, right_back).astype(half), 'gx',...  2.96 us
    ppermute x1, waiting for transfers between devices, local(): lax.ppermute(jnp.where(even_x, first, last), 'gx', pairs_odd(count_x, Fal...  2.09 us
    ppermute x1, starting transfers between devices, local(): lax.ppermute(jnp.concatenate([jnp.where(even_x, right_back, left_back), r...  1.59 us
  transfers between devices with their start and end apart: 12, of which 8 were waited for; matrix products, arithmetic and copies ran while one was open for 1% of the time, Pallas kernels for 0%

profile of v1, /device:TPU:22, one launch (start us, length us, event | category | flops | bytes accessed | tf_op | source)
XLA Modules:
  0.0 41.4 jit_solution(1216998553978600918)
XLA Ops:
  0.6 0.0 copy-start.6
  0.7 1.0 %convert_reduce_fusion = f32[16,384]{1,0:T(8,128)S(1)} fusion(bf16[8,16,384]{2,1,0:T(8,128)(2,1)} %param.7), kind=kLoop, calls=%fused_computation.6 | loop fusion | flops 92160 | bytes 122880 | tf_op jit(solution)/shard_map/reduce_sum | solution.py:203
  1.6 0.0 copy-done.6
  1.7 0.0 copy-start.5
  1.7 0.6 %copy-done.5 = s32[1,2]{1,0:T(1,128)S(1)} copy-done((s32[1,2]{1,0:T(1,128)S(1)}, s32[1,2]{1,0:T(1,128)}, u32[]{:S(2)}) %copy-start.5) | copy-done | bytes 32
  2.4 0.1 broadcast_in_dim.20
  2.5 0.6 %collective-permute-start.1 = (bf16[28,384]{1,0:T(8,128)(2,1)S(1)}, bf16[28,384]{1,0:T(8,128)(2,1)S(1)}, u32[]{:S(2)}, u32[]{:S(2)}) collective-permute-start(bf16[28,384]{1,0:T(8,128)(2,1)S(1)} %pad_maximum_fusion.7), channel_id=1, source_target_pairs={{0,1},{1,0},{2,3},{3,2},{4,5},{5,4},{6,7},{7,6},{8,9},{9,8},{10,11... | collective-permute-start | bytes 64520 | tf_op jit(solution)/shard_map/ppermute | solution.py:208
  3.1 4.4 %collective-permute-start = (bf16[24,384]{1,0:T(8,128)(2,1)S(1)}, bf16[24,384]{1,0:T(8,128)(2,1)S(1)}, u32[]{:S(2)}, u32[]{:S(2)}) collective-permute-start(bf16[24,384]{1,0:T(8,128)(2,1)S(1)} %select_n.119), channel_id=1, source_target_pairs={{1,2},{2,1},{3,4},{4,3},{5,6},{6,5},{9,10},{10,9},{11,12},{12,11},... | collective-permute-start | bytes 55304 | tf_op jit(solution)/shard_map/ppermute | solution.py:211
  7.5 2.1 %collective-permute-done = bf16[24,384]{1,0:T(8,128)(2,1)S(1)} collective-permute-done((bf16[24,384]{1,0:T(8,128)(2,1)S(1)}, bf16[24,384]{1,0:T(8,128)(2,1)S(1)}, u32[]{:S(2)}, u32[]{:S(2)}) %collective-permute-start) | collective-permute-done | bytes 18464 | tf_op jit(solution)/shard_map/ppermute | solution.py:211
  9.6 0.0 collective-permute-done.1
  9.7 0.1 broadcast_select_fusion.1
  9.7 0.0 copy-start
  9.8 0.1 collective-permute-start.2
  9.9 0.1 collective-permute-start.4
  10.0 1.1 %collective-permute-done.2 = bf16[70,384]{1,0:T(8,128)(2,1)S(1)} collective-permute-done((bf16[70,384]{1,0:T(8,128)(2,1)S(1)}, bf16[70,384]{1,0:T(8,128)(2,1)S(1)}, u32[]{:S(2)}, u32[]{:S(2)}) %collective-permute-start.2) | collective-permute-done | bytes 53792 | tf_op jit(solution)/shard_map/ppermute | solution.py:221
  11.1 0.4 collective-permute-start.3
  11.5 2.1 %collective-permute-done.4 = bf16[8,384]{1,0:T(8,128)(2,1)S(1)} collective-permute-done((bf16[8,384]{1,0:T(8,128)(2,1)S(1)}, bf16[8,384]{1,0:T(8,128)(2,1)S(1)}, u32[]{:S(2)}, u32[]{:S(2)}) %collective-permute-start.4) | collective-permute-done | bytes 6176 | tf_op jit(solution)/shard_map/ppermute | solution.py:216
  13.7 0.4 collective-permute-start.5
  14.1 1.1 %collective-permute-done.3 = bf16[74,384]{1,0:T(8,128)(2,1)S(1)} collective-permute-done((bf16[74,384]{1,0:T(8,128)(2,1)S(1)}, bf16[74,384]{1,0:T(8,128)(2,1)S(1)}, u32[]{:S(2)}, u32[]{:S(2)}) %collective-permute-start.3) | collective-permute-done | bytes 56864 | tf_op jit(solution)/shard_map/ppermute | solution.py:224
  15.2 3.1 %collective-permute-done.5 = bf16[16,384]{1,0:T(8,128)(2,1)S(1)} collective-permute-done((bf16[16,384]{1,0:T(8,128)(2,1)S(1)}, bf16[16,384]{1,0:T(8,128)(2,1)S(1)}, u32[]{:S(2)}, u32[]{:S(2)}) %collective-permute-start.5) | collective-permute-done | bytes 12320 | tf_op jit(solution)/shard_map/ppermute | solution.py:216
  18.3 0.1 concatenate.57
  18.5 0.0 copy-start.3
  18.6 0.0 copy-start.1
  18.6 0.0 copy-start.2
  18.6 0.0 copy-start.4
  18.6 0.5 %concatenate.58.x_ref = bf16[384,384]{1,0:T(8,128)(2,1)S(1)} concatenate(bf16[128,384]{1,0:T(8,128)(2,1)S(1)} %bitcast.20, bf16[24,384]{1,0:T(8,128)(2,1)S(1)} %get-tuple-element.24, bf16[24,384]{1,0:T(8,128)(2,1)S(1)} %get-tuple-element.23, bf16[66,384]{1,0:T(8,128)(2,1)S(1)} %get-tuple-element.18, bf16[66,384]{1,0:T(8,128)(2,1)S(1)} %get-tuple-element.17, ...), dimensions={0} | concatenate | bytes 589824 | tf_op jit(solution)/shard_map/concatenate | solution.py:233
  19.1 0.0 copy-done
  19.1 0.3 copy-done.3
  19.4 0.2 copy-done.1
  19.6 0.0 copy-done.2
  19.6 0.1 copy-done.4
  19.7 4.1 %attention.1 = (bf16[128,384]{1,0:T(8,128)(2,1)}, f32[384,384]{1,0:T(8,128)S(1)}) custom-call(s32[1,2]{1,0:T(1,128)S(1)} %copy-done.5, bf16[384,384]{1,0:T(8,128)(2,1)S(1)} %concatenate.58.x_ref, f32[64,128]{1,0:T(8,128)S(1)} %pad_convert_fusion.flags_ref, f32[384,128]{1,0:T(8,128)S(1)} %copy-done.2, s32[384,128]{1,0:T(8,128)S(1)} %copy-done.3, ...), custom_call_target="tpu_custom_call" | custom-call | tf_op jit(solution)/shard_map/attention/pallas_call | solution.py:172
  23.9 0.4 collective-permute-start.9
  24.3 0.1 collective-permute-start.6
  24.4 4.0 %collective-permute-done.9 = bf16[8,384]{1,0:T(8,128)(2,1)S(1)} collective-permute-done((bf16[8,384]{1,0:T(8,128)(2,1)S(1)}, bf16[8,384]{1,0:T(8,128)(2,1)S(1)}, u32[]{:S(2)}, u32[]{:S(2)}) %collective-permute-start.9) | collective-permute-done | bytes 6176 | tf_op jit(solution)/shard_map/ppermute | solution.py:257
  28.5 0.1 collective-permute-start.10
  28.6 0.0 collective-permute-done.6
  28.6 0.1 collective-permute-start.7
  28.7 3.4 %collective-permute-done.10 = bf16[4,384]{1,0:T(4,128)(2,1)S(1)} collective-permute-done((bf16[4,384]{1,0:T(4,128)(2,1)S(1)}, bf16[4,384]{1,0:T(4,128)(2,1)S(1)}, u32[]{:S(2)}, u32[]{:S(2)}) %collective-permute-start.10) | collective-permute-done | bytes 3104 | tf_op jit(solution)/shard_map/ppermute | solution.py:257
  32.1 0.0 collective-permute-done.7
  32.3 1.6 %collective-permute-start.11 = (bf16[26,384]{1,0:T(8,128)(2,1)S(1)}, bf16[26,384]{1,0:T(8,128)(2,1)S(1)}, u32[]{:S(2)}, u32[]{:S(2)}) collective-permute-start(bf16[26,384]{1,0:T(8,128)(2,1)S(1)} %pad_maximum_fusion.8), channel_id=1, source_target_pairs={{0,1},{1,0},{2,3},{3,2},{4,5},{5,4},{6,7},{7,6},{8,9},{9,8},{10,11... | collective-permute-start | bytes 59912 | tf_op jit(solution)/shard_map/ppermute | solution.py:295
  34.0 0.1 fusion
  34.0 3.0 %collective-permute-start.8 = (bf16[24,384]{1,0:T(8,128)(2,1)S(1)}, bf16[24,384]{1,0:T(8,128)(2,1)S(1)}, u32[]{:S(2)}, u32[]{:S(2)}) collective-permute-start(bf16[24,384]{1,0:T(8,128)(2,1)S(1)} %convert_element_type.65), channel_id=1, source_target_pairs={{1,2},{2,1},{3,4},{4,3},{5,6},{6,5},{9,10},{10,9},{11,12},{12,11},... | collective-permute-start | bytes 55304 | tf_op jit(solution)/shard_map/ppermute | solution.py:292
  37.0 0.0 collective-permute-done.11
  37.1 3.5 %collective-permute-done.8 = bf16[24,384]{1,0:T(8,128)(2,1)S(1)} collective-permute-done((bf16[24,384]{1,0:T(8,128)(2,1)S(1)}, bf16[24,384]{1,0:T(8,128)(2,1)S(1)}, u32[]{:S(2)}, u32[]{:S(2)}) %collective-permute-start.8) | collective-permute-done | bytes 18464 | tf_op jit(solution)/shard_map/ppermute | solution.py:292
  40.7 0.7 %fusion.3 = bf16[8,16,384]{2,1,0:T(8,128)(2,1)} fusion(f32[8,22,384]{2,1,0:T(8,128)S(1)} %fusion, f32[8,3,384]{2,1,0:T(4,128)S(1)} %reshape.90, f32[8,3,384]{2,1,0:T(4,128)S(1)} %reshape.89, f32[16,384]{1,0:T(8,128)S(1)} %broadcast_bitcast_fusion), kind=kLoop, calls=%fused_computation.5 | loop fusion | flops 196608 | bytes 393216 | tf_op jit(solution)/shard_map/convert_element_type | solution.py:308
  (59 shorter events, 0.8 us)
Async XLA Ops:
  0.6 1.0 %copy-start.6 = (bf16[8,16,384]{2,1,0:T(8,128)(2,1)S(1)}, bf16[8,16,384]{2,1,0:T(8,128)(2,1)}, u32[]{:S(2)}) copy-start(bf16[8,16,384]{2,1,0:T(8,128)(2,1)} %param.7) | copy-start | bytes 294916
  1.7 0.7 %copy-start.5 = (s32[1,2]{1,0:T(1,128)S(1)}, s32[1,2]{1,0:T(1,128)}, u32[]{:S(2)}) copy-start(s32[1,2]{1,0:T(1,128)} %mask_ref.1) | copy-start | bytes 28
  2.5 7.2 %collective-permute-start.1 = (bf16[28,384]{1,0:T(8,128)(2,1)S(1)}, bf16[28,384]{1,0:T(8,128)(2,1)S(1)}, u32[]{:S(2)}, u32[]{:S(2)}) collective-permute-start(bf16[28,384]{1,0:T(8,128)(2,1)S(1)} %pad_maximum_fusion.7), channel_id=1, source_target_pairs={{0,1},{1,0},{2,3},{3,2},{4,5},{5,4},{6,7},{7,6},{8,9},{9,8},{10,11... | collective-permute-start | bytes 64520 | tf_op jit(solution)/shard_map/ppermute | solution.py:208
  3.1 6.6 %collective-permute-start = (bf16[24,384]{1,0:T(8,128)(2,1)S(1)}, bf16[24,384]{1,0:T(8,128)(2,1)S(1)}, u32[]{:S(2)}, u32[]{:S(2)}) collective-permute-start(bf16[24,384]{1,0:T(8,128)(2,1)S(1)} %select_n.119), channel_id=1, source_target_pairs={{1,2},{2,1},{3,4},{4,3},{5,6},{6,5},{9,10},{10,9},{11,12},{12,11},... | collective-permute-start | bytes 55304 | tf_op jit(solution)/shard_map/ppermute | solution.py:211
  9.7 9.4 %copy-start = (bf16[384,1152]{1,0:T(8,128)(2,1)S(1)}, bf16[384,1152]{1,0:T(8,128)(2,1)}, u32[]{:S(2)}) copy-start(bf16[384,1152]{1,0:T(8,128)(2,1)} %wqkv_ref.1) | copy-start | bytes 2654212
  9.8 1.3 %collective-permute-start.2 = (bf16[70,384]{1,0:T(8,128)(2,1)S(1)}, bf16[70,384]{1,0:T(8,128)(2,1)S(1)}, u32[]{:S(2)}, u32[]{:S(2)}) collective-permute-start(bf16[70,384]{1,0:T(8,128)(2,1)S(1)} %pad_maximum_fusion.4), channel_id=1, source_target_pairs={{0,8},{8,0},{16,24},{24,16},{1,9},{9,1},{17,25},{25,17},{2,10},{10... | collective-permute-start | bytes 161288 | tf_op jit(solution)/shard_map/ppermute | solution.py:221
  9.9 3.7 %collective-permute-start.4 = (bf16[8,384]{1,0:T(8,128)(2,1)S(1)}, bf16[8,384]{1,0:T(8,128)(2,1)S(1)}, u32[]{:S(2)}, u32[]{:S(2)}) collective-permute-start(bf16[8,384]{1,0:T(8,128)(2,1)S(1)} %pad_maximum_fusion.10), channel_id=1, source_target_pairs={{0,2},{1,3},{2,0},{3,1},{4,6},{5,7},{6,4},{7,5},{8,10},{9,11},{10,... | collective-permute-start | bytes 18440 | tf_op jit(solution)/shard_map/ppermute | solution.py:216
  11.1 4.0 %collective-permute-start.3 = (bf16[74,384]{1,0:T(8,128)(2,1)S(1)}, bf16[74,384]{1,0:T(8,128)(2,1)S(1)}, u32[]{:S(2)}, u32[]{:S(2)}) collective-permute-start(bf16[74,384]{1,0:T(8,128)(2,1)S(1)} %pad_maximum_fusion), channel_id=1, source_target_pairs={{0,24},{8,16},{16,8},{24,0},{1,25},{9,17},{17,9},{25,1},{2,26},{10... | collective-permute-start | bytes 170504 | tf_op jit(solution)/shard_map/ppermute | solution.py:224
  13.7 4.7 %collective-permute-start.5 = (bf16[16,384]{1,0:T(8,128)(2,1)S(1)}, bf16[16,384]{1,0:T(8,128)(2,1)S(1)}, u32[]{:S(2)}, u32[]{:S(2)}) collective-permute-start(bf16[16,384]{1,0:T(8,128)(2,1)S(1)} %pad_maximum_fusion.9), channel_id=1, source_target_pairs={{0,4},{1,5},{2,6},{3,7},{4,0},{5,1},{6,2},{7,3},{8,12},{9,13},{10,... | collective-permute-start | bytes 36872 | tf_op jit(solution)/shard_map/ppermute | solution.py:216
  18.5 0.9 %copy-start.3 = (s32[384,128]{1,0:T(8,128)S(1)}, s32[384,128]{1,0:T(8,128)}, u32[]{:S(2)}) copy-start(s32[384,128]{1,0:T(8,128)} %constant.44.clone.cols_ref) | copy-start | bytes 589828
  18.6 1.0 %copy-start.1 = (bf16[384,384]{1,0:T(8,128)(2,1)S(1)}, bf16[384,384]{1,0:T(8,128)(2,1)}, u32[]{:S(2)}) copy-start(bf16[384,384]{1,0:T(8,128)(2,1)} %wout_ref.1) | copy-start | bytes 884740
  18.6 1.1 %copy-start.2 = (f32[384,128]{1,0:T(8,128)S(1)}, f32[384,128]{1,0:T(8,128)}, u32[]{:S(2)}) copy-start(f32[384,128]{1,0:T(8,128)} %constant.43.clone.band_ref) | copy-start | bytes 589828
  18.6 1.1 %copy-start.4 = (bf16[8,16,384]{2,1,0:T(8,128)(2,1)S(1)}, bf16[8,16,384]{2,1,0:T(8,128)(2,1)}, u32[]{:S(2)}) copy-start(bf16[8,16,384]{2,1,0:T(8,128)(2,1)} %param.11) | copy-start | bytes 294916
  23.9 4.6 %collective-permute-start.9 = (bf16[8,384]{1,0:T(8,128)(2,1)S(1)}, bf16[8,384]{1,0:T(8,128)(2,1)S(1)}, u32[]{:S(2)}, u32[]{:S(2)}) collective-permute-start(bf16[8,384]{1,0:T(8,128)(2,1)S(1)} %slice.174), channel_id=1, source_target_pairs={{0,4},{1,5},{2,6},{3,7},{4,0},{5,1},{6,2},{7,3},{8,12},{9,13},{10,... | collective-permute-start | bytes 18440 | tf_op jit(solution)/shard_map/ppermute | solution.py:257
  24.3 4.3 %collective-permute-start.6 = (bf16[70,384]{1,0:T(8,128)(2,1)S(1)}, bf16[70,384]{1,0:T(8,128)(2,1)S(1)}, u32[]{:S(2)}, u32[]{:S(2)}) collective-permute-start(bf16[70,384]{1,0:T(8,128)(2,1)S(1)} %pad_maximum_fusion.5), channel_id=1, source_target_pairs={{0,24},{8,16},{16,8},{24,0},{1,25},{9,17},{17,9},{25,1},{2,26},{10... | collective-permute-start | bytes 161288 | tf_op jit(solution)/shard_map/ppermute | solution.py:264
  28.5 3.7 %collective-permute-start.10 = (bf16[4,384]{1,0:T(4,128)(2,1)S(1)}, bf16[4,384]{1,0:T(4,128)(2,1)S(1)}, u32[]{:S(2)}, u32[]{:S(2)}) collective-permute-start(bf16[4,384]{1,0:T(4,128)(2,1)S(1)} %slice.228), channel_id=1, source_target_pairs={{0,2},{1,3},{2,0},{3,1},{4,6},{5,7},{6,4},{7,5},{8,10},{9,11},{10,... | collective-permute-start | bytes 9224 | tf_op jit(solution)/shard_map/ppermute | solution.py:257
  28.6 3.5 %collective-permute-start.7 = (bf16[68,384]{1,0:T(8,128)(2,1)S(1)}, bf16[68,384]{1,0:T(8,128)(2,1)S(1)}, u32[]{:S(2)}, u32[]{:S(2)}) collective-permute-start(bf16[68,384]{1,0:T(8,128)(2,1)S(1)} %pad_maximum_fusion.6), channel_id=1, source_target_pairs={{0,8},{8,0},{16,24},{24,16},{1,9},{9,1},{17,25},{25,17},{2,10},{10... | collective-permute-start | bytes 156680 | tf_op jit(solution)/shard_map/ppermute | solution.py:271
  32.3 4.7 %collective-permute-start.11 = (bf16[26,384]{1,0:T(8,128)(2,1)S(1)}, bf16[26,384]{1,0:T(8,128)(2,1)S(1)}, u32[]{:S(2)}, u32[]{:S(2)}) collective-permute-start(bf16[26,384]{1,0:T(8,128)(2,1)S(1)} %pad_maximum_fusion.8), channel_id=1, source_target_pairs={{0,1},{1,0},{2,3},{3,2},{4,5},{5,4},{6,7},{7,6},{8,9},{9,8},{10,11... | collective-permute-start | bytes 59912 | tf_op jit(solution)/shard_map/ppermute | solution.py:295
  34.0 6.6 %collective-permute-start.8 = (bf16[24,384]{1,0:T(8,128)(2,1)S(1)}, bf16[24,384]{1,0:T(8,128)(2,1)S(1)}, u32[]{:S(2)}, u32[]{:S(2)}) collective-permute-start(bf16[24,384]{1,0:T(8,128)(2,1)S(1)} %convert_element_type.65), channel_id=1, source_target_pairs={{1,2},{2,1},{3,4},{4,3},{5,6},{6,5},{9,10},{10,9},{11,12},{12,11},... | collective-permute-start | bytes 55304 | tf_op jit(solution)/shard_map/ppermute | solution.py:292

commit v2 on v1

v2 whole, which is shorter than its diff:
```python
import functools

import jax
import jax.numpy as jnp
import numpy as np
from jax import lax
from jax.experimental import pallas as pl
from jax.experimental.pallas import tpu as pltpu
from jax.sharding import PartitionSpec as P

NH = 6
HEAD_SIZE = 64
KS = 7
TISSUE_BLOCK = 8
REACH = KS // 2
NEG_FILL = -1e30
LANES = 128
ALIGN = 16
FAR = -1000


def pairs_low(count):
    return [(i, i ^ 1) for i in range(count)]


def pairs_odd(count, wrap):
    moves = []
    for i in range(count):
        j = (i + 1) % count if i % 2 else (i - 1) % count
        if wrap or abs(i - j) == 1:
            moves.append((i, j))
    return moves


def pairs_far(count, step):
    return [(i, i ^ step) for i in range(count)]


def window_pairs(count, step):
    moves = []
    for i in range(count):
        group, side = divmod((i - 1) % count, 2)
        moves.append((i, (2 * (group ^ step) + 1 + side) % count))
    return moves


def steps_above(count, first):
    steps = []
    while first < count:
        steps.append(first)
        first *= 2
    return steps


def padded(count, unit=ALIGN):
    return -(-count // unit) * unit


class Rows:
    def __init__(self, tile_rows, tile_cols, pooled):
        self.tile_rows, self.tile_cols = tile_rows, tile_cols
        self.wide = tile_cols + 2 * REACH
        self.own = tile_rows * tile_cols
        self.side = tile_rows * REACH
        self.edge = REACH * self.wide
        self.low_x = self.own
        self.odd_x = self.low_x + padded(self.side)
        self.low_y = self.odd_x + padded(self.side)
        self.odd_y = self.low_y + padded(self.edge)
        self.pool = self.odd_y + padded(self.edge)
        self.pooled = pooled
        self.used = self.pool + pooled
        self.total = padded(self.used, LANES)


def places(rows):
    tile_rows, tile_cols = rows.tile_rows, rows.tile_cols
    place = np.full((2, 2, rows.total, 2), FAR, np.int32)

    def grid(first, second):
        return np.stack(np.meshgrid(np.asarray(first), np.asarray(second), indexing="ij"), -1).reshape(-1, 2)

    before, own_cols, after = np.arange(-REACH, 0), np.arange(tile_cols), tile_cols + np.arange(REACH)
    above, own_rows, below = np.arange(-REACH, 0), np.arange(tile_rows), tile_rows + np.arange(REACH)
    for odd_y in range(2):
        for odd_x in range(2):
            low_cols, odd_cols = (before, after) if odd_x else (after, before)
            low_rows, odd_rows = (above, below) if odd_y else (below, above)
            wide_cols = np.concatenate([low_cols, own_cols, odd_cols])
            spot = place[odd_y, odd_x]
            spot[: rows.own] = grid(own_rows, own_cols)
            spot[rows.low_x : rows.low_x + rows.side] = grid(own_rows, low_cols)
            spot[rows.odd_x : rows.odd_x + rows.side] = grid(own_rows, odd_cols)
            spot[rows.low_y : rows.low_y + rows.edge] = grid(low_rows, wide_cols)
            spot[rows.odd_y : rows.odd_y + rows.edge] = grid(odd_rows, wide_cols)
    return place


def window_bias(rows, count_y, count_x):
    iy, ix = lax.axis_index("gy"), lax.axis_index("gx")
    table = jnp.asarray(places(rows))
    key = table[iy % 2, ix % 2]
    key_row, key_col = key[:, :1], key[:, 1:]
    token = np.arange(rows.own)[None, :]
    near = (jnp.abs(key_row - token // rows.tile_cols) <= REACH) & (jnp.abs(key_col - token % rows.tile_cols) <= REACH)
    row, col = iy * rows.tile_rows + key_row, ix * rows.tile_cols + key_col
    inside = (row >= 0) & (row < count_y * rows.tile_rows) & (col >= 0) & (col < count_x * rows.tile_cols)
    return jnp.where(near & inside, 0.0, NEG_FILL).astype(jnp.float32)


DOT = functools.partial(lax.dot_general, preferred_element_type=jnp.float32)
NN = (((1,), (0,)), ((), ()))
NT = (((1,), (1,)), ((), ()))
SCALE = HEAD_SIZE**-0.5


def token_flags(rows, mask_ref, width):
    token = lax.broadcasted_iota(jnp.int32, (rows.own, width), 0)
    block_cols = rows.tile_cols // TISSUE_BLOCK
    block = token // (rows.tile_cols * TISSUE_BLOCK) * block_cols + token % rows.tile_cols // TISSUE_BLOCK
    flag = jnp.zeros((rows.own, width), jnp.float32)
    for b in range(mask_ref.shape[0] * mask_ref.shape[1]):
        value = mask_ref[b // block_cols, b % block_cols].astype(jnp.float32)
        flag = jnp.where(block == b, value, flag)
    return flag


def own_kernel(rows, mask_ref, tokens_ref, grad_ref, wqkv_ref, wout_ref, query_ref, kv_ref, datt_ref):
    width = NH * HEAD_SIZE
    tokens = tokens_ref[...]
    query = DOT(tokens, wqkv_ref[:, :width], NN).astype(jnp.bfloat16).astype(jnp.float32) * SCALE
    query_ref[...] = query.astype(jnp.bfloat16)
    kv_ref[...] = DOT(tokens, wqkv_ref[:, width:], NN).astype(jnp.bfloat16)
    flag = token_flags(rows, mask_ref, width)
    datt_ref[...] = (DOT(grad_ref[...], wout_ref[...], NT) * flag).astype(jnp.bfloat16)


def attention_kernel(
    rows,
    low_x_ref, odd_x_ref, low_y_ref, odd_y_ref, pool_ref, flags_ref, bias_ref, query_ref, kv_ref, datt_ref, wkv_ref,
    back_ref, dkv_ref, att_ref, dq_ref,
    x_ref, all_kv_ref, all_dkv_ref,
):
    width = NH * HEAD_SIZE
    own = rows.own
    pooled = jnp.where(flags_ref[...] > 0, 0.0, NEG_FILL)
    bias = jnp.concatenate([bias_ref[: rows.pool], pooled], axis=0)
    bias2 = jnp.concatenate([bias, bias], axis=1)

    x_ref[...] = jnp.zeros_like(x_ref)
    for start, ref, count in (
        (rows.low_x, low_x_ref, rows.side),
        (rows.odd_x, odd_x_ref, rows.side),
        (rows.low_y, low_y_ref, rows.edge),
        (rows.odd_y, odd_y_ref, rows.edge),
        (rows.pool, pool_ref, rows.total - rows.pool),
    ):
        x_ref[start - own : start - own + count] = ref[:count]
    all_kv_ref[:own] = kv_ref[...]
    all_kv_ref[own:] = DOT(x_ref[...], wkv_ref[...], NN).astype(jnp.bfloat16)
    keys, values = all_kv_ref[:, :width], all_kv_ref[:, width:]
    query, d_att = query_ref[...], datt_ref[...]
    keys_t, values_t, d_att_t = keys.T, values.T, d_att.T
    low = lax.broadcasted_iota(jnp.int32, (own, LANES), 1) < HEAD_SIZE
    none = jnp.zeros((own, LANES), jnp.bfloat16)

    for pair in range(width // LANES):
        lanes = slice(pair * LANES, (pair + 1) * LANES)
        heads = [slice(pair * LANES + h * HEAD_SIZE, pair * LANES + (h + 1) * HEAD_SIZE) for h in range(2)]
        k_pair, v_pair = keys[:, lanes], values[:, lanes]
        q_pair, d_pair = query[:, lanes], d_att[:, lanes]
        q_two = jnp.concatenate([jnp.where(low, q_pair, none), jnp.where(low, none, q_pair)], axis=0)
        d_two = jnp.concatenate([jnp.where(low, d_pair, none), jnp.where(low, none, d_pair)], axis=0)
        scores = DOT(k_pair, q_two, NT) + bias2
        top = jnp.max(scores, axis=0, keepdims=True)
        raised = jnp.exp(scores - top)
        prob = raised * (1.0 / jnp.sum(raised, axis=0, keepdims=True))
        prob_half = prob.astype(jnp.bfloat16)
        deltas = []
        for h, head in enumerate(heads):
            part = DOT(values_t[head], prob_half[:, h * own : (h + 1) * own], NN).astype(jnp.bfloat16)
            att_ref[head] = part
            deltas.append(
                jnp.sum(d_att_t[head].astype(jnp.float32) * part.astype(jnp.float32), axis=0, keepdims=True)
            )
        delta = jnp.concatenate(deltas, axis=1)
        prob_grad = DOT(v_pair, d_two, NT)
        score_grad = (prob * (prob_grad - delta)).astype(jnp.bfloat16)
        all_dkv_ref[:, lanes] = DOT(score_grad, q_two, NN).astype(jnp.bfloat16)
        all_dkv_ref[:, width + pair * LANES : width + (pair + 1) * LANES] = DOT(prob_half, d_two, NN).astype(jnp.bfloat16)
        for h, head in enumerate(heads):
            part = DOT(keys_t[head], score_grad[:, h * own : (h + 1) * own], NN) * SCALE
            dq_ref[head] = part.astype(jnp.bfloat16)
    back_ref[...] = DOT(all_dkv_ref[own:], wkv_ref[...], NT)
    dkv_ref[...] = all_dkv_ref[:own]


def final_kernel(
    rows, mask_ref, tokens_ref, grad_ref, att_ref, dq_ref, dkv_ref, wqkv_ref, wout_ref, mixed_ref, own_ref
):
    width = NH * HEAD_SIZE
    flag = token_flags(rows, mask_ref, width)
    attended = (att_ref[...].T.astype(jnp.float32) * flag).astype(jnp.bfloat16)
    mixed = tokens_ref[...].astype(jnp.float32) + DOT(attended, wout_ref[...], NN)
    mixed_ref[...] = mixed.astype(jnp.bfloat16)
    own_ref[...] = (
        grad_ref[...].astype(jnp.float32)
        + DOT(dq_ref[...].T, wqkv_ref[:, :width], NT)
        + DOT(dkv_ref[...], wqkv_ref[:, width:], NT)
    )


def call(kernel, name, outs, scratch, flops, smem, *operands):
    vmem = pl.BlockSpec(memory_space=pltpu.VMEM)
    in_specs = [pl.BlockSpec(memory_space=pltpu.SMEM)] * smem + [vmem] * (len(operands) - smem)
    moved = sum(a.size * a.dtype.itemsize for a in operands)
    return pl.pallas_call(
        kernel,
        out_shape=tuple(jax.ShapeDtypeStruct(shape, dtype) for shape, dtype in outs),
        in_specs=in_specs,
        out_specs=tuple(vmem for _ in outs),
        scratch_shapes=[pltpu.VMEM(shape, dtype) for shape, dtype in scratch],
        compiler_params=pltpu.CompilerParams(vmem_limit_bytes=40 << 20),
        cost_estimate=pl.CostEstimate(flops=flops, transcendentals=0, bytes_accessed=moved),
        name=name,
    )(*operands)


def local(tokens, w_qkv, w_out, block_mask, grad_out):
    tile_rows, tile_cols, width = tokens.shape
    count_y, count_x = lax.axis_size("gy"), lax.axis_size("gx")
    blocks = block_mask.shape[0] * block_mask.shape[1]
    rows = Rows(tile_rows, tile_cols, blocks * (count_y + count_x))
    own, side, edge, wide = rows.own, rows.side, rows.edge, rows.wide
    even_y, even_x = lax.axis_index("gy") % 2 == 0, lax.axis_index("gx") % 2 == 0
    flat_tokens = tokens.reshape(own, width)
    grad_flat = grad_out.reshape(own, width)
    half, full = jnp.bfloat16, jnp.float32

    first = tokens[:, :REACH].reshape(side, width)
    last = tokens[:, tile_cols - REACH :].reshape(side, width)
    odd_x = lax.ppermute(jnp.where(even_x, first, last), "gx", pairs_odd(count_x, False))
    grouped = tokens.astype(full).reshape(
        tile_rows // TISSUE_BLOCK, TISSUE_BLOCK, tile_cols // TISSUE_BLOCK, TISSUE_BLOCK, width
    )
    sums = (jnp.sum(grouped, axis=(1, 3)) / TISSUE_BLOCK).reshape(blocks, width).astype(half)
    marks = jnp.broadcast_to(block_mask.reshape(blocks, 1), (blocks, width)).astype(half)
    mine = jnp.concatenate([sums, marks], axis=0)
    low_x = lax.ppermute(
        jnp.concatenate([jnp.where(even_x, last, first), mine], axis=0), "gx", pairs_low(count_x)
    )
    row_pool = jnp.concatenate([mine, low_x[side:]], axis=0)
    for step in steps_above(count_x, 2):
        row_pool = jnp.concatenate([row_pool, lax.ppermute(row_pool, "gx", pairs_far(count_x, step))], axis=0)
    spread = jnp.concatenate(
        [low_x[:side].reshape(tile_rows, REACH, width), tokens, odd_x.reshape(tile_rows, REACH, width)], axis=1
    )
    top, bottom = spread[:REACH].reshape(edge, width), spread[tile_rows - REACH :].reshape(edge, width)
    low_y = lax.ppermute(
        jnp.concatenate([jnp.where(even_y, bottom, top), mine], axis=0), "gy", pairs_low(count_y)
    )
    odd_y = lax.ppermute(
        jnp.concatenate([jnp.where(even_y, top, bottom), mine, low_y[edge:]], axis=0), "gy", pairs_odd(count_y, True)
    )
    col_pool = jnp.concatenate([mine, low_y[edge:], odd_y[edge:]], axis=0)
    for step in steps_above(count_y // 2, 2):
        col_pool = jnp.concatenate([col_pool, lax.ppermute(col_pool, "gy", window_pairs(count_y, step))], axis=0)
    pool = jnp.concatenate([row_pool, col_pool], axis=0).reshape(count_x + count_y, 2, blocks, width)
    spare = ((0, rows.total - rows.used), (0, 0))
    pool_tokens = jnp.pad(pool[:, 0].reshape(-1, width), spare)
    flags = jnp.pad(pool[:, 1, :, :own].reshape(-1, own), spare).astype(full)

    macs = own * width * width
    query, kv, d_att = call(
        functools.partial(own_kernel, rows), "own", [((own, width), half), ((own, 2 * width), half), ((own, width), half)],
        [], 8 * macs, 1, block_mask, flat_tokens, grad_flat, w_qkv, w_out,
    )
    bias = window_bias(rows, count_y, count_x)
    back, d_kv, att, d_query = call(
        functools.partial(attention_kernel, rows), "attention",
        [((rows.total - own, width), full), ((own, 2 * width), half), ((width, own), half), ((width, own), half)],
        [((rows.total - own, width), half), ((rows.total, 2 * width), half), ((rows.total, 2 * width), half)],
        40 * macs, 0, low_x, odd_x, low_y, odd_y, pool_tokens, flags, bias, query, kv, d_att, w_qkv[:, width:],
    )
    mixed, own_back = call(
        functools.partial(final_kernel, rows), "final", [((own, width), half), ((own, width), full)],
        [], 8 * macs, 1, block_mask, flat_tokens, grad_flat, att, d_query, d_kv, w_qkv, w_out,
    )

    def piece(start, count):
        return back[start - own : start - own + count]

    row_grad = piece(rows.pool, count_x * blocks).reshape(count_x // 2, 2, blocks, width)
    col_grad = piece(rows.pool + count_x * blocks, count_y * blocks)
    low_edge, odd_edge = (
        piece(start, edge).reshape(REACH, wide, width) for start in (rows.low_y, rows.odd_y)
    )

    def tall(start, cols):
        return jnp.concatenate(
            [low_edge[:, cols], piece(start, side).reshape(tile_rows, REACH, width), odd_edge[:, cols]], axis=0
        ).reshape(-1, width)

    tall_rows = tile_rows + 2 * REACH
    odd_got = lax.ppermute(
        tall(rows.odd_x, slice(wide - REACH, wide)).astype(half), "gx", pairs_odd(count_x, False)
    ).astype(full).reshape(tall_rows, REACH, width)
    low_got = lax.ppermute(
        jnp.concatenate([tall(rows.low_x, slice(0, REACH)), row_grad[:, 1].reshape(-1, width)], axis=0).astype(half),
        "gx",
        pairs_low(count_x),
    ).astype(full)
    row_grad = row_grad[:, 0].reshape(-1, width) + low_got[tall_rows * REACH :]
    low_got = low_got[: tall_rows * REACH].reshape(tall_rows, REACH, width)
    for step in reversed(steps_above(count_x, 2)):
        middle = row_grad.shape[0] // 2
        row_grad = row_grad[:middle] + lax.ppermute(
            row_grad[middle:].astype(half), "gx", pairs_far(count_x, step)
        ).astype(full)
    at_first = jnp.where(even_x, odd_got, low_got)
    at_last = jnp.where(even_x, low_got, odd_got)
    room = tile_cols - REACH
    added = jnp.pad(at_first, ((0, 0), (0, room), (0, 0))) + jnp.pad(at_last, ((0, 0), (room, 0), (0, 0)))
    inner = slice(REACH, REACH + tile_cols)
    low_send = (low_edge[:, inner] + added[:REACH]).reshape(-1, width)
    odd_send = (odd_edge[:, inner] + added[tall_rows - REACH :]).reshape(-1, width)
    for step in reversed(steps_above(count_y // 2, 2)):
        middle = col_grad.shape[0] // 2
        col_grad = col_grad[:middle] + lax.ppermute(
            col_grad[middle:].astype(half), "gy", window_pairs(count_y, step)
        ).astype(full)
    strip = REACH * tile_cols
    got = lax.ppermute(
        jnp.concatenate([odd_send, col_grad[2 * blocks :]], axis=0).astype(half), "gy", pairs_odd(count_y, True)
    ).astype(full)
    odd_rows = got[:strip].reshape(REACH, tile_cols, width)
    col_grad = col_grad[: 2 * blocks] + got[strip:]
    got = lax.ppermute(
        jnp.concatenate([low_send, col_grad[blocks:]], axis=0).astype(half), "gy", pairs_low(count_y)
    ).astype(full)
    low_rows = got[:strip].reshape(REACH, tile_cols, width)
    block_grad = col_grad[:blocks] + got[strip:] + row_grad
    at_top = jnp.where(even_y, odd_rows, low_rows)
    at_bottom = jnp.where(even_y, low_rows, odd_rows)
    room = tile_rows - REACH
    d_tokens = own_back.reshape(tile_rows, tile_cols, width) + added[REACH : REACH + tile_rows]
    d_tokens = d_tokens + jnp.pad(at_top, ((0, room), (0, 0), (0, 0))) + jnp.pad(at_bottom, ((room, 0), (0, 0), (0, 0)))
    shaped = (block_grad / TISSUE_BLOCK).reshape(tile_rows // TISSUE_BLOCK, tile_cols // TISSUE_BLOCK, width)
    d_tokens = d_tokens + jnp.repeat(jnp.repeat(shaped, TISSUE_BLOCK, 0), TISSUE_BLOCK, 1)
    return mixed.reshape(tile_rows, tile_cols, width), d_tokens.astype(half)


def solution(mesh):
    placed = (P("gy", "gx", None), P(), P(), P("gy", "gx"), P("gy", "gx", None))
    return jax.shard_map(
        local,
        mesh=mesh,
        in_specs=placed,
        out_specs=(P("gy", "gx", None), P("gy", "gx", None)),
        check_vma=False,
    )
```

time: 41.6 us -> 39.7 us (0.954)
  the two profiles are of different devices: /device:TPU:22 before, /device:TPU:0 now
where the time goes in v2:
time: 39.7 us; the launch traced here: 39.4 us
  starting transfers between devices  22.3 us (56%)
  Pallas kernels  5.25 us (13%)
  waiting for transfers between devices  5.13 us (13%)
  local copies, waits for them, and re-layouts  3.3 us (8%)
  other arithmetic  2.26 us (6%)
  between operations  1.21 us (3%)
    ppermute x1, starting transfers between devices, local(): lax.ppermute(jnp.concatenate([jnp.where(even_x, last, first), mine], axis...  5.8 us
    pallas_call x3, Pallas kernels, call(): pl.pallas_call(kernel, out_shape=tuple((jax.ShapeDtypeStruct(shape, dtype...  5.25 us
    ppermute x2, starting transfers between devices, local(): lax.ppermute(row_grad[middle:].astype(half), 'gx', pairs_far(count_x, step))  4.63 us
    ppermute x1, starting transfers between devices, local(): lax.ppermute(jnp.concatenate([tall(rows.low_x, slice(0, REACH)), row_grad...  4.35 us
    ppermute x2, starting transfers between devices, local(): lax.ppermute(row_pool, 'gx', pairs_far(count_x, step))  4.3 us
    ppermute x2, waiting for transfers between devices, local(): lax.ppermute(row_grad[middle:].astype(half), 'gx', pairs_far(count_x, step))  2.11 us
    ppermute x2, waiting for transfers between devices, local(): lax.ppermute(row_pool, 'gx', pairs_far(count_x, step))  1.62 us
    ppermute x1, starting transfers between devices, local(): lax.ppermute(jnp.concatenate([jnp.where(even_y, top, bottom), mine, low_y...  1.37 us
  transfers between devices with their start and end apart: 12, of which 6 were waited for; matrix products, arithmetic and copies ran while one was open for 6% of the time, Pallas kernels for 6%

profile of v2, /device:TPU:0, one launch (start us, length us, event | category | flops | bytes accessed | tf_op | source)
XLA Modules:
  0.0 39.4 jit_solution(5052247554229367427)
XLA Ops:
  0.6 0.0 copy-start.1
  0.7 0.9 %broadcast_select_fusion.2 = (bf16[8,3,384]{2,1,0:T(4,128)(2,1)S(1)}, bf16[8,3,384]{2,1,0:T(4,128)(2,1)S(1)}) fusion(pred[]{:T(512)S(6)} %eq.11, bf16[8,16,384]{2,1,0:T(8,128)(2,1)} %param.8), kind=kLoop, calls=%fused_computation.42 | loop fusion | flops 18432 | bytes 73729 | tf_op jit(solution)/shard_map/jit(_where)/select_n | solution.py:242
  1.6 0.0 copy-start.4
  1.6 0.7 %collective-permute-start.1 = (bf16[24,384]{1,0:T(8,128)(2,1)S(1)}, bf16[24,384]{1,0:T(8,128)(2,1)S(1)}, u32[]{:S(2)}, u32[]{:S(2)}) collective-permute-start(bf16[24,384]{1,0:T(8,128)(2,1)S(1)} %select_n.102), channel_id=1, source_target_pairs={{1,2},{2,1},{3,4},{4,3},{5,6},{6,5},{9,10},{10,9},{11,12},{12,11},... | collective-permute-start | bytes 55304 | tf_op jit(solution)/shard_map/ppermute | solution.py:242
  2.3 0.0 copy-done.1
  2.3 0.0 copy-done.4
  2.4 0.1 broadcast_in_dim.21
  2.5 5.8 %collective-permute-start = (bf16[28,384]{1,0:T(8,128)(2,1)S(1)}, bf16[28,384]{1,0:T(8,128)(2,1)S(1)}, u32[]{:S(2)}, u32[]{:S(2)}) collective-permute-start(bf16[28,384]{1,0:T(8,128)(2,1)S(1)} %pad_maximum_fusion.10), channel_id=1, source_target_pairs={{0,1},{1,0},{2,3},{3,2},{4,5},{5,4},{6,7},{7,6},{8,9},{9,8},{10,11... | collective-permute-start | bytes 64520 | tf_op jit(solution)/shard_map/ppermute | solution.py:249
  8.3 0.7 %dynamic-slice_bitcast_fusion = s32[384,2]{0,1:T(2,128)S(1)} fusion(s32[2,2,384,2]{2,3,1,0:T(2,128)} %constant.59.clone, s32[]{:T(128)S(6)} %select_n.109, s32[]{:T(128)S(6)} %select_n.110), kind=kLoop, calls=%fused_computation.61 | loop fusion | bytes 6152 | tf_op jit(solution)/shard_map/squeeze | solution.py:102
  9.0 0.0 copy-start.6
  9.0 0.6 %copy-done.5 = s32[128]{0:T(128)S(1)} copy-done((s32[128]{0:T(128)S(1)}, s32[128]{0:T(128)}, u32[]{:S(2)}) %copy-start.5) | copy-done | bytes 536
  9.7 0.0 copy-done.6
  9.7 0.2 fusion.10.bias_ref
  9.9 0.0 copy-start
  9.9 1.2 %slice.156.wkv_ref = bf16[384,768]{1,0:T(8,128)(2,1)S(1)} slice(bf16[384,1152]{1,0:T(8,128)(2,1)} %wqkv_ref.3), slice={[0:384], [384:1152]} | slice | bytes 1179648 | tf_op jit(solution)/shard_map/slice | solution.py:283
  11.1 0.0 collective-permute-done.1.odd_x_ref
  11.1 0.0 collective-permute-done.low_x_ref
  11.2 0.1 broadcast_select_fusion
  11.2 0.0 copy-start.2
  11.3 0.1 collective-permute-start.2
  11.4 1.6 %collective-permute-start.4 = (bf16[8,384]{1,0:T(8,128)(2,1)S(1)}, bf16[8,384]{1,0:T(8,128)(2,1)S(1)}, u32[]{:S(2)}, u32[]{:S(2)}) collective-permute-start(bf16[8,384]{1,0:T(8,128)(2,1)S(1)} %pad_maximum_fusion.12), channel_id=1, source_target_pairs={{0,2},{1,3},{2,0},{3,1},{4,6},{5,7},{6,4},{7,5},{8,10},{9,11},{10,... | collective-permute-start | bytes 18440 | tf_op jit(solution)/shard_map/ppermute | solution.py:254
  13.1 0.0 copy-start.3
  13.1 0.0 collective-permute-done.2.low_y_ref
  13.1 1.4 %collective-permute-start.3 = (bf16[74,384]{1,0:T(8,128)(2,1)S(1)}, bf16[74,384]{1,0:T(8,128)(2,1)S(1)}, u32[]{:S(2)}, u32[]{:S(2)}) collective-permute-start(bf16[74,384]{1,0:T(8,128)(2,1)S(1)} %pad_maximum_fusion), channel_id=1, source_target_pairs={{0,24},{8,16},{16,8},{24,0},{1,25},{9,17},{17,9},{25,1},{2,26},{10... | collective-permute-start | bytes 170504 | tf_op jit(solution)/shard_map/ppermute | solution.py:262
  14.5 0.6 %collective-permute-done.4 = bf16[8,384]{1,0:T(8,128)(2,1)S(1)} collective-permute-done((bf16[8,384]{1,0:T(8,128)(2,1)S(1)}, bf16[8,384]{1,0:T(8,128)(2,1)S(1)}, u32[]{:S(2)}, u32[]{:S(2)}) %collective-permute-start.4) | collective-permute-done | bytes 6176 | tf_op jit(solution)/shard_map/ppermute | solution.py:254
  15.1 2.7 %collective-permute-start.5 = (bf16[16,384]{1,0:T(8,128)(2,1)S(1)}, bf16[16,384]{1,0:T(8,128)(2,1)S(1)}, u32[]{:S(2)}, u32[]{:S(2)}) collective-permute-start(bf16[16,384]{1,0:T(8,128)(2,1)S(1)} %pad_maximum_fusion.11), channel_id=1, source_target_pairs={{0,4},{1,5},{2,6},{3,7},{4,0},{5,1},{6,2},{7,3},{8,12},{9,13},{10,... | collective-permute-start | bytes 36872 | tf_op jit(solution)/shard_map/ppermute | solution.py:254
  17.8 0.0 copy-done
  17.8 0.0 copy-done.2
  17.8 0.0 copy-done.3
  17.8 0.9 %own.1 = (bf16[128,384]{1,0:T(8,128)(2,1)S(1)}, bf16[128,768]{1,0:T(8,128)(2,1)S(1)}, bf16[128,384]{1,0:T(8,128)(2,1)S(1)}) custom-call(s32[1,2]{1,0:T(1,128)S(1)} %copy-done.4, bf16[128,384]{1,0:T(8,128)(2,1)S(1)} %bitcast.29, bf16[128,384]{1,0:T(8,128)(2,1)S(1)} %bitcast.31, bf16[384,1152]{1,0:T(8,128)(2,1)S(1)} %copy-done, bf16[384,384]{1,0:T(8,128)(2,1)S(1)} %copy-done.2), custom_call_target="tpu_custom_call" | custom-call | flops 150994944 | bytes 1376264 | tf_op jit(solution)/shard_map/own/pallas_call | solution.py:217
  18.7 0.0 collective-permute-done.3.odd_y_ref
  18.8 1.0 %collective-permute-done.5 = bf16[16,384]{1,0:T(8,128)(2,1)S(1)} collective-permute-done((bf16[16,384]{1,0:T(8,128)(2,1)S(1)}, bf16[16,384]{1,0:T(8,128)(2,1)S(1)}, u32[]{:S(2)}, u32[]{:S(2)}) %collective-permute-start.5) | collective-permute-done | bytes 12320 | tf_op jit(solution)/shard_map/ppermute | solution.py:254
  19.8 0.1 concatenate.54
  20.0 2.7 %attention.1 = (f32[256,384]{1,0:T(8,128)S(1)}, bf16[128,768]{1,0:T(8,128)(2,1)S(1)}, bf16[384,128]{1,0:T(8,128)(2,1)S(1)}, bf16[384,128]{1,0:T(8,128)(2,1)S(1)}) custom-call(bf16[28,384]{1,0:T(8,128)(2,1)S(1)} %collective-permute-done.low_x_ref, bf16[24,384]{1,0:T(8,128)(2,1)S(1)} %collective-permute-done.1.odd_x_ref, ...), custom_call_target="tpu_custom_call" | custom-call | flops 754974720 | bytes 1371136 | tf_op jit(solution)/shard_map/attention/pallas_call | solution.py:217
  23.2 0.7 %collective-permute-start.6 = (bf16[42,384]{1,0:T(8,128)(2,1)S(1)}, bf16[42,384]{1,0:T(8,128)(2,1)S(1)}, u32[]{:S(2)}, u32[]{:S(2)}) collective-permute-start(bf16[42,384]{1,0:T(8,128)(2,1)S(1)} %convert_element_type.63), channel_id=1, source_target_pairs={{1,2},{2,1},{3,4},{4,3},{5,6},{6,5},{9,10},{10,9},{11,12},{12,11},... | collective-permute-start | bytes 96776 | tf_op jit(solution)/shard_map/ppermute | solution.py:305
  23.9 4.3 %collective-permute-start.7 = (bf16[50,384]{1,0:T(8,128)(2,1)S(1)}, bf16[50,384]{1,0:T(8,128)(2,1)S(1)}, u32[]{:S(2)}, u32[]{:S(2)}) collective-permute-start(bf16[50,384]{1,0:T(8,128)(2,1)S(1)} %pad_maximum_fusion.7), channel_id=1, source_target_pairs={{0,1},{1,0},{2,3},{3,2},{4,5},{5,4},{6,7},{7,6},{8,9},{9,8},{10,11... | collective-permute-start | bytes 115208 | tf_op jit(solution)/shard_map/ppermute | solution.py:308
  28.3 1.6 %final.1 = (bf16[128,384]{1,0:T(8,128)(2,1)}, f32[128,384]{1,0:T(8,128)S(1)}) custom-call(s32[1,2]{1,0:T(1,128)S(1)} %copy-done.4, bf16[128,384]{1,0:T(8,128)(2,1)S(1)} %bitcast.30, bf16[128,384]{1,0:T(8,128)(2,1)S(1)} %bitcast.32, bf16[384,128]{1,0:T(8,128)(2,1)S(1)} %get-tuple-element.14.att_ref, bf16[384,128]{1,0:T(8,128)(2,1)S(1)} %get-tuple-element.15.dq_ref, ...), custom_call_target="tpu_custom_call" | custom-call | flops 150994944 | bytes 1769480 | tf_op jit(solution)/shard_map/final/pallas_call | solution.py:217
  29.8 0.4 collective-permute-done.7
  30.2 0.0 collective-permute-done.6
  30.4 0.1 collective-permute-start.8
  30.5 2.8 %collective-permute-start.10 = (bf16[4,384]{1,0:T(4,128)(2,1)S(1)}, bf16[4,384]{1,0:T(4,128)(2,1)S(1)}, u32[]{:S(2)}, u32[]{:S(2)}) collective-permute-start(bf16[4,384]{1,0:T(4,128)(2,1)S(1)} %slice.281), channel_id=1, source_target_pairs={{0,4},{1,5},{2,6},{3,7},{4,0},{5,1},{6,2},{7,3},{8,12},{9,13},{10,... | collective-permute-start | bytes 9224 | tf_op jit(solution)/shard_map/ppermute | solution.py:317
  33.3 1.0 %collective-permute-done.8 = bf16[52,384]{1,0:T(8,128)(2,1)S(1)} collective-permute-done((bf16[52,384]{1,0:T(8,128)(2,1)S(1)}, bf16[52,384]{1,0:T(8,128)(2,1)S(1)}, u32[]{:S(2)}, u32[]{:S(2)}) %collective-permute-start.8) | collective-permute-done | bytes 39968 | tf_op jit(solution)/shard_map/ppermute | solution.py:333
  34.4 0.4 collective-permute-start.9
  34.8 0.3 collective-permute-done.10
  35.1 1.8 %collective-permute-start.11 = (bf16[2,384]{1,0:T(2,128)(2,1)S(1)}, bf16[2,384]{1,0:T(2,128)(2,1)S(1)}, u32[]{:S(2)}, u32[]{:S(2)}) collective-permute-start(bf16[2,384]{1,0:T(2,128)(2,1)S(1)} %slice.282), channel_id=1, source_target_pairs={{0,2},{1,3},{2,0},{3,1},{4,6},{5,7},{6,4},{7,5},{8,10},{9,11},{10,... | collective-permute-start | bytes 4616 | tf_op jit(solution)/shard_map/ppermute | solution.py:317
  36.9 0.0 collective-permute-done.9
  36.9 1.8 %collective-permute-done.11 = bf16[2,384]{1,0:T(2,128)(2,1)S(1)} collective-permute-done((bf16[2,384]{1,0:T(2,128)(2,1)S(1)}, bf16[2,384]{1,0:T(2,128)(2,1)S(1)}, u32[]{:S(2)}, u32[]{:S(2)}) %collective-permute-start.11) | collective-permute-done | bytes 1568 | tf_op jit(solution)/shard_map/ppermute | solution.py:317
  38.7 0.7 %fusion.5 = bf16[8,16,384]{2,1,0:T(8,128)(2,1)} fusion(f32[8,16,384]{2,1,0:T(8,128)S(1)} %bitcast.33, f32[14,3,384]{2,1,0:T(4,128)S(1)} %select_n.114, f32[14,3,384]{2,1,0:T(4,128)S(1)} %select_n.116, f32[3,16,384]{2,1,0:T(8,128)S(1)} %bitcast.35, f32[3,16,384]{2,1,0:T(8,128)S(1)} %bitcast.34, f32[16,384]{1,0:T(8,128)S(1)} %broadcast_bitcast_fusion), kind=kLoop, calls=%fused_computation.9 | loop fusion | flops 294912 | bytes 595968 | tf_op jit(solution)/shard_map/convert_element_type | solution.py:350
  (69 shorter events, 1.0 us)
Async XLA Ops:
  0.6 1.6 %copy-start.1 = (bf16[8,16,384]{2,1,0:T(8,128)(2,1)S(1)}, bf16[8,16,384]{2,1,0:T(8,128)(2,1)}, u32[]{:S(2)}) copy-start(bf16[8,16,384]{2,1,0:T(8,128)(2,1)} %param.8) | copy-start | bytes 294916
  1.6 0.7 %copy-start.4 = (s32[1,2]{1,0:T(1,128)S(1)}, s32[1,2]{1,0:T(1,128)}, u32[]{:S(2)}) copy-start(s32[1,2]{1,0:T(1,128)} %mask_ref.3) | copy-start | bytes 28
  1.6 9.5 %collective-permute-start.1 = (bf16[24,384]{1,0:T(8,128)(2,1)S(1)}, bf16[24,384]{1,0:T(8,128)(2,1)S(1)}, u32[]{:S(2)}, u32[]{:S(2)}) collective-permute-start(bf16[24,384]{1,0:T(8,128)(2,1)S(1)} %select_n.102), channel_id=1, source_target_pairs={{1,2},{2,1},{3,4},{4,3},{5,6},{6,5},{9,10},{10,9},{11,12},{12,11},... | collective-permute-start | bytes 55304 | tf_op jit(solution)/shard_map/ppermute | solution.py:242
  2.5 8.7 %collective-permute-start = (bf16[28,384]{1,0:T(8,128)(2,1)S(1)}, bf16[28,384]{1,0:T(8,128)(2,1)S(1)}, u32[]{:S(2)}, u32[]{:S(2)}) collective-permute-start(bf16[28,384]{1,0:T(8,128)(2,1)S(1)} %pad_maximum_fusion.10), channel_id=1, source_target_pairs={{0,1},{1,0},{2,3},{3,2},{4,5},{5,4},{6,7},{7,6},{8,9},{9,8},{10,11... | collective-permute-start | bytes 64520 | tf_op jit(solution)/shard_map/ppermute | solution.py:249
  9.0 0.7 %copy-start.5 = (s32[128]{0:T(128)S(1)}, s32[128]{0:T(128)}, u32[]{:S(2)}) copy-start(s32[128]{0:T(128)} %constant.78) | copy-start | bytes 1540
  9.0 0.7 %copy-start.6 = (s32[128]{0:T(128)S(1)}, s32[128]{0:T(128)}, u32[]{:S(2)}) copy-start(s32[128]{0:T(128)} %constant.77) | copy-start | bytes 1540
  9.9 7.9 %copy-start = (bf16[384,1152]{1,0:T(8,128)(2,1)S(1)}, bf16[384,1152]{1,0:T(8,128)(2,1)}, u32[]{:S(2)}) copy-start(bf16[384,1152]{1,0:T(8,128)(2,1)} %wqkv_ref.3) | copy-start | bytes 2654212
  11.2 6.5 %copy-start.2 = (bf16[384,384]{1,0:T(8,128)(2,1)S(1)}, bf16[384,384]{1,0:T(8,128)(2,1)}, u32[]{:S(2)}) copy-start(bf16[384,384]{1,0:T(8,128)(2,1)} %wout_ref.3) | copy-start | bytes 884740
  11.3 1.8 %collective-permute-start.2 = (bf16[70,384]{1,0:T(8,128)(2,1)S(1)}, bf16[70,384]{1,0:T(8,128)(2,1)S(1)}, u32[]{:S(2)}, u32[]{:S(2)}) collective-permute-start(bf16[70,384]{1,0:T(8,128)(2,1)S(1)} %pad_maximum_fusion.4), channel_id=1, source_target_pairs={{0,8},{8,0},{16,24},{24,16},{1,9},{9,1},{17,25},{25,17},{2,10},{10... | collective-permute-start | bytes 161288 | tf_op jit(solution)/shard_map/ppermute | solution.py:259
  11.4 3.7 %collective-permute-start.4 = (bf16[8,384]{1,0:T(8,128)(2,1)S(1)}, bf16[8,384]{1,0:T(8,128)(2,1)S(1)}, u32[]{:S(2)}, u32[]{:S(2)}) collective-permute-start(bf16[8,384]{1,0:T(8,128)(2,1)S(1)} %pad_maximum_fusion.12), channel_id=1, source_target_pairs={{0,2},{1,3},{2,0},{3,1},{4,6},{5,7},{6,4},{7,5},{8,10},{9,11},{10,... | collective-permute-start | bytes 18440 | tf_op jit(solution)/shard_map/ppermute | solution.py:254
  13.1 4.7 %copy-start.3 = (bf16[8,16,384]{2,1,0:T(8,128)(2,1)S(1)}, bf16[8,16,384]{2,1,0:T(8,128)(2,1)}, u32[]{:S(2)}) copy-start(bf16[8,16,384]{2,1,0:T(8,128)(2,1)} %param.12) | copy-start | bytes 294916
  13.1 5.6 %collective-permute-start.3 = (bf16[74,384]{1,0:T(8,128)(2,1)S(1)}, bf16[74,384]{1,0:T(8,128)(2,1)S(1)}, u32[]{:S(2)}, u32[]{:S(2)}) collective-permute-start(bf16[74,384]{1,0:T(8,128)(2,1)S(1)} %pad_maximum_fusion), channel_id=1, source_target_pairs={{0,24},{8,16},{16,8},{24,0},{1,25},{9,17},{17,9},{25,1},{2,26},{10... | collective-permute-start | bytes 170504 | tf_op jit(solution)/shard_map/ppermute | solution.py:262
  15.1 4.7 %collective-permute-start.5 = (bf16[16,384]{1,0:T(8,128)(2,1)S(1)}, bf16[16,384]{1,0:T(8,128)(2,1)S(1)}, u32[]{:S(2)}, u32[]{:S(2)}) collective-permute-start(bf16[16,384]{1,0:T(8,128)(2,1)S(1)} %pad_maximum_fusion.11), channel_id=1, source_target_pairs={{0,4},{1,5},{2,6},{3,7},{4,0},{5,1},{6,2},{7,3},{8,12},{9,13},{10,... | collective-permute-start | bytes 36872 | tf_op jit(solution)/shard_map/ppermute | solution.py:254
  23.2 7.1 %collective-permute-start.6 = (bf16[42,384]{1,0:T(8,128)(2,1)S(1)}, bf16[42,384]{1,0:T(8,128)(2,1)S(1)}, u32[]{:S(2)}, u32[]{:S(2)}) collective-permute-start(bf16[42,384]{1,0:T(8,128)(2,1)S(1)} %convert_element_type.63), channel_id=1, source_target_pairs={{1,2},{2,1},{3,4},{4,3},{5,6},{6,5},{9,10},{10,9},{11,12},{12,11},... | collective-permute-start | bytes 96776 | tf_op jit(solution)/shard_map/ppermute | solution.py:305
  23.9 6.4 %collective-permute-start.7 = (bf16[50,384]{1,0:T(8,128)(2,1)S(1)}, bf16[50,384]{1,0:T(8,128)(2,1)S(1)}, u32[]{:S(2)}, u32[]{:S(2)}) collective-permute-start(bf16[50,384]{1,0:T(8,128)(2,1)S(1)} %pad_maximum_fusion.7), channel_id=1, source_target_pairs={{0,1},{1,0},{2,3},{3,2},{4,5},{5,4},{6,7},{7,6},{8,9},{9,8},{10,11... | collective-permute-start | bytes 115208 | tf_op jit(solution)/shard_map/ppermute | solution.py:308
  30.4 3.9 %collective-permute-start.8 = (bf16[52,384]{1,0:T(8,128)(2,1)S(1)}, bf16[52,384]{1,0:T(8,128)(2,1)S(1)}, u32[]{:S(2)}, u32[]{:S(2)}) collective-permute-start(bf16[52,384]{1,0:T(8,128)(2,1)S(1)} %pad_maximum_fusion.8), channel_id=1, source_target_pairs={{0,24},{8,16},{16,8},{24,0},{1,25},{9,17},{17,9},{25,1},{2,26},{10... | collective-permute-start | bytes 119816 | tf_op jit(solution)/shard_map/ppermute | solution.py:333
  30.5 4.6 %collective-permute-start.10 = (bf16[4,384]{1,0:T(4,128)(2,1)S(1)}, bf16[4,384]{1,0:T(4,128)(2,1)S(1)}, u32[]{:S(2)}, u32[]{:S(2)}) collective-permute-start(bf16[4,384]{1,0:T(4,128)(2,1)S(1)} %slice.281), channel_id=1, source_target_pairs={{0,4},{1,5},{2,6},{3,7},{4,0},{5,1},{6,2},{7,3},{8,12},{9,13},{10,... | collective-permute-start | bytes 9224 | tf_op jit(solution)/shard_map/ppermute | solution.py:317
  34.4 2.5 %collective-permute-start.9 = (bf16[50,384]{1,0:T(8,128)(2,1)S(1)}, bf16[50,384]{1,0:T(8,128)(2,1)S(1)}, u32[]{:S(2)}, u32[]{:S(2)}) collective-permute-start(bf16[50,384]{1,0:T(8,128)(2,1)S(1)} %pad_maximum_fusion.9), channel_id=1, source_target_pairs={{0,8},{8,0},{16,24},{24,16},{1,9},{9,1},{17,25},{25,17},{2,10},{10... | collective-permute-start | bytes 115208 | tf_op jit(solution)/shard_map/ppermute | solution.py:338
  35.1 3.6 %collective-permute-start.11 = (bf16[2,384]{1,0:T(2,128)(2,1)S(1)}, bf16[2,384]{1,0:T(2,128)(2,1)S(1)}, u32[]{:S(2)}, u32[]{:S(2)}) collective-permute-start(bf16[2,384]{1,0:T(2,128)(2,1)S(1)} %slice.282), channel_id=1, source_target_pairs={{0,2},{1,3},{2,0},{3,1},{4,6},{5,7},{6,4},{7,5},{8,10},{9,11},{10,... | collective-permute-start | bytes 4616 | tf_op jit(solution)/shard_map/ppermute | solution.py:317

commit v3 on v2

--- a/solution.py
+++ b/solution.py
@@ -191,7 +191,7 @@
         for h, head in enumerate(heads):
             part = DOT(keys_t[head], score_grad[:, h * own : (h + 1) * own], NN) * SCALE
             dq_ref[head] = part.astype(jnp.bfloat16)
-    back_ref[...] = DOT(all_dkv_ref[own:], wkv_ref[...], NT)
+    back_ref[...] = DOT(all_dkv_ref[own:], wkv_ref[...], NT).astype(jnp.bfloat16)
     dkv_ref[...] = all_dkv_ref[:own]
 
 
@@ -226,6 +226,11 @@
     )(*operands)
 
 
+def swap(name, value, axis, moves):
+    with jax.named_scope(name):
+        return lax.ppermute(value, axis, moves)
+
+
 def local(tokens, w_qkv, w_out, block_mask, grad_out):
     tile_rows, tile_cols, width = tokens.shape
     count_y, count_x = lax.axis_size("gy"), lax.axis_size("gx")
@@ -239,32 +244,32 @@
 
     first = tokens[:, :REACH].reshape(side, width)
     last = tokens[:, tile_cols - REACH :].reshape(side, width)
-    odd_x = lax.ppermute(jnp.where(even_x, first, last), "gx", pairs_odd(count_x, False))
+    odd_x = swap("r1_odd_columns", jnp.where(even_x, first, last), "gx", pairs_odd(count_x, False))
     grouped = tokens.astype(full).reshape(
         tile_rows // TISSUE_BLOCK, TISSUE_BLOCK, tile_cols // TISSUE_BLOCK, TISSUE_BLOCK, width
     )
     sums = (jnp.sum(grouped, axis=(1, 3)) / TISSUE_BLOCK).reshape(blocks, width).astype(half)
     marks = jnp.broadcast_to(block_mask.reshape(blocks, 1), (blocks, width)).astype(half)
     mine = jnp.concatenate([sums, marks], axis=0)
-    low_x = lax.ppermute(
+    low_x = swap("r1_low_columns",
         jnp.concatenate([jnp.where(even_x, last, first), mine], axis=0), "gx", pairs_low(count_x)
     )
     row_pool = jnp.concatenate([mine, low_x[side:]], axis=0)
     for step in steps_above(count_x, 2):
-        row_pool = jnp.concatenate([row_pool, lax.ppermute(row_pool, "gx", pairs_far(count_x, step))], axis=0)
+        row_pool = jnp.concatenate([row_pool, swap(f"r1_far_columns_{step}", row_pool, "gx", pairs_far(count_x, step))], axis=0)
     spread = jnp.concatenate(
         [low_x[:side].reshape(tile_rows, REACH, width), tokens, odd_x.reshape(tile_rows, REACH, width)], axis=1
     )
     top, bottom = spread[:REACH].reshape(edge, width), spread[tile_rows - REACH :].reshape(edge, width)
-    low_y = lax.ppermute(
+    low_y = swap("r1_low_rows",
         jnp.concatenate([jnp.where(even_y, bottom, top), mine], axis=0), "gy", pairs_low(count_y)
     )
-    odd_y = lax.ppermute(
+    odd_y = swap("r1_odd_rows",
         jnp.concatenate([jnp.where(even_y, top, bottom), mine, low_y[edge:]], axis=0), "gy", pairs_odd(count_y, True)
     )
     col_pool = jnp.concatenate([mine, low_y[edge:], odd_y[edge:]], axis=0)
     for step in steps_above(count_y // 2, 2):
-        col_pool = jnp.concatenate([col_pool, lax.ppermute(col_pool, "gy", window_pairs(count_y, step))], axis=0)
+        col_pool = jnp.concatenate([col_pool, swap(f"r1_far_rows_{step}", col_pool, "gy", window_pairs(count_y, step))], axis=0)
     pool = jnp.concatenate([row_pool, col_pool], axis=0).reshape(count_x + count_y, 2, blocks, width)
     spare = ((0, rows.total - rows.used), (0, 0))
     pool_tokens = jnp.pad(pool[:, 0].reshape(-1, width), spare)
@@ -278,7 +283,7 @@
     bias = window_bias(rows, count_y, count_x)
     back, d_kv, att, d_query = call(
         functools.partial(attention_kernel, rows), "attention",
-        [((rows.total - own, width), full), ((own, 2 * width), half), ((width, own), half), ((width, own), half)],
+        [((rows.total - own, width), half), ((own, 2 * width), half), ((width, own), half), ((width, own), half)],
         [((rows.total - own, width), half), ((rows.total, 2 * width), half), ((rows.total, 2 * width), half)],
         40 * macs, 0, low_x, odd_x, low_y, odd_y, pool_tokens, flags, bias, query, kv, d_att, w_qkv[:, width:],
     )
@@ -290,61 +295,60 @@
     def piece(start, count):
         return back[start - own : start - own + count]
 
-    row_grad = piece(rows.pool, count_x * blocks).reshape(count_x // 2, 2, blocks, width)
+    def fold(grads, got):
+        return (grads.astype(full) + got.astype(full)).astype(half)
+
+    row_grad = piece(rows.pool, count_x * blocks)
     col_grad = piece(rows.pool + count_x * blocks, count_y * blocks)
-    low_edge, odd_edge = (
-        piece(start, edge).reshape(REACH, wide, width) for start in (rows.low_y, rows.odd_y)
-    )
-
-    def tall(start, cols):
-        return jnp.concatenate(
-            [low_edge[:, cols], piece(start, side).reshape(tile_rows, REACH, width), odd_edge[:, cols]], axis=0
-        ).reshape(-1, width)
-
-    tall_rows = tile_rows + 2 * REACH
-    odd_got = lax.ppermute(
-        tall(rows.odd_x, slice(wide - REACH, wide)).astype(half), "gx", pairs_odd(count_x, False)
-    ).astype(full).reshape(tall_rows, REACH, width)
-    low_got = lax.ppermute(
-        jnp.concatenate([tall(rows.low_x, slice(0, REACH)), row_grad[:, 1].reshape(-1, width)], axis=0).astype(half),
+    for step in reversed(steps_above(count_x, 2)):
+        if step == 2:
+            row_grad, own_back = lax.optimization_barrier((row_grad, own_back))
+        middle = row_grad.shape[0] // 2
+        got = swap(f"r2_far_columns_{step}", row_grad[middle:], "gx", pairs_far(count_x, step))
+        row_grad = fold(row_grad[:middle], got)
+    for step in reversed(steps_above(count_y // 2, 2)):
+        middle = col_grad.shape[0] // 2
+        got = swap(f"r2_far_rows_{step}", col_grad[middle:], "gy", window_pairs(count_y, step))
+        col_grad = fold(col_grad[:middle], got)
+    odd_rows = swap(
+        "r2_odd_rows",
+        jnp.concatenate([piece(rows.odd_y, edge), col_grad[2 * blocks :]], axis=0),
+        "gy",
+        pairs_odd(count_y, True),
+    )
+    col_grad = fold(col_grad[: 2 * blocks], odd_rows[edge:])
+    low_rows = swap(
+        "r2_low_rows", jnp.concatenate([piece(rows.low_y, edge), col_grad[blocks:]], axis=0), "gy", pairs_low(count_y)
+    )
+    col_grad = fold(col_grad[:blocks], low_rows[edge:])
+    odd_rows = odd_rows[:edge].astype(full).reshape(REACH, wide, width)
+    low_rows = low_rows[:edge].astype(full).reshape(REACH, wide, width)
+    at_top, at_bottom = jnp.where(even_y, odd_rows, low_rows), jnp.where(even_y, low_rows, odd_rows)
+    room = tile_rows - REACH
+
+    def lines(start, stop):
+        top, bottom = at_top[:, start:stop], at_bottom[:, start:stop]
+        return jnp.pad(top, ((0, room), (0, 0), (0, 0))) + jnp.pad(bottom, ((room, 0), (0, 0), (0, 0)))
+
+    odd_side = piece(rows.odd_x, side).astype(full) + lines(wide - REACH, wide).reshape(side, width)
+    odd_got = swap("r2_odd_columns", odd_side.astype(half), "gx", pairs_odd(count_x, False))
+    low_side = piece(rows.low_x, side).astype(full) + lines(0, REACH).reshape(side, width)
+    low_got = swap(
+        "r2_low_columns",
+        jnp.concatenate([low_side.astype(half), row_grad[blocks:]], axis=0),
         "gx",
         pairs_low(count_x),
-    ).astype(full)
-    row_grad = row_grad[:, 0].reshape(-1, width) + low_got[tall_rows * REACH :]
-    low_got = low_got[: tall_rows * REACH].reshape(tall_rows, REACH, width)
-    for step in reversed(steps_above(count_x, 2)):
-        middle = row_grad.shape[0] // 2
-        row_grad = row_grad[:middle] + lax.ppermute(
-            row_grad[middle:].astype(half), "gx", pairs_far(count_x, step)
-        ).astype(full)
-    at_first = jnp.where(even_x, odd_got, low_got)
-    at_last = jnp.where(even_x, low_got, odd_got)
+    )
+    block_grad = row_grad[:blocks].astype(full) + low_got[side:].astype(full) + col_grad.astype(full)
+    odd_got = odd_got.astype(full).reshape(tile_rows, REACH, width)
+    low_got = low_got[:side].astype(full).reshape(tile_rows, REACH, width)
+    at_first, at_last = jnp.where(even_x, odd_got, low_got), jnp.where(even_x, low_got, odd_got)
     room = tile_cols - REACH
-    added = jnp.pad(at_first, ((0, 0), (0, room), (0, 0))) + jnp.pad(at_last, ((0, 0), (room, 0), (0, 0)))
-    inner = slice(REACH, REACH + tile_cols)
-    low_send = (low_edge[:, inner] + added[:REACH]).reshape(-1, width)
-    odd_send = (odd_edge[:, inner] + added[tall_rows - REACH :]).reshape(-1, width)
-    for step in reversed(steps_above(count_y // 2, 2)):
-        middle = col_grad.shape[0] // 2
-        col_grad = col_grad[:middle] + lax.ppermute(
-            col_grad[middle:].astype(half), "gy", window_pairs(count_y, step)
-        ).astype(full)
-    strip = REACH * tile_cols
-    got = lax.ppermute(
-        jnp.concatenate([odd_send, col_grad[2 * blocks :]], axis=0).astype(half), "gy", pairs_odd(count_y, True)
-    ).astype(full)
-    odd_rows = got[:strip].reshape(REACH, tile_cols, width)
-    col_grad = col_grad[: 2 * blocks] + got[strip:]
-    got = lax.ppermute(
-        jnp.concatenate([low_send, col_grad[blocks:]], axis=0).astype(half), "gy", pairs_low(count_y)
-    ).astype(full)
-    low_rows = got[:strip].reshape(REACH, tile_cols, width)
-    block_grad = col_grad[:blocks] + got[strip:] + row_grad
-    at_top = jnp.where(even_y, odd_rows, low_rows)
-    at_bottom = jnp.where(even_y, low_rows, odd_rows)
-    room = tile_rows - REACH
-    d_tokens = own_back.reshape(tile_rows, tile_cols, width) + added[REACH : REACH + tile_rows]
-    d_tokens = d_tokens + jnp.pad(at_top, ((0, room), (0, 0), (0, 0))) + jnp.pad(at_bottom, ((room, 0), (0, 0), (0, 0)))
+    d_tokens = own_back.reshape(tile_rows, tile_cols, width) + jnp.pad(
+        at_top[:, REACH : REACH + tile_cols], ((0, tile_rows - REACH), (0, 0), (0, 0))
+    )
+    d_tokens = d_tokens + jnp.pad(at_bottom[:, REACH : REACH + tile_cols], ((tile_rows - REACH, 0), (0, 0), (0, 0)))
+    d_tokens = d_tokens + jnp.pad(at_first, ((0, 0), (0, room), (0, 0))) + jnp.pad(at_last, ((0, 0), (room, 0), (0, 0)))
     shaped = (block_grad / TISSUE_BLOCK).reshape(tile_rows // TISSUE_BLOCK, tile_cols // TISSUE_BLOCK, width)
     d_tokens = d_tokens + jnp.repeat(jnp.repeat(shaped, TISSUE_BLOCK, 0), TISSUE_BLOCK, 1)
     return mixed.reshape(tile_rows, tile_cols, width), d_tokens.astype(half)

time: 39.7 us -> 38.4 us (0.967)
  the two profiles are of different devices: /device:TPU:0 before, /device:TPU:8 now
where the time goes in v3:
time: 38.4 us; the launch traced here: 38.2 us
  starting transfers between devices  15.5 us (40%)
  waiting for transfers between devices  11 us (29%)
  Pallas kernels  5.27 us (14%)
  local copies, waits for them, and re-layouts  3.16 us (8%)
  other arithmetic  2.13 us (6%)
  between operations  1.12 us (3%)
    ppermute x12, starting transfers between devices, swap(): return lax.ppermute(value, axis, moves)  15.5 us
    ppermute x12, waiting for transfers between devices, swap(): return lax.ppermute(value, axis, moves)  11 us
    pallas_call x3, Pallas kernels, call(): pl.pallas_call(kernel, out_shape=tuple((jax.ShapeDtypeStruct(shape, dtype...  5.27 us
    slice x1, local copies, waits for them, and re-layouts, local(): w_qkv[:, width:]  1.18 us
    select_n x1, other arithmetic, local(): jnp.where(even_x, first, last)  0.89 us
  transfers between devices with their start and end apart: 12, of which 7 were waited for; matrix products, arithmetic and copies ran while one was open for 7% of the time, Pallas kernels for 7%

profile of v3, /device:TPU:8, one launch (start us, length us, event | category | flops | bytes accessed | tf_op | source)
XLA Modules:
  0.0 38.2 jit_solution(18424805165144435223)
XLA Ops:
  0.6 0.0 copy-start.1
  0.7 0.9 %broadcast_select_fusion.2 = (bf16[8,3,384]{2,1,0:T(4,128)(2,1)S(1)}, bf16[8,3,384]{2,1,0:T(4,128)(2,1)S(1)}) fusion(pred[]{:T(512)S(6)} %eq.11, bf16[8,16,384]{2,1,0:T(8,128)(2,1)} %param.8), kind=kLoop, calls=%fused_computation.29 | loop fusion | flops 18432 | bytes 73729 | tf_op jit(solution)/shard_map/jit(_where)/select_n | solution.py:247
  1.6 0.0 copy-start.4
  1.6 3.3 %collective-permute-start.1 = (bf16[24,384]{1,0:T(8,128)(2,1)S(1)}, bf16[24,384]{1,0:T(8,128)(2,1)S(1)}, u32[]{:S(2)}, u32[]{:S(2)}) collective-permute-start(bf16[24,384]{1,0:T(8,128)(2,1)S(1)} %select_n.102), channel_id=1, source_target_pairs={{1,2},{2,1},{3,4},{4,3},{5,6},{6,5},{9,10},{10,9},{11,12},{12,11},... | collective-permute-start | bytes 55304 | tf_op jit(solution)/shard_map/r1_odd_columns/ppermute | solution.py:231
  4.9 0.0 copy-done.1
  4.9 0.0 copy-done.4
  5.0 0.1 broadcast_in_dim.21
  5.1 1.7 %collective-permute-start = (bf16[28,384]{1,0:T(8,128)(2,1)S(1)}, bf16[28,384]{1,0:T(8,128)(2,1)S(1)}, u32[]{:S(2)}, u32[]{:S(2)}) collective-permute-start(bf16[28,384]{1,0:T(8,128)(2,1)S(1)} %pad_maximum_fusion.7), channel_id=1, source_target_pairs={{0,1},{1,0},{2,3},{3,2},{4,5},{5,4},{6,7},{7,6},{8,9},{9,8},{10,11... | collective-permute-start | bytes 64520 | tf_op jit(solution)/shard_map/r1_low_columns/ppermute | solution.py:231
  6.8 0.7 %dynamic-slice_bitcast_fusion = s32[384,2]{0,1:T(2,128)S(1)} fusion(s32[2,2,384,2]{2,3,1,0:T(2,128)} %constant.59.clone, s32[]{:T(128)S(6)} %select_n.109, s32[]{:T(128)S(6)} %select_n.110), kind=kLoop, calls=%fused_computation.42 | loop fusion | bytes 6152 | tf_op jit(solution)/shard_map/squeeze | solution.py:102
  7.6 0.0 copy-start.6
  7.6 0.6 %copy-done.5 = s32[128]{0:T(128)S(1)} copy-done((s32[128]{0:T(128)S(1)}, s32[128]{0:T(128)}, u32[]{:S(2)}) %copy-start.5) | copy-done | bytes 536
  8.2 0.0 copy-done.6
  8.2 0.2 fusion.4.bias_ref
  8.5 0.0 copy-start
  8.5 1.2 %slice.136.wkv_ref = bf16[384,768]{1,0:T(8,128)(2,1)S(1)} slice(bf16[384,1152]{1,0:T(8,128)(2,1)} %wqkv_ref.3), slice={[0:384], [384:1152]} | slice | bytes 1179648 | tf_op jit(solution)/shard_map/slice | solution.py:288
  9.7 0.0 collective-permute-done.1.odd_x_ref
  9.7 0.0 collective-permute-done.low_x_ref
  9.7 0.1 broadcast_select_fusion
  9.8 0.0 copy-start.2
  9.9 0.1 collective-permute-start.2
  10.0 0.5 %collective-permute-start.4 = (bf16[8,384]{1,0:T(8,128)(2,1)S(1)}, bf16[8,384]{1,0:T(8,128)(2,1)S(1)}, u32[]{:S(2)}, u32[]{:S(2)}) collective-permute-start(bf16[8,384]{1,0:T(8,128)(2,1)S(1)} %pad_maximum_fusion.10), channel_id=1, source_target_pairs={{0,2},{1,3},{2,0},{3,1},{4,6},{5,7},{6,4},{7,5},{8,10},{9,11},{10,... | collective-permute-start | bytes 18440 | tf_op jit(solution)/shard_map/r1_far_columns_2/ppermute | solution.py:231
  10.5 0.0 copy-start.3
  10.5 0.6 %collective-permute-done.2.low_y_ref = bf16[70,384]{1,0:T(8,128)(2,1)S(1)} collective-permute-done((bf16[70,384]{1,0:T(8,128)(2,1)S(1)}, bf16[70,384]{1,0:T(8,128)(2,1)S(1)}, u32[]{:S(2)}, u32[]{:S(2)}) %collective-permute-start.2) | collective-permute-done | bytes 53792 | tf_op jit(solution)/shard_map/r1_low_rows/ppermute | solution.py:231
  11.2 1.3 %collective-permute-start.3 = (bf16[74,384]{1,0:T(8,128)(2,1)S(1)}, bf16[74,384]{1,0:T(8,128)(2,1)S(1)}, u32[]{:S(2)}, u32[]{:S(2)}) collective-permute-start(bf16[74,384]{1,0:T(8,128)(2,1)S(1)} %pad_maximum_fusion), channel_id=1, source_target_pairs={{0,24},{8,16},{16,8},{24,0},{1,25},{9,17},{17,9},{25,1},{2,26},{10... | collective-permute-start | bytes 170504 | tf_op jit(solution)/shard_map/r1_odd_rows/ppermute | solution.py:231
  12.5 1.1 %collective-permute-done.4 = bf16[8,384]{1,0:T(8,128)(2,1)S(1)} collective-permute-done((bf16[8,384]{1,0:T(8,128)(2,1)S(1)}, bf16[8,384]{1,0:T(8,128)(2,1)S(1)}, u32[]{:S(2)}, u32[]{:S(2)}) %collective-permute-start.4) | collective-permute-done | bytes 6176 | tf_op jit(solution)/shard_map/r1_far_columns_2/ppermute | solution.py:231
  13.7 2.0 %collective-permute-start.5 = (bf16[16,384]{1,0:T(8,128)(2,1)S(1)}, bf16[16,384]{1,0:T(8,128)(2,1)S(1)}, u32[]{:S(2)}, u32[]{:S(2)}) collective-permute-start(bf16[16,384]{1,0:T(8,128)(2,1)S(1)} %pad_maximum_fusion.9), channel_id=1, source_target_pairs={{0,4},{1,5},{2,6},{3,7},{4,0},{5,1},{6,2},{7,3},{8,12},{9,13},{10,... | collective-permute-start | bytes 36872 | tf_op jit(solution)/shard_map/r1_far_columns_4/ppermute | solution.py:231
  15.6 0.0 copy-done
  15.6 0.0 copy-done.2
  15.6 0.0 copy-done.3
  15.6 0.9 %own.1 = (bf16[128,384]{1,0:T(8,128)(2,1)S(1)}, bf16[128,768]{1,0:T(8,128)(2,1)S(1)}, bf16[128,384]{1,0:T(8,128)(2,1)S(1)}) custom-call(s32[1,2]{1,0:T(1,128)S(1)} %copy-done.4, bf16[128,384]{1,0:T(8,128)(2,1)S(1)} %bitcast.19, bf16[128,384]{1,0:T(8,128)(2,1)S(1)} %bitcast.21, bf16[384,1152]{1,0:T(8,128)(2,1)S(1)} %copy-done, bf16[384,384]{1,0:T(8,128)(2,1)S(1)} %copy-done.2), custom_call_target="tpu_custom_call" | custom-call | flops 150994944 | bytes 1376264 | tf_op jit(solution)/shard_map/own/pallas_call | solution.py:217
  16.6 0.0 collective-permute-done.3.odd_y_ref
  16.6 1.7 %collective-permute-done.5 = bf16[16,384]{1,0:T(8,128)(2,1)S(1)} collective-permute-done((bf16[16,384]{1,0:T(8,128)(2,1)S(1)}, bf16[16,384]{1,0:T(8,128)(2,1)S(1)}, u32[]{:S(2)}, u32[]{:S(2)}) %collective-permute-start.5) | collective-permute-done | bytes 12320 | tf_op jit(solution)/shard_map/r1_far_columns_4/ppermute | solution.py:231
  18.3 0.1 concatenate.43
  18.5 2.7 %attention.1 = (bf16[256,384]{1,0:T(8,128)(2,1)S(1)}, bf16[128,768]{1,0:T(8,128)(2,1)S(1)}, bf16[384,128]{1,0:T(8,128)(2,1)S(1)}, bf16[384,128]{1,0:T(8,128)(2,1)S(1)}) custom-call(bf16[28,384]{1,0:T(8,128)(2,1)S(1)} %collective-permute-done.low_x_ref, bf16[24,384]{1,0:T(8,128)(2,1)S(1)} %collective-permute-done.1.odd_x_ref, ...), custom_call_target="tpu_custom_call" | custom-call | flops 754974720 | bytes 1371136 | tf_op jit(solution)/shard_map/attention/pallas_call | solution.py:217
  21.3 2.0 %collective-permute-start.6 = (bf16[8,384]{1,0:T(8,128)(2,1)S(1)}, bf16[8,384]{1,0:T(8,128)(2,1)S(1)}, u32[]{:S(2)}, u32[]{:S(2)}) collective-permute-start(bf16[8,384]{1,0:T(8,128)(2,1)S(1)} %slice.138), channel_id=1, source_target_pairs={{0,4},{1,5},{2,6},{3,7},{4,0},{5,1},{6,2},{7,3},{8,12},{9,13},{10,... | collective-permute-start | bytes 18440 | tf_op jit(solution)/shard_map/r2_far_columns_4/ppermute | solution.py:231
  23.3 0.1 collective-permute-start.7
  23.4 1.6 %final.1 = (bf16[128,384]{1,0:T(8,128)(2,1)}, f32[128,384]{1,0:T(8,128)S(1)}) custom-call(s32[1,2]{1,0:T(1,128)S(1)} %copy-done.4, bf16[128,384]{1,0:T(8,128)(2,1)S(1)} %bitcast.20, bf16[128,384]{1,0:T(8,128)(2,1)S(1)} %bitcast.22, bf16[384,128]{1,0:T(8,128)(2,1)S(1)} %get-tuple-element.16.att_ref, bf16[384,128]{1,0:T(8,128)(2,1)S(1)} %get-tuple-element.17.dq_ref, ...), custom_call_target="tpu_custom_call" | custom-call | flops 150994944 | bytes 1769480 | tf_op jit(solution)/shard_map/final/pallas_call | solution.py:217
  25.0 1.0 %collective-permute-done.6 = bf16[8,384]{1,0:T(8,128)(2,1)S(1)} collective-permute-done((bf16[8,384]{1,0:T(8,128)(2,1)S(1)}, bf16[8,384]{1,0:T(8,128)(2,1)S(1)}, u32[]{:S(2)}, u32[]{:S(2)}) %collective-permute-start.6) | collective-permute-done | bytes 6176 | tf_op jit(solution)/shard_map/r2_far_columns_4/ppermute | solution.py:231
  25.9 0.5 %collective-permute-start.10 = (bf16[4,384]{1,0:T(4,128)(2,1)S(1)}, bf16[4,384]{1,0:T(4,128)(2,1)S(1)}, u32[]{:S(2)}, u32[]{:S(2)}) collective-permute-start(bf16[4,384]{1,0:T(4,128)(2,1)S(1)} %slice.156), channel_id=1, source_target_pairs={{0,2},{1,3},{2,0},{3,1},{4,6},{5,7},{6,4},{7,5},{8,10},{9,11},{10,... | collective-permute-start | bytes 9224 | tf_op jit(solution)/shard_map/r2_far_columns_2/ppermute | solution.py:231
  26.5 1.0 %collective-permute-done.7 = bf16[70,384]{1,0:T(8,128)(2,1)S(1)} collective-permute-done((bf16[70,384]{1,0:T(8,128)(2,1)S(1)}, bf16[70,384]{1,0:T(8,128)(2,1)S(1)}, u32[]{:S(2)}, u32[]{:S(2)}) %collective-permute-start.7) | collective-permute-done | bytes 53792 | tf_op jit(solution)/shard_map/r2_odd_rows/ppermute | solution.py:231
  27.5 0.2 collective-permute-start.8
  27.7 1.9 %collective-permute-done.10 = bf16[4,384]{1,0:T(4,128)(2,1)S(1)} collective-permute-done((bf16[4,384]{1,0:T(4,128)(2,1)S(1)}, bf16[4,384]{1,0:T(4,128)(2,1)S(1)}, u32[]{:S(2)}, u32[]{:S(2)}) %collective-permute-start.10) | collective-permute-done | bytes 3104 | tf_op jit(solution)/shard_map/r2_far_columns_2/ppermute | solution.py:231
  29.6 0.0 collective-permute-done.8
  29.9 1.0 %collective-permute-start.11 = (bf16[26,384]{1,0:T(8,128)(2,1)S(1)}, bf16[26,384]{1,0:T(8,128)(2,1)S(1)}, u32[]{:S(2)}, u32[]{:S(2)}) collective-permute-start(bf16[26,384]{1,0:T(8,128)(2,1)S(1)} %pad_maximum_fusion.8), channel_id=1, source_target_pairs={{0,1},{1,0},{2,3},{3,2},{4,5},{5,4},{6,7},{7,6},{8,9},{9,8},{10,11... | collective-permute-start | bytes 59912 | tf_op jit(solution)/shard_map/r2_low_columns/ppermute | solution.py:231
  30.9 2.9 %collective-permute-start.9 = (bf16[24,384]{1,0:T(8,128)(2,1)S(1)}, bf16[24,384]{1,0:T(8,128)(2,1)S(1)}, u32[]{:S(2)}, u32[]{:S(2)}) collective-permute-start(bf16[24,384]{1,0:T(8,128)(2,1)S(1)} %get-tuple-element.27), channel_id=1, source_target_pairs={{1,2},{2,1},{3,4},{4,3},{5,6},{6,5},{9,10},{10,9},{11,12},{12,11},... | collective-permute-start | bytes 55304 | tf_op jit(solution)/shard_map/r2_odd_columns/ppermute | solution.py:231
  33.8 0.0 collective-permute-done.11
  33.8 3.6 %collective-permute-done.9 = bf16[24,384]{1,0:T(8,128)(2,1)S(1)} collective-permute-done((bf16[24,384]{1,0:T(8,128)(2,1)S(1)}, bf16[24,384]{1,0:T(8,128)(2,1)S(1)}, u32[]{:S(2)}, u32[]{:S(2)}) %collective-permute-start.9) | collective-permute-done | bytes 18464 | tf_op jit(solution)/shard_map/r2_odd_columns/ppermute | solution.py:231
  37.5 0.7 %add_convert_fusion = bf16[8,16,384]{2,1,0:T(8,128)(2,1)} fusion(f32[8,3,384]{2,1,0:T(4,128)S(1)} %select_n.121, f32[8,3,384]{2,1,0:T(4,128)S(1)} %select_n.119, f32[3,16,384]{2,1,0:T(8,128)S(1)} %slice.176, f32[8,16,384]{2,1,0:T(8,128)S(1)} %bitcast.23, f32[3,16,384]{2,1,0:T(8,128)S(1)} %slice.175, f32[16,384]{1,0:T(8,128)S(1)} %broadcast_bitcast_fusion), kind=kLoop, calls=%fused_computation.4 | loop fusion | flops 294912 | bytes 540672 | tf_op jit(solution)/shard_map/convert_element_type | solution.py:354
  (56 shorter events, 0.7 us)
Async XLA Ops:
  0.6 4.3 %copy-start.1 = (bf16[8,16,384]{2,1,0:T(8,128)(2,1)S(1)}, bf16[8,16,384]{2,1,0:T(8,128)(2,1)}, u32[]{:S(2)}) copy-start(bf16[8,16,384]{2,1,0:T(8,128)(2,1)} %param.8) | copy-start | bytes 294916
  1.6 3.4 %copy-start.4 = (s32[1,2]{1,0:T(1,128)S(1)}, s32[1,2]{1,0:T(1,128)}, u32[]{:S(2)}) copy-start(s32[1,2]{1,0:T(1,128)} %mask_ref.3) | copy-start | bytes 28
  1.6 8.1 %collective-permute-start.1 = (bf16[24,384]{1,0:T(8,128)(2,1)S(1)}, bf16[24,384]{1,0:T(8,128)(2,1)S(1)}, u32[]{:S(2)}, u32[]{:S(2)}) collective-permute-start(bf16[24,384]{1,0:T(8,128)(2,1)S(1)} %select_n.102), channel_id=1, source_target_pairs={{1,2},{2,1},{3,4},{4,3},{5,6},{6,5},{9,10},{10,9},{11,12},{12,11},... | collective-permute-start | bytes 55304 | tf_op jit(solution)/shard_map/r1_odd_columns/ppermute | solution.py:231
  5.1 4.6 %collective-permute-start = (bf16[28,384]{1,0:T(8,128)(2,1)S(1)}, bf16[28,384]{1,0:T(8,128)(2,1)S(1)}, u32[]{:S(2)}, u32[]{:S(2)}) collective-permute-start(bf16[28,384]{1,0:T(8,128)(2,1)S(1)} %pad_maximum_fusion.7), channel_id=1, source_target_pairs={{0,1},{1,0},{2,3},{3,2},{4,5},{5,4},{6,7},{7,6},{8,9},{9,8},{10,11... | collective-permute-start | bytes 64520 | tf_op jit(solution)/shard_map/r1_low_columns/ppermute | solution.py:231
  7.6 0.7 %copy-start.5 = (s32[128]{0:T(128)S(1)}, s32[128]{0:T(128)}, u32[]{:S(2)}) copy-start(s32[128]{0:T(128)} %constant.86) | copy-start | bytes 1540
  7.6 0.7 %copy-start.6 = (s32[128]{0:T(128)S(1)}, s32[128]{0:T(128)}, u32[]{:S(2)}) copy-start(s32[128]{0:T(128)} %constant.85) | copy-start | bytes 1540
  8.5 7.2 %copy-start = (bf16[384,1152]{1,0:T(8,128)(2,1)S(1)}, bf16[384,1152]{1,0:T(8,128)(2,1)}, u32[]{:S(2)}) copy-start(bf16[384,1152]{1,0:T(8,128)(2,1)} %wqkv_ref.3) | copy-start | bytes 2654212
  9.8 5.8 %copy-start.2 = (bf16[384,384]{1,0:T(8,128)(2,1)S(1)}, bf16[384,384]{1,0:T(8,128)(2,1)}, u32[]{:S(2)}) copy-start(bf16[384,384]{1,0:T(8,128)(2,1)} %wout_ref.3) | copy-start | bytes 884740
  9.9 1.3 %collective-permute-start.2 = (bf16[70,384]{1,0:T(8,128)(2,1)S(1)}, bf16[70,384]{1,0:T(8,128)(2,1)S(1)}, u32[]{:S(2)}, u32[]{:S(2)}) collective-permute-start(bf16[70,384]{1,0:T(8,128)(2,1)S(1)} %pad_maximum_fusion.4), channel_id=1, source_target_pairs={{0,8},{8,0},{16,24},{24,16},{1,9},{9,1},{17,25},{25,17},{2,10},{10... | collective-permute-start | bytes 161288 | tf_op jit(solution)/shard_map/r1_low_rows/ppermute | solution.py:231
  10.0 3.7 %collective-permute-start.4 = (bf16[8,384]{1,0:T(8,128)(2,1)S(1)}, bf16[8,384]{1,0:T(8,128)(2,1)S(1)}, u32[]{:S(2)}, u32[]{:S(2)}) collective-permute-start(bf16[8,384]{1,0:T(8,128)(2,1)S(1)} %pad_maximum_fusion.10), channel_id=1, source_target_pairs={{0,2},{1,3},{2,0},{3,1},{4,6},{5,7},{6,4},{7,5},{8,10},{9,11},{10,... | collective-permute-start | bytes 18440 | tf_op jit(solution)/shard_map/r1_far_columns_2/ppermute | solution.py:231
  10.5 5.1 %copy-start.3 = (bf16[8,16,384]{2,1,0:T(8,128)(2,1)S(1)}, bf16[8,16,384]{2,1,0:T(8,128)(2,1)}, u32[]{:S(2)}) copy-start(bf16[8,16,384]{2,1,0:T(8,128)(2,1)} %param.12) | copy-start | bytes 294916
  11.2 5.4 %collective-permute-start.3 = (bf16[74,384]{1,0:T(8,128)(2,1)S(1)}, bf16[74,384]{1,0:T(8,128)(2,1)S(1)}, u32[]{:S(2)}, u32[]{:S(2)}) collective-permute-start(bf16[74,384]{1,0:T(8,128)(2,1)S(1)} %pad_maximum_fusion), channel_id=1, source_target_pairs={{0,24},{8,16},{16,8},{24,0},{1,25},{9,17},{17,9},{25,1},{2,26},{10... | collective-permute-start | bytes 170504 | tf_op jit(solution)/shard_map/r1_odd_rows/ppermute | solution.py:231
  13.7 4.7 %collective-permute-start.5 = (bf16[16,384]{1,0:T(8,128)(2,1)S(1)}, bf16[16,384]{1,0:T(8,128)(2,1)S(1)}, u32[]{:S(2)}, u32[]{:S(2)}) collective-permute-start(bf16[16,384]{1,0:T(8,128)(2,1)S(1)} %pad_maximum_fusion.9), channel_id=1, source_target_pairs={{0,4},{1,5},{2,6},{3,7},{4,0},{5,1},{6,2},{7,3},{8,12},{9,13},{10,... | collective-permute-start | bytes 36872 | tf_op jit(solution)/shard_map/r1_far_columns_4/ppermute | solution.py:231
  21.3 4.6 %collective-permute-start.6 = (bf16[8,384]{1,0:T(8,128)(2,1)S(1)}, bf16[8,384]{1,0:T(8,128)(2,1)S(1)}, u32[]{:S(2)}, u32[]{:S(2)}) collective-permute-start(bf16[8,384]{1,0:T(8,128)(2,1)S(1)} %slice.138), channel_id=1, source_target_pairs={{0,4},{1,5},{2,6},{3,7},{4,0},{5,1},{6,2},{7,3},{8,12},{9,13},{10,... | collective-permute-start | bytes 18440 | tf_op jit(solution)/shard_map/r2_far_columns_4/ppermute | solution.py:231
  23.3 4.2 %collective-permute-start.7 = (bf16[70,384]{1,0:T(8,128)(2,1)S(1)}, bf16[70,384]{1,0:T(8,128)(2,1)S(1)}, u32[]{:S(2)}, u32[]{:S(2)}) collective-permute-start(bf16[70,384]{1,0:T(8,128)(2,1)S(1)} %pad_maximum_fusion.5), channel_id=1, source_target_pairs={{0,24},{8,16},{16,8},{24,0},{1,25},{9,17},{17,9},{25,1},{2,26},{10... | collective-permute-start | bytes 161288 | tf_op jit(solution)/shard_map/r2_odd_rows/ppermute | solution.py:231
  25.9 3.7 %collective-permute-start.10 = (bf16[4,384]{1,0:T(4,128)(2,1)S(1)}, bf16[4,384]{1,0:T(4,128)(2,1)S(1)}, u32[]{:S(2)}, u32[]{:S(2)}) collective-permute-start(bf16[4,384]{1,0:T(4,128)(2,1)S(1)} %slice.156), channel_id=1, source_target_pairs={{0,2},{1,3},{2,0},{3,1},{4,6},{5,7},{6,4},{7,5},{8,10},{9,11},{10,... | collective-permute-start | bytes 9224 | tf_op jit(solution)/shard_map/r2_far_columns_2/ppermute | solution.py:231
  27.5 2.1 %collective-permute-start.8 = (bf16[68,384]{1,0:T(8,128)(2,1)S(1)}, bf16[68,384]{1,0:T(8,128)(2,1)S(1)}, u32[]{:S(2)}, u32[]{:S(2)}) collective-permute-start(bf16[68,384]{1,0:T(8,128)(2,1)S(1)} %pad_maximum_fusion.6), channel_id=1, source_target_pairs={{0,8},{8,0},{16,24},{24,16},{1,9},{9,1},{17,25},{25,17},{2,10},{10... | collective-permute-start | bytes 156680 | tf_op jit(solution)/shard_map/r2_low_rows/ppermute | solution.py:231
  29.9 3.9 %collective-permute-start.11 = (bf16[26,384]{1,0:T(8,128)(2,1)S(1)}, bf16[26,384]{1,0:T(8,128)(2,1)S(1)}, u32[]{:S(2)}, u32[]{:S(2)}) collective-permute-start(bf16[26,384]{1,0:T(8,128)(2,1)S(1)} %pad_maximum_fusion.8), channel_id=1, source_target_pairs={{0,1},{1,0},{2,3},{3,2},{4,5},{5,4},{6,7},{7,6},{8,9},{9,8},{10,11... | collective-permute-start | bytes 59912 | tf_op jit(solution)/shard_map/r2_low_columns/ppermute | solution.py:231
  30.9 6.6 %collective-permute-start.9 = (bf16[24,384]{1,0:T(8,128)(2,1)S(1)}, bf16[24,384]{1,0:T(8,128)(2,1)S(1)}, u32[]{:S(2)}, u32[]{:S(2)}) collective-permute-start(bf16[24,384]{1,0:T(8,128)(2,1)S(1)} %get-tuple-element.27), channel_id=1, source_target_pairs={{1,2},{2,1},{3,4},{4,3},{5,6},{6,5},{9,10},{10,9},{11,12},{12,11},... | collective-permute-start | bytes 55304 | tf_op jit(solution)/shard_map/r2_odd_columns/ppermute | solution.py:231

commit v4 on v3

--- a/solution.py
+++ b/solution.py
@@ -244,8 +244,10 @@
 
     first = tokens[:, :REACH].reshape(side, width)
     last = tokens[:, tile_cols - REACH :].reshape(side, width)
-    odd_x = swap("r1_odd_columns", jnp.where(even_x, first, last), "gx", pairs_odd(count_x, False))
-    grouped = tokens.astype(full).reshape(
+    odd_send = jnp.where(even_x, first, last)
+    odd_x = swap("r1_odd_columns", odd_send, "gx", pairs_odd(count_x, False))
+    tokens_later, _ = lax.optimization_barrier((tokens, odd_send))
+    grouped = tokens_later.astype(full).reshape(
         tile_rows // TISSUE_BLOCK, TISSUE_BLOCK, tile_cols // TISSUE_BLOCK, TISSUE_BLOCK, width
     )
     sums = (jnp.sum(grouped, axis=(1, 3)) / TISSUE_BLOCK).reshape(blocks, width).astype(half)
@@ -287,11 +289,6 @@
         [((rows.total - own, width), half), ((rows.total, 2 * width), half), ((rows.total, 2 * width), half)],
         40 * macs, 0, low_x, odd_x, low_y, odd_y, pool_tokens, flags, bias, query, kv, d_att, w_qkv[:, width:],
     )
-    mixed, own_back = call(
-        functools.partial(final_kernel, rows), "final", [((own, width), half), ((own, width), full)],
-        [], 8 * macs, 1, block_mask, flat_tokens, grad_flat, att, d_query, d_kv, w_qkv, w_out,
-    )
-
     def piece(start, count):
         return back[start - own : start - own + count]
 
@@ -300,12 +297,6 @@
 
     row_grad = piece(rows.pool, count_x * blocks)
     col_grad = piece(rows.pool + count_x * blocks, count_y * blocks)
-    for step in reversed(steps_above(count_x, 2)):
-        if step == 2:
-            row_grad, own_back = lax.optimization_barrier((row_grad, own_back))
-        middle = row_grad.shape[0] // 2
-        got = swap(f"r2_far_columns_{step}", row_grad[middle:], "gx", pairs_far(count_x, step))
-        row_grad = fold(row_grad[:middle], got)
     for step in reversed(steps_above(count_y // 2, 2)):
         middle = col_grad.shape[0] // 2
         got = swap(f"r2_far_rows_{step}", col_grad[middle:], "gy", window_pairs(count_y, step))
@@ -320,6 +311,17 @@
     low_rows = swap(
         "r2_low_rows", jnp.concatenate([piece(rows.low_y, edge), col_grad[blocks:]], axis=0), "gy", pairs_low(count_y)
     )
+    for step in reversed(steps_above(count_x, 2)):
+        if step == 2:
+            row_grad, low_rows = lax.optimization_barrier((row_grad, low_rows))
+        middle = row_grad.shape[0] // 2
+        got = swap(f"r2_far_columns_{step}", row_grad[middle:], "gx", pairs_far(count_x, step))
+        row_grad = fold(row_grad[:middle], got)
+    att, row_grad = lax.optimization_barrier((att, row_grad))
+    mixed, own_back = call(
+        functools.partial(final_kernel, rows), "final", [((own, width), half), ((own, width), full)],
+        [], 8 * macs, 1, block_mask, flat_tokens, grad_flat, att, d_query, d_kv, w_qkv, w_out,
+    )
     col_grad = fold(col_grad[:blocks], low_rows[edge:])
     odd_rows = odd_rows[:edge].astype(full).reshape(REACH, wide, width)
     low_rows = low_rows[:edge].astype(full).reshape(REACH, wide, width)
@@ -333,22 +335,27 @@
     odd_side = piece(rows.odd_x, side).astype(full) + lines(wide - REACH, wide).reshape(side, width)
     odd_got = swap("r2_odd_columns", odd_side.astype(half), "gx", pairs_odd(count_x, False))
     low_side = piece(rows.low_x, side).astype(full) + lines(0, REACH).reshape(side, width)
+    room = tile_cols - REACH
+    d_tokens = own_back.reshape(tile_rows, tile_cols, width) + jnp.pad(
+        at_top[:, REACH : REACH + tile_cols], ((0, tile_rows - REACH), (0, 0), (0, 0))
+    )
+    d_tokens = d_tokens + jnp.pad(at_bottom[:, REACH : REACH + tile_cols], ((tile_rows - REACH, 0), (0, 0), (0, 0)))
+
+    def columns(got, at_first):
+        got = got.astype(full).reshape(tile_rows, REACH, width)
+        first, last = jnp.pad(got, ((0, 0), (0, room), (0, 0))), jnp.pad(got, ((0, 0), (room, 0), (0, 0)))
+        return jnp.where(at_first, first, last)
+
+    d_tokens = d_tokens + columns(odd_got, even_x)
     low_got = swap(
         "r2_low_columns",
         jnp.concatenate([low_side.astype(half), row_grad[blocks:]], axis=0),
         "gx",
         pairs_low(count_x),
     )
+    low_got, d_tokens = lax.optimization_barrier((low_got, d_tokens))
     block_grad = row_grad[:blocks].astype(full) + low_got[side:].astype(full) + col_grad.astype(full)
-    odd_got = odd_got.astype(full).reshape(tile_rows, REACH, width)
-    low_got = low_got[:side].astype(full).reshape(tile_rows, REACH, width)
-    at_first, at_last = jnp.where(even_x, odd_got, low_got), jnp.where(even_x, low_got, odd_got)
-    room = tile_cols - REACH
-    d_tokens = own_back.reshape(tile_rows, tile_cols, width) + jnp.pad(
-        at_top[:, REACH : REACH + tile_cols], ((0, tile_rows - REACH), (0, 0), (0, 0))
-    )
-    d_tokens = d_tokens + jnp.pad(at_bottom[:, REACH : REACH + tile_cols], ((tile_rows - REACH, 0), (0, 0), (0, 0)))
-    d_tokens = d_tokens + jnp.pad(at_first, ((0, 0), (0, room), (0, 0))) + jnp.pad(at_last, ((0, 0), (room, 0), (0, 0)))
+    d_tokens = d_tokens + columns(low_got[:side], ~even_x)
     shaped = (block_grad / TISSUE_BLOCK).reshape(tile_rows // TISSUE_BLOCK, tile_cols // TISSUE_BLOCK, width)
     d_tokens = d_tokens + jnp.repeat(jnp.repeat(shaped, TISSUE_BLOCK, 0), TISSUE_BLOCK, 1)
     return mixed.reshape(tile_rows, tile_cols, width), d_tokens.astype(half)

time: 38.4 us -> 37.7 us (0.982)
  the two profiles are of different devices: /device:TPU:8 before, /device:TPU:0 now
where the time goes in v4:
time: 37.7 us; the launch traced here: 37.5 us
  starting transfers between devices  19.4 us (51%)
  waiting for transfers between devices  5.81 us (15%)
  Pallas kernels  5.25 us (14%)
  local copies, waits for them, and re-layouts  3.78 us (10%)
  other arithmetic  2.16 us (6%)
  between operations  1.11 us (3%)
    ppermute x12, starting transfers between devices, swap(): return lax.ppermute(value, axis, moves)  19.4 us
    ppermute x12, waiting for transfers between devices, swap(): return lax.ppermute(value, axis, moves)  5.81 us
    pallas_call x3, Pallas kernels, call(): pl.pallas_call(kernel, out_shape=tuple((jax.ShapeDtypeStruct(shape, dtype...  5.25 us
    unnamed x15, local copies, waits for them, and re-layouts  1.32 us
    slice x1, local copies, waits for them, and re-layouts, local(): w_qkv[:, width:]  1.18 us
    select_n x1, other arithmetic, local(): jnp.where(even_x, last, first)  0.89 us
  transfers between devices with their start and end apart: 12, of which 7 were waited for; matrix products, arithmetic and copies ran while one was open for 7% of the time, Pallas kernels for 7%

profile of v4, /device:TPU:0, one launch (start us, length us, event | category | flops | bytes accessed | tf_op | source)
XLA Modules:
  0.0 37.5 jit_solution(17961402216395886272)
XLA Ops:
  0.6 0.0 copy-start.1
  0.7 0.9 %broadcast_select_fusion.3 = (bf16[8,3,384]{2,1,0:T(4,128)(2,1)S(1)}, bf16[8,3,384]{2,1,0:T(4,128)(2,1)S(1)}) fusion(pred[]{:T(512)S(6)} %eq.11, bf16[8,16,384]{2,1,0:T(8,128)(2,1)} %param.8), kind=kLoop, calls=%fused_computation.29 | loop fusion | flops 18432 | bytes 73729 | tf_op jit(solution)/shard_map/jit(_where)/select_n | solution.py:257
  1.6 0.7 %collective-permute-start.1 = (bf16[24,384]{1,0:T(8,128)(2,1)S(1)}, bf16[24,384]{1,0:T(8,128)(2,1)S(1)}, u32[]{:S(2)}, u32[]{:S(2)}) collective-permute-start(bf16[24,384]{1,0:T(8,128)(2,1)S(1)} %select_n.98), channel_id=1, source_target_pairs={{1,2},{2,1},{3,4},{4,3},{5,6},{6,5},{9,10},{10,9},{11,12},{12,11},... | collective-permute-start | bytes 55304 | tf_op jit(solution)/shard_map/r1_odd_columns/ppermute | solution.py:231
  2.2 0.0 copy-done.1
  2.3 0.0 copy-start.4
  2.4 0.6 %copy-done.4 = s32[1,2]{1,0:T(1,128)S(1)} copy-done((s32[1,2]{1,0:T(1,128)S(1)}, s32[1,2]{1,0:T(1,128)}, u32[]{:S(2)}) %copy-start.4) | copy-done | bytes 32
  3.0 0.1 broadcast_in_dim.21
  3.1 5.8 %collective-permute-start = (bf16[28,384]{1,0:T(8,128)(2,1)S(1)}, bf16[28,384]{1,0:T(8,128)(2,1)S(1)}, u32[]{:S(2)}, u32[]{:S(2)}) collective-permute-start(bf16[28,384]{1,0:T(8,128)(2,1)S(1)} %pad_maximum_fusion.7), channel_id=1, source_target_pairs={{0,1},{1,0},{2,3},{3,2},{4,5},{5,4},{6,7},{7,6},{8,9},{9,8},{10,11... | collective-permute-start | bytes 64520 | tf_op jit(solution)/shard_map/r1_low_columns/ppermute | solution.py:231
  8.9 0.7 %dynamic-slice_bitcast_fusion = s32[384,2]{0,1:T(2,128)S(1)} fusion(s32[2,2,384,2]{2,3,1,0:T(2,128)} %constant.59.clone, s32[]{:T(128)S(6)} %select_n.105, s32[]{:T(128)S(6)} %select_n.106), kind=kLoop, calls=%fused_computation.42 | loop fusion | bytes 6152 | tf_op jit(solution)/shard_map/squeeze | solution.py:102
  9.6 0.0 copy-start.6
  9.6 0.6 %copy-done.5 = s32[128]{0:T(128)S(1)} copy-done((s32[128]{0:T(128)S(1)}, s32[128]{0:T(128)}, u32[]{:S(2)}) %copy-start.5) | copy-done | bytes 536
  10.3 0.0 copy-done.6
  10.3 0.2 fusion.4.bias_ref
  10.5 0.0 copy-start
  10.5 1.2 %slice.136.wkv_ref = bf16[384,768]{1,0:T(8,128)(2,1)S(1)} slice(bf16[384,1152]{1,0:T(8,128)(2,1)} %wqkv_ref.3), slice={[0:384], [384:1152]} | slice | bytes 1179648 | tf_op jit(solution)/shard_map/slice | solution.py:290
  11.7 0.0 collective-permute-done.1.odd_x_ref
  11.7 0.0 collective-permute-done.low_x_ref
  11.8 0.1 broadcast_select_fusion
  11.8 0.0 copy-start.2
  11.9 0.1 collective-permute-start.2
  12.0 0.0 copy-start.3
  12.1 1.6 %collective-permute-start.4 = (bf16[8,384]{1,0:T(8,128)(2,1)S(1)}, bf16[8,384]{1,0:T(8,128)(2,1)S(1)}, u32[]{:S(2)}, u32[]{:S(2)}) collective-permute-start(bf16[8,384]{1,0:T(8,128)(2,1)S(1)} %pad_maximum_fusion.10), channel_id=1, source_target_pairs={{0,2},{1,3},{2,0},{3,1},{4,6},{5,7},{6,4},{7,5},{8,10},{9,11},{10,... | collective-permute-start | bytes 18440 | tf_op jit(solution)/shard_map/r1_far_columns_2/ppermute | solution.py:231
  13.7 0.0 collective-permute-done.2.low_y_ref
  13.7 1.4 %collective-permute-start.3 = (bf16[74,384]{1,0:T(8,128)(2,1)S(1)}, bf16[74,384]{1,0:T(8,128)(2,1)S(1)}, u32[]{:S(2)}, u32[]{:S(2)}) collective-permute-start(bf16[74,384]{1,0:T(8,128)(2,1)S(1)} %pad_maximum_fusion), channel_id=1, source_target_pairs={{0,24},{8,16},{16,8},{24,0},{1,25},{9,17},{17,9},{25,1},{2,26},{10... | collective-permute-start | bytes 170504 | tf_op jit(solution)/shard_map/r1_odd_rows/ppermute | solution.py:231
  15.1 0.6 %collective-permute-done.4 = bf16[8,384]{1,0:T(8,128)(2,1)S(1)} collective-permute-done((bf16[8,384]{1,0:T(8,128)(2,1)S(1)}, bf16[8,384]{1,0:T(8,128)(2,1)S(1)}, u32[]{:S(2)}, u32[]{:S(2)}) %collective-permute-start.4) | collective-permute-done | bytes 6176 | tf_op jit(solution)/shard_map/r1_far_columns_2/ppermute | solution.py:231
  15.8 2.7 %collective-permute-start.5 = (bf16[16,384]{1,0:T(8,128)(2,1)S(1)}, bf16[16,384]{1,0:T(8,128)(2,1)S(1)}, u32[]{:S(2)}, u32[]{:S(2)}) collective-permute-start(bf16[16,384]{1,0:T(8,128)(2,1)S(1)} %pad_maximum_fusion.9), channel_id=1, source_target_pairs={{0,4},{1,5},{2,6},{3,7},{4,0},{5,1},{6,2},{7,3},{8,12},{9,13},{10,... | collective-permute-start | bytes 36872 | tf_op jit(solution)/shard_map/r1_far_columns_4/ppermute | solution.py:231
  18.4 0.0 copy-done
  18.4 0.0 copy-done.2
  18.4 0.0 copy-done.3
  18.4 0.9 %own.1 = (bf16[128,384]{1,0:T(8,128)(2,1)S(1)}, bf16[128,768]{1,0:T(8,128)(2,1)S(1)}, bf16[128,384]{1,0:T(8,128)(2,1)S(1)}) custom-call(s32[1,2]{1,0:T(1,128)S(1)} %copy-done.4, bf16[128,384]{1,0:T(8,128)(2,1)S(1)} %bitcast.19, bf16[128,384]{1,0:T(8,128)(2,1)S(1)} %bitcast.21, bf16[384,1152]{1,0:T(8,128)(2,1)S(1)} %copy-done, bf16[384,384]{1,0:T(8,128)(2,1)S(1)} %copy-done.2), custom_call_target="tpu_custom_call" | custom-call | flops 150994944 | bytes 1376264 | tf_op jit(solution)/shard_map/own/pallas_call | solution.py:217
  19.4 0.0 collective-permute-done.3.odd_y_ref
  19.4 1.0 %collective-permute-done.5 = bf16[16,384]{1,0:T(8,128)(2,1)S(1)} collective-permute-done((bf16[16,384]{1,0:T(8,128)(2,1)S(1)}, bf16[16,384]{1,0:T(8,128)(2,1)S(1)}, u32[]{:S(2)}, u32[]{:S(2)}) %collective-permute-start.5) | collective-permute-done | bytes 12320 | tf_op jit(solution)/shard_map/r1_far_columns_4/ppermute | solution.py:231
  20.4 0.1 concatenate.43
  20.6 2.7 %attention.1 = (bf16[256,384]{1,0:T(8,128)(2,1)S(1)}, bf16[128,768]{1,0:T(8,128)(2,1)S(1)}, bf16[384,128]{1,0:T(8,128)(2,1)S(1)}, bf16[384,128]{1,0:T(8,128)(2,1)S(1)}) custom-call(bf16[28,384]{1,0:T(8,128)(2,1)S(1)} %collective-permute-done.low_x_ref, bf16[24,384]{1,0:T(8,128)(2,1)S(1)} %collective-permute-done.1.odd_x_ref, ...), custom_call_target="tpu_custom_call" | custom-call | flops 754974720 | bytes 1371136 | tf_op jit(solution)/shard_map/attention/pallas_call | solution.py:217
  23.4 0.1 collective-permute-start.7
  23.5 2.7 %collective-permute-start.6 = (bf16[8,384]{1,0:T(8,128)(2,1)S(1)}, bf16[8,384]{1,0:T(8,128)(2,1)S(1)}, u32[]{:S(2)}, u32[]{:S(2)}) collective-permute-start(bf16[8,384]{1,0:T(8,128)(2,1)S(1)} %slice.138), channel_id=1, source_target_pairs={{0,4},{1,5},{2,6},{3,7},{4,0},{5,1},{6,2},{7,3},{8,12},{9,13},{10,... | collective-permute-start | bytes 18440 | tf_op jit(solution)/shard_map/r2_far_columns_4/ppermute | solution.py:231
  26.2 1.4 %collective-permute-done.7 = bf16[70,384]{1,0:T(8,128)(2,1)S(1)} collective-permute-done((bf16[70,384]{1,0:T(8,128)(2,1)S(1)}, bf16[70,384]{1,0:T(8,128)(2,1)S(1)}, u32[]{:S(2)}, u32[]{:S(2)}) %collective-permute-start.7) | collective-permute-done | bytes 53792 | tf_op jit(solution)/shard_map/r2_odd_rows/ppermute | solution.py:231
  27.7 0.2 collective-permute-start.8
  27.9 0.2 collective-permute-done.6
  28.1 0.8 %collective-permute-done.8 = bf16[68,384]{1,0:T(8,128)(2,1)S(1)} collective-permute-done((bf16[68,384]{1,0:T(8,128)(2,1)S(1)}, bf16[68,384]{1,0:T(8,128)(2,1)S(1)}, u32[]{:S(2)}, u32[]{:S(2)}) %collective-permute-start.8) | collective-permute-done | bytes 52256 | tf_op jit(solution)/shard_map/r2_low_rows/ppermute | solution.py:231
  29.2 1.6 %collective-permute-start.9 = (bf16[4,384]{1,0:T(4,128)(2,1)S(1)}, bf16[4,384]{1,0:T(4,128)(2,1)S(1)}, u32[]{:S(2)}, u32[]{:S(2)}) collective-permute-start(bf16[4,384]{1,0:T(4,128)(2,1)S(1)} %slice.146), channel_id=1, source_target_pairs={{0,2},{1,3},{2,0},{3,1},{4,6},{5,7},{6,4},{7,5},{8,10},{9,11},{10,... | collective-permute-start | bytes 9224 | tf_op jit(solution)/shard_map/r2_far_columns_2/ppermute | solution.py:231
  30.9 0.7 %collective-permute-start.11 = (bf16[24,384]{1,0:T(8,128)(2,1)S(1)}, bf16[24,384]{1,0:T(8,128)(2,1)S(1)}, u32[]{:S(2)}, u32[]{:S(2)}) collective-permute-start(bf16[24,384]{1,0:T(8,128)(2,1)S(1)} %get-tuple-element.36), channel_id=1, source_target_pairs={{1,2},{2,1},{3,4},{4,3},{5,6},{6,5},{9,10},{10,9},{11,12},{12,11},... | collective-permute-start | bytes 55304 | tf_op jit(solution)/shard_map/r2_odd_columns/ppermute | solution.py:231
  31.5 1.3 %collective-permute-done.9 = bf16[4,384]{1,0:T(4,128)(2,1)S(1)} collective-permute-done((bf16[4,384]{1,0:T(4,128)(2,1)S(1)}, bf16[4,384]{1,0:T(4,128)(2,1)S(1)}, u32[]{:S(2)}, u32[]{:S(2)}) %collective-permute-start.9) | collective-permute-done | bytes 3104 | tf_op jit(solution)/shard_map/r2_far_columns_2/ppermute | solution.py:231
  32.9 1.9 %collective-permute-start.10 = (bf16[26,384]{1,0:T(8,128)(2,1)S(1)}, bf16[26,384]{1,0:T(8,128)(2,1)S(1)}, u32[]{:S(2)}, u32[]{:S(2)}) collective-permute-start(bf16[26,384]{1,0:T(8,128)(2,1)S(1)} %pad_maximum_fusion.8), channel_id=1, source_target_pairs={{0,1},{1,0},{2,3},{3,2},{4,5},{5,4},{6,7},{7,6},{8,9},{9,8},{10,11... | collective-permute-start | bytes 59912 | tf_op jit(solution)/shard_map/r2_low_columns/ppermute | solution.py:231
  34.8 1.6 %final.1 = (bf16[128,384]{1,0:T(8,128)(2,1)}, f32[128,384]{1,0:T(8,128)S(1)}) custom-call(s32[1,2]{1,0:T(1,128)S(1)} %copy-done.4, bf16[128,384]{1,0:T(8,128)(2,1)S(1)} %bitcast.20, bf16[128,384]{1,0:T(8,128)(2,1)S(1)} %bitcast.22, bf16[384,128]{1,0:T(8,128)(2,1)S(1)} %get-tuple-element.25.att_ref, bf16[384,128]{1,0:T(8,128)(2,1)S(1)} %get-tuple-element.26.dq_ref, ...), custom_call_target="tpu_custom_call" | custom-call | flops 150994944 | bytes 1769480 | tf_op jit(solution)/shard_map/final/pallas_call | solution.py:217
  36.4 0.0 collective-permute-done.11
  36.4 0.3 collective-permute-done.10
  36.8 0.7 %add_convert_fusion = bf16[8,16,384]{2,1,0:T(8,128)(2,1)} fusion(f32[8,16,384]{2,1,0:T(8,128)S(1)} %select_add_fusion, f32[8,3,384]{2,1,0:T(4,128)S(1)} %reshape.92, f32[16,384]{1,0:T(8,128)S(1)} %broadcast_bitcast_fusion, pred[]{:T(512)S(6)} %not.3), kind=kLoop, calls=%fused_computation.4 | loop fusion | flops 196608 | bytes 356353 | tf_op jit(solution)/shard_map/convert_element_type | solution.py:361
  (57 shorter events, 0.8 us)
Async XLA Ops:
  0.6 1.6 %copy-start.1 = (bf16[8,16,384]{2,1,0:T(8,128)(2,1)S(1)}, bf16[8,16,384]{2,1,0:T(8,128)(2,1)}, u32[]{:S(2)}) copy-start(bf16[8,16,384]{2,1,0:T(8,128)(2,1)} %param.8) | copy-start | bytes 294916
  1.6 10.1 %collective-permute-start.1 = (bf16[24,384]{1,0:T(8,128)(2,1)S(1)}, bf16[24,384]{1,0:T(8,128)(2,1)S(1)}, u32[]{:S(2)}, u32[]{:S(2)}) collective-permute-start(bf16[24,384]{1,0:T(8,128)(2,1)S(1)} %select_n.98), channel_id=1, source_target_pairs={{1,2},{2,1},{3,4},{4,3},{5,6},{6,5},{9,10},{10,9},{11,12},{12,11},... | collective-permute-start | bytes 55304 | tf_op jit(solution)/shard_map/r1_odd_columns/ppermute | solution.py:231
  2.3 0.7 %copy-start.4 = (s32[1,2]{1,0:T(1,128)S(1)}, s32[1,2]{1,0:T(1,128)}, u32[]{:S(2)}) copy-start(s32[1,2]{1,0:T(1,128)} %mask_ref.3) | copy-start | bytes 28
  3.1 8.7 %collective-permute-start = (bf16[28,384]{1,0:T(8,128)(2,1)S(1)}, bf16[28,384]{1,0:T(8,128)(2,1)S(1)}, u32[]{:S(2)}, u32[]{:S(2)}) collective-permute-start(bf16[28,384]{1,0:T(8,128)(2,1)S(1)} %pad_maximum_fusion.7), channel_id=1, source_target_pairs={{0,1},{1,0},{2,3},{3,2},{4,5},{5,4},{6,7},{7,6},{8,9},{9,8},{10,11... | collective-permute-start | bytes 64520 | tf_op jit(solution)/shard_map/r1_low_columns/ppermute | solution.py:231
  9.6 0.7 %copy-start.5 = (s32[128]{0:T(128)S(1)}, s32[128]{0:T(128)}, u32[]{:S(2)}) copy-start(s32[128]{0:T(128)} %constant.89) | copy-start | bytes 1540
  9.6 0.7 %copy-start.6 = (s32[128]{0:T(128)S(1)}, s32[128]{0:T(128)}, u32[]{:S(2)}) copy-start(s32[128]{0:T(128)} %constant.90) | copy-start | bytes 1540
  10.5 7.9 %copy-start = (bf16[384,1152]{1,0:T(8,128)(2,1)S(1)}, bf16[384,1152]{1,0:T(8,128)(2,1)}, u32[]{:S(2)}) copy-start(bf16[384,1152]{1,0:T(8,128)(2,1)} %wqkv_ref.3) | copy-start | bytes 2654212
  11.8 6.6 %copy-start.2 = (bf16[384,384]{1,0:T(8,128)(2,1)S(1)}, bf16[384,384]{1,0:T(8,128)(2,1)}, u32[]{:S(2)}) copy-start(bf16[384,384]{1,0:T(8,128)(2,1)} %wout_ref.3) | copy-start | bytes 884740
  11.9 1.8 %collective-permute-start.2 = (bf16[70,384]{1,0:T(8,128)(2,1)S(1)}, bf16[70,384]{1,0:T(8,128)(2,1)S(1)}, u32[]{:S(2)}, u32[]{:S(2)}) collective-permute-start(bf16[70,384]{1,0:T(8,128)(2,1)S(1)} %pad_maximum_fusion.4), channel_id=1, source_target_pairs={{0,8},{8,0},{16,24},{24,16},{1,9},{9,1},{17,25},{25,17},{2,10},{10... | collective-permute-start | bytes 161288 | tf_op jit(solution)/shard_map/r1_low_rows/ppermute | solution.py:231
  12.0 6.4 %copy-start.3 = (bf16[8,16,384]{2,1,0:T(8,128)(2,1)S(1)}, bf16[8,16,384]{2,1,0:T(8,128)(2,1)}, u32[]{:S(2)}) copy-start(bf16[8,16,384]{2,1,0:T(8,128)(2,1)} %param.12) | copy-start | bytes 294916
  12.1 3.7 %collective-permute-start.4 = (bf16[8,384]{1,0:T(8,128)(2,1)S(1)}, bf16[8,384]{1,0:T(8,128)(2,1)S(1)}, u32[]{:S(2)}, u32[]{:S(2)}) collective-permute-start(bf16[8,384]{1,0:T(8,128)(2,1)S(1)} %pad_maximum_fusion.10), channel_id=1, source_target_pairs={{0,2},{1,3},{2,0},{3,1},{4,6},{5,7},{6,4},{7,5},{8,10},{9,11},{10,... | collective-permute-start | bytes 18440 | tf_op jit(solution)/shard_map/r1_far_columns_2/ppermute | solution.py:231
  13.7 5.6 %collective-permute-start.3 = (bf16[74,384]{1,0:T(8,128)(2,1)S(1)}, bf16[74,384]{1,0:T(8,128)(2,1)S(1)}, u32[]{:S(2)}, u32[]{:S(2)}) collective-permute-start(bf16[74,384]{1,0:T(8,128)(2,1)S(1)} %pad_maximum_fusion), channel_id=1, source_target_pairs={{0,24},{8,16},{16,8},{24,0},{1,25},{9,17},{17,9},{25,1},{2,26},{10... | collective-permute-start | bytes 170504 | tf_op jit(solution)/shard_map/r1_odd_rows/ppermute | solution.py:231
  15.8 4.7 %collective-permute-start.5 = (bf16[16,384]{1,0:T(8,128)(2,1)S(1)}, bf16[16,384]{1,0:T(8,128)(2,1)S(1)}, u32[]{:S(2)}, u32[]{:S(2)}) collective-permute-start(bf16[16,384]{1,0:T(8,128)(2,1)S(1)} %pad_maximum_fusion.9), channel_id=1, source_target_pairs={{0,4},{1,5},{2,6},{3,7},{4,0},{5,1},{6,2},{7,3},{8,12},{9,13},{10,... | collective-permute-start | bytes 36872 | tf_op jit(solution)/shard_map/r1_far_columns_4/ppermute | solution.py:231
  23.4 4.2 %collective-permute-start.7 = (bf16[70,384]{1,0:T(8,128)(2,1)S(1)}, bf16[70,384]{1,0:T(8,128)(2,1)S(1)}, u32[]{:S(2)}, u32[]{:S(2)}) collective-permute-start(bf16[70,384]{1,0:T(8,128)(2,1)S(1)} %pad_maximum_fusion.5), channel_id=1, source_target_pairs={{0,24},{8,16},{16,8},{24,0},{1,25},{9,17},{17,9},{25,1},{2,26},{10... | collective-permute-start | bytes 161288 | tf_op jit(solution)/shard_map/r2_odd_rows/ppermute | solution.py:231
  23.5 4.6 %collective-permute-start.6 = (bf16[8,384]{1,0:T(8,128)(2,1)S(1)}, bf16[8,384]{1,0:T(8,128)(2,1)S(1)}, u32[]{:S(2)}, u32[]{:S(2)}) collective-permute-start(bf16[8,384]{1,0:T(8,128)(2,1)S(1)} %slice.138), channel_id=1, source_target_pairs={{0,4},{1,5},{2,6},{3,7},{4,0},{5,1},{6,2},{7,3},{8,12},{9,13},{10,... | collective-permute-start | bytes 18440 | tf_op jit(solution)/shard_map/r2_far_columns_4/ppermute | solution.py:231
  27.7 1.3 %collective-permute-start.8 = (bf16[68,384]{1,0:T(8,128)(2,1)S(1)}, bf16[68,384]{1,0:T(8,128)(2,1)S(1)}, u32[]{:S(2)}, u32[]{:S(2)}) collective-permute-start(bf16[68,384]{1,0:T(8,128)(2,1)S(1)} %pad_maximum_fusion.6), channel_id=1, source_target_pairs={{0,8},{8,0},{16,24},{24,16},{1,9},{9,1},{17,25},{25,17},{2,10},{10... | collective-permute-start | bytes 156680 | tf_op jit(solution)/shard_map/r2_low_rows/ppermute | solution.py:231
  29.2 3.7 %collective-permute-start.9 = (bf16[4,384]{1,0:T(4,128)(2,1)S(1)}, bf16[4,384]{1,0:T(4,128)(2,1)S(1)}, u32[]{:S(2)}, u32[]{:S(2)}) collective-permute-start(bf16[4,384]{1,0:T(4,128)(2,1)S(1)} %slice.146), channel_id=1, source_target_pairs={{0,2},{1,3},{2,0},{3,1},{4,6},{5,7},{6,4},{7,5},{8,10},{9,11},{10,... | collective-permute-start | bytes 9224 | tf_op jit(solution)/shard_map/r2_far_columns_2/ppermute | solution.py:231
  30.9 5.5 %collective-permute-start.11 = (bf16[24,384]{1,0:T(8,128)(2,1)S(1)}, bf16[24,384]{1,0:T(8,128)(2,1)S(1)}, u32[]{:S(2)}, u32[]{:S(2)}) collective-permute-start(bf16[24,384]{1,0:T(8,128)(2,1)S(1)} %get-tuple-element.36), channel_id=1, source_target_pairs={{1,2},{2,1},{3,4},{4,3},{5,6},{6,5},{9,10},{10,9},{11,12},{12,11},... | collective-permute-start | bytes 55304 | tf_op jit(solution)/shard_map/r2_odd_columns/ppermute | solution.py:231
  32.9 3.9 %collective-permute-start.10 = (bf16[26,384]{1,0:T(8,128)(2,1)S(1)}, bf16[26,384]{1,0:T(8,128)(2,1)S(1)}, u32[]{:S(2)}, u32[]{:S(2)}) collective-permute-start(bf16[26,384]{1,0:T(8,128)(2,1)S(1)} %pad_maximum_fusion.8), channel_id=1, source_target_pairs={{0,1},{1,0},{2,3},{3,2},{4,5},{5,4},{6,7},{7,6},{8,9},{9,8},{10,11... | collective-permute-start | bytes 59912 | tf_op jit(solution)/shard_map/r2_low_columns/ppermute | solution.py:231

commit v5 on v4

--- a/solution.py
+++ b/solution.py
@@ -125,73 +125,131 @@
     return flag
 
 
-def own_kernel(rows, mask_ref, tokens_ref, grad_ref, wqkv_ref, wout_ref, query_ref, kv_ref, datt_ref):
-    width = NH * HEAD_SIZE
-    tokens = tokens_ref[...]
-    query = DOT(tokens, wqkv_ref[:, :width], NN).astype(jnp.bfloat16).astype(jnp.float32) * SCALE
-    query_ref[...] = query.astype(jnp.bfloat16)
-    kv_ref[...] = DOT(tokens, wqkv_ref[:, width:], NN).astype(jnp.bfloat16)
-    flag = token_flags(rows, mask_ref, width)
-    datt_ref[...] = (DOT(grad_ref[...], wout_ref[...], NT) * flag).astype(jnp.bfloat16)
-
-
-def attention_kernel(
+def two_heads(pair, own, query, d_att):
+    low = lax.broadcasted_iota(jnp.int32, (own, LANES), 1) < HEAD_SIZE
+    none = jnp.zeros((own, LANES), jnp.bfloat16)
+
+    def stack(field):
+        part = field[:, pair * LANES : (pair + 1) * LANES]
+        return jnp.concatenate([jnp.where(low, part, none), jnp.where(low, none, part)], axis=0)
+
+    return stack(query), stack(d_att)
+
+
+def window_kernel(
     rows,
-    low_x_ref, odd_x_ref, low_y_ref, odd_y_ref, pool_ref, flags_ref, bias_ref, query_ref, kv_ref, datt_ref, wkv_ref,
-    back_ref, dkv_ref, att_ref, dq_ref,
-    x_ref, all_kv_ref, all_dkv_ref,
+    mask_ref, tokens_ref, low_x_ref, odd_x_ref, low_y_ref, odd_y_ref, bias_ref, grad_ref, wqkv_ref, wout_ref,
+    query_ref, datt_ref, datt_t_ref, kv_t_ref, raised_ref, stats_ref, grads_ref,
+    x_ref,
 ):
     width = NH * HEAD_SIZE
-    own = rows.own
-    pooled = jnp.where(flags_ref[...] > 0, 0.0, NEG_FILL)
-    bias = jnp.concatenate([bias_ref[: rows.pool], pooled], axis=0)
-    bias2 = jnp.concatenate([bias, bias], axis=1)
-
+    own, count = rows.own, rows.pool
+    tokens = tokens_ref[...]
     x_ref[...] = jnp.zeros_like(x_ref)
-    for start, ref, count in (
+    x_ref[:own] = tokens
+    for start, ref, size in (
         (rows.low_x, low_x_ref, rows.side),
         (rows.odd_x, odd_x_ref, rows.side),
         (rows.low_y, low_y_ref, rows.edge),
         (rows.odd_y, odd_y_ref, rows.edge),
-        (rows.pool, pool_ref, rows.total - rows.pool),
     ):
-        x_ref[start - own : start - own + count] = ref[:count]
-    all_kv_ref[:own] = kv_ref[...]
-    all_kv_ref[own:] = DOT(x_ref[...], wkv_ref[...], NN).astype(jnp.bfloat16)
-    keys, values = all_kv_ref[:, :width], all_kv_ref[:, width:]
-    query, d_att = query_ref[...], datt_ref[...]
-    keys_t, values_t, d_att_t = keys.T, values.T, d_att.T
-    low = lax.broadcasted_iota(jnp.int32, (own, LANES), 1) < HEAD_SIZE
-    none = jnp.zeros((own, LANES), jnp.bfloat16)
-
+        x_ref[start : start + size] = ref[:size]
+    query = DOT(tokens, wqkv_ref[:, :width], NN).astype(jnp.bfloat16).astype(jnp.float32) * SCALE
+    query = query.astype(jnp.bfloat16)
+    query_ref[...] = query
+    flag = token_flags(rows, mask_ref, width)
+    d_att = (DOT(grad_ref[...], wout_ref[...], NT) * flag).astype(jnp.bfloat16)
+    datt_ref[...] = d_att
+    datt_t_ref[...] = d_att.T
+    kv = DOT(x_ref[...], wqkv_ref[:, width:], NN).astype(jnp.bfloat16)
+    kv_t_ref[...] = kv.T
+    bias = bias_ref[:count]
+    bias2 = jnp.concatenate([bias, bias], axis=1)
+    tops, totals = [], []
     for pair in range(width // LANES):
         lanes = slice(pair * LANES, (pair + 1) * LANES)
-        heads = [slice(pair * LANES + h * HEAD_SIZE, pair * LANES + (h + 1) * HEAD_SIZE) for h in range(2)]
-        k_pair, v_pair = keys[:, lanes], values[:, lanes]
-        q_pair, d_pair = query[:, lanes], d_att[:, lanes]
-        q_two = jnp.concatenate([jnp.where(low, q_pair, none), jnp.where(low, none, q_pair)], axis=0)
-        d_two = jnp.concatenate([jnp.where(low, d_pair, none), jnp.where(low, none, d_pair)], axis=0)
-        scores = DOT(k_pair, q_two, NT) + bias2
+        q_two, d_two = two_heads(pair, own, query, d_att)
+        scores = DOT(kv[:, lanes], q_two, NT) + bias2
         top = jnp.max(scores, axis=0, keepdims=True)
         raised = jnp.exp(scores - top)
-        prob = raised * (1.0 / jnp.sum(raised, axis=0, keepdims=True))
-        prob_half = prob.astype(jnp.bfloat16)
+        raised_ref[pair * count : (pair + 1) * count] = raised
+        grads_ref[pair * count : (pair + 1) * count] = DOT(kv[:, width + pair * LANES : width + (pair + 1) * LANES], d_two, NT)
+        tops.append(top)
+        totals.append(jnp.sum(raised, axis=0, keepdims=True))
+    stats_ref[...] = jnp.concatenate(tops + totals, axis=0)
+
+
+def attention_kernel(
+    rows,
+    blocks, sources,
+    near_ref, far_ref, low_ref, odd_ref, *refs
+):
+    more = len(sources) - 5
+    attention_body(rows, blocks, sources, [near_ref, far_ref, low_ref, odd_ref, *refs[:more]], *refs[more:])
+
+
+def attention_body(
+    rows, blocks, sources, pool_refs,
+    kv_t_ref, raised_ref, stats_ref, grads_ref, query_ref, datt_ref, datt_t_ref, wqkv_ref,
+    back_ref, dkv_ref, att_ref, dq_ref,
+    all_dkv_ref,
+):
+    width = NH * HEAD_SIZE
+    own, count, pairs = rows.own, rows.pool, width // LANES
+    pool = flags = 0.0
+    for index, start, first, count_lines in sources:
+        stack = pool_refs[index][...]
+        shape = (rows.total - rows.pool, stack.shape[0])
+        line = lax.broadcasted_iota(jnp.int32, shape, 0) - first
+        source = lax.broadcasted_iota(jnp.int32, shape, 1) - start
+        spot = line // blocks * (2 * blocks) + line % blocks
+        given = (line >= 0) & (line < count_lines)
+        pick_sum = jnp.where(given & (source == spot), 1.0, 0.0).astype(jnp.bfloat16)
+        pick_flag = jnp.where(given & (source == spot + blocks), 1.0, 0.0).astype(jnp.bfloat16)
+        pool = pool + DOT(pick_sum, stack, NN)
+        flags = flags + DOT(pick_flag, stack[:, :own], NN)
+    pool = pool.astype(jnp.bfloat16)
+    pooled = jnp.where(flags > 0, 0.0, NEG_FILL)
+    pooled2 = jnp.concatenate([pooled, pooled], axis=1)
+    pool_kv = DOT(pool, wqkv_ref[:, width:], NN).astype(jnp.bfloat16)
+    pool_kv_t = pool_kv.T
+    query, d_att, d_att_t, stats = query_ref[...], datt_ref[...], datt_t_ref[...], stats_ref[...]
+
+    for pair in range(pairs):
+        lanes = slice(pair * LANES, (pair + 1) * LANES)
+        value_lanes = slice(width + pair * LANES, width + (pair + 1) * LANES)
+        heads = [slice(pair * LANES + h * HEAD_SIZE, pair * LANES + (h + 1) * HEAD_SIZE) for h in range(2)]
+        q_two, d_two = two_heads(pair, own, query, d_att)
+        scores = DOT(pool_kv[:, lanes], q_two, NT) + pooled2
+        window_top = stats[pair : pair + 1]
+        top = jnp.maximum(window_top, jnp.max(scores, axis=0, keepdims=True))
+        raised = jnp.exp(scores - top)
+        shrink = jnp.exp(window_top - top)
+        scale = 1.0 / (stats[pairs + pair : pairs + pair + 1] * shrink + jnp.sum(raised, axis=0, keepdims=True))
+        window_prob = raised_ref[pair * count : (pair + 1) * count] * (shrink * scale)
+        pool_prob = raised * scale
+        window_half, pool_half = window_prob.astype(jnp.bfloat16), pool_prob.astype(jnp.bfloat16)
         deltas = []
         for h, head in enumerate(heads):
-            part = DOT(values_t[head], prob_half[:, h * own : (h + 1) * own], NN).astype(jnp.bfloat16)
+            mine, value = slice(h * own, (h + 1) * own), slice(width + head.start, width + head.stop)
+            part = DOT(kv_t_ref[value], window_half[:, mine], NN) + DOT(pool_kv_t[value], pool_half[:, mine], NN)
+            part = part.astype(jnp.bfloat16)
             att_ref[head] = part
             deltas.append(
                 jnp.sum(d_att_t[head].astype(jnp.float32) * part.astype(jnp.float32), axis=0, keepdims=True)
             )
         delta = jnp.concatenate(deltas, axis=1)
-        prob_grad = DOT(v_pair, d_two, NT)
-        score_grad = (prob * (prob_grad - delta)).astype(jnp.bfloat16)
+        window_grad = (window_prob * (grads_ref[pair * count : (pair + 1) * count] - delta)).astype(jnp.bfloat16)
+        pool_grad = (pool_prob * (DOT(pool_kv[:, value_lanes], d_two, NT) - delta)).astype(jnp.bfloat16)
+        score_grad = jnp.concatenate([window_grad, pool_grad], axis=0)
+        prob_half = jnp.concatenate([window_half, pool_half], axis=0)
         all_dkv_ref[:, lanes] = DOT(score_grad, q_two, NN).astype(jnp.bfloat16)
-        all_dkv_ref[:, width + pair * LANES : width + (pair + 1) * LANES] = DOT(prob_half, d_two, NN).astype(jnp.bfloat16)
+        all_dkv_ref[:, value_lanes] = DOT(prob_half, d_two, NN).astype(jnp.bfloat16)
         for h, head in enumerate(heads):
-            part = DOT(keys_t[head], score_grad[:, h * own : (h + 1) * own], NN) * SCALE
-            dq_ref[head] = part.astype(jnp.bfloat16)
-    back_ref[...] = DOT(all_dkv_ref[own:], wkv_ref[...], NT).astype(jnp.bfloat16)
+            mine = slice(h * own, (h + 1) * own)
+            part = DOT(kv_t_ref[head], window_grad[:, mine], NN) + DOT(pool_kv_t[head], pool_grad[:, mine], NN)
+            dq_ref[head] = (part * SCALE).astype(jnp.bfloat16)
+    back_ref[...] = DOT(all_dkv_ref[own:], wqkv_ref[:, width:], NT).astype(jnp.bfloat16)
     dkv_ref[...] = all_dkv_ref[:own]
 
 
@@ -220,7 +278,7 @@
         in_specs=in_specs,
         out_specs=tuple(vmem for _ in outs),
         scratch_shapes=[pltpu.VMEM(shape, dtype) for shape, dtype in scratch],
-        compiler_params=pltpu.CompilerParams(vmem_limit_bytes=40 << 20),
+        compiler_params=pltpu.CompilerParams(vmem_limit_bytes=12 << 20),
         cost_estimate=pl.CostEstimate(flops=flops, transcendentals=0, bytes_accessed=moved),
         name=name,
     )(*operands)
@@ -242,11 +300,17 @@
     grad_flat = grad_out.reshape(own, width)
     half, full = jnp.bfloat16, jnp.float32
 
-    first = tokens[:, :REACH].reshape(side, width)
-    last = tokens[:, tile_cols - REACH :].reshape(side, width)
+    macs = own * width * width
+    bias = window_bias(rows, count_y, count_x)
+
+    wide_tokens = lax.optimization_barrier(tokens.astype(full))
+    sent_tokens = wide_tokens.astype(half)
+
+    first = sent_tokens[:, :REACH].reshape(side, width)
+    last = sent_tokens[:, tile_cols - REACH :].reshape(side, width)
     odd_send = jnp.where(even_x, first, last)
     odd_x = swap("r1_odd_columns", odd_send, "gx", pairs_odd(count_x, False))
-    tokens_later, _ = lax.optimization_barrier((tokens, odd_send))
+    tokens_later, _ = lax.optimization_barrier((wide_tokens, odd_send))
     grouped = tokens_later.astype(full).reshape(
         tile_rows // TISSUE_BLOCK, TISSUE_BLOCK, tile_cols // TISSUE_BLOCK, TISSUE_BLOCK, width
     )
@@ -257,10 +321,13 @@
         jnp.concatenate([jnp.where(even_x, last, first), mine], axis=0), "gx", pairs_low(count_x)
     )
     row_pool = jnp.concatenate([mine, low_x[side:]], axis=0)
-    for step in steps_above(count_x, 2):
-        row_pool = jnp.concatenate([row_pool, swap(f"r1_far_columns_{step}", row_pool, "gx", pairs_far(count_x, step))], axis=0)
+    *near_steps, last_step = steps_above(count_x, 2)
+    for step in near_steps:
+        got = swap(f"r1_far_columns_{step}", row_pool, "gx", pairs_far(count_x, step))
+        row_pool = jnp.concatenate([row_pool, got], axis=0)
+    got = swap(f"r1_far_columns_{last_step}", row_pool, "gx", pairs_far(count_x, last_step))
     spread = jnp.concatenate(
-        [low_x[:side].reshape(tile_rows, REACH, width), tokens, odd_x.reshape(tile_rows, REACH, width)], axis=1
+        [low_x[:side].reshape(tile_rows, REACH, width), sent_tokens, odd_x.reshape(tile_rows, REACH, width)], axis=1
     )
     top, bottom = spread[:REACH].reshape(edge, width), spread[tile_rows - REACH :].reshape(edge, width)
     low_y = swap("r1_low_rows",
@@ -269,26 +336,40 @@
     odd_y = swap("r1_odd_rows",
         jnp.concatenate([jnp.where(even_y, top, bottom), mine, low_y[edge:]], axis=0), "gy", pairs_odd(count_y, True)
     )
-    col_pool = jnp.concatenate([mine, low_y[edge:], odd_y[edge:]], axis=0)
+    row_lines, half_lines = count_x * blocks, row_pool.shape[0] // 2
+    sources = [
+        (0, 0, 0, half_lines),
+        (1, 0, half_lines, half_lines),
+        (0, 0, row_lines, blocks),
+        (2, edge, row_lines + blocks, blocks),
+        (3, edge, row_lines + 2 * blocks, 2 * blocks),
+    ]
+    more = []
+    if count_y > 4:
+        col_pool = jnp.concatenate([mine, low_y[edge:], odd_y[edge:]], axis=0)
     for step in steps_above(count_y // 2, 2):
-        col_pool = jnp.concatenate([col_pool, swap(f"r1_far_rows_{step}", col_pool, "gy", window_pairs(count_y, step))], axis=0)
-    pool = jnp.concatenate([row_pool, col_pool], axis=0).reshape(count_x + count_y, 2, blocks, width)
-    spare = ((0, rows.total - rows.used), (0, 0))
-    pool_tokens = jnp.pad(pool[:, 0].reshape(-1, width), spare)
-    flags = jnp.pad(pool[:, 1, :, :own].reshape(-1, own), spare).astype(full)
-
-    macs = own * width * width
-    query, kv, d_att = call(
-        functools.partial(own_kernel, rows), "own", [((own, width), half), ((own, 2 * width), half), ((own, width), half)],
-        [], 8 * macs, 1, block_mask, flat_tokens, grad_flat, w_qkv, w_out,
-    )
-    bias = window_bias(rows, count_y, count_x)
+        more.append(swap(f"r1_far_rows_{step}", col_pool, "gy", window_pairs(count_y, step)))
+        col_pool = jnp.concatenate([col_pool, more[-1]], axis=0)
+        lines = more[-1].shape[0] // 2
+        sources.append((3 + len(more), 0, row_lines + lines, lines))
+    count = rows.pool
+    pairs = width // LANES
+    query, d_att, d_att_t, kv_t, raised, stats, grads = call(
+        functools.partial(window_kernel, rows), "window",
+        [
+            ((own, width), half), ((own, width), half), ((width, own), half), ((2 * width, count), half),
+            ((pairs * count, 2 * own), full), ((2 * pairs, 2 * own), full), ((pairs * count, 2 * own), full),
+        ],
+        [((count, width), half)],
+        22 * macs, 1, block_mask, flat_tokens, low_x, odd_x, low_y, odd_y, bias, grad_flat, w_qkv, w_out,
+    )
     back, d_kv, att, d_query = call(
-        functools.partial(attention_kernel, rows), "attention",
+        functools.partial(attention_kernel, rows, blocks, sources), "attention",
         [((rows.total - own, width), half), ((own, 2 * width), half), ((width, own), half), ((width, own), half)],
-        [((rows.total - own, width), half), ((rows.total, 2 * width), half), ((rows.total, 2 * width), half)],
-        40 * macs, 0, low_x, odd_x, low_y, odd_y, pool_tokens, flags, bias, query, kv, d_att, w_qkv[:, width:],
-    )
+        [((rows.total, 2 * width), half)],
+        26 * macs, 0, row_pool, got, low_y, odd_y, *more, kv_t, raised, stats, grads, query, d_att, d_att_t, w_qkv,
+    )
+
     def piece(start, count):
         return back[start - own : start - own + count]
 

time: 37.7 us -> 36.7 us (0.973)
  local copies, waits for them, and re-layouts: 3.78 us -> 1.16 us
  starting transfers between devices: 19.4 us -> 21 us
  waiting for transfers between devices: 5.81 us -> 4.39 us
  other arithmetic: 2.16 us -> 2.98 us
    ppermute x12, starting transfers between devices: 19.4 us -> 21 us  [swap(): return lax.ppermute(value, axis, moves)]
    ppermute x12, waiting for transfers between devices: 5.81 us -> 4.39 us  [swap(): return lax.ppermute(value, axis, moves)]
    unnamed x15 -> x14, local copies, waits for them, and re-layouts: 1.32 us -> 0.04 us
    slice x3 -> x0, local copies, waits for them, and re-layouts: 1.2 us -> none  [the longest x1 1.18 us: local(): w_qkv[:, width:]]
    convert_element_type x1 -> x2, other arithmetic: 0.01 us -> 1.02 us  [the longest x1 1.01 us: local(): wide_tokens = lax.optimization_barrier(tokens.astype(full))]
    select_n x1, other arithmetic: 0.89 us -> 0.03 us  [local(): jnp.where(even_x, last, first)]
    convert_element_type x1, other arithmetic: 0.01 us -> 0.66 us  [local(): jnp.broadcast_to(block_mask.reshape(blocks, 1), (blocks, width))]
  transfers between devices with their start and end apart: 12 -> 12, of which waited for: 7 -> 8; matrix products, arithmetic and copies ran while one was open for 7% -> 6% of each run, Pallas kernels for 7% -> 9%
where the time goes in v5:
time: 36.7 us; the launch traced here: 36.1 us
  starting transfers between devices  21 us (57%)
  Pallas kernels  5.5 us (15%)
  waiting for transfers between devices  4.39 us (12%)
  other arithmetic  2.98 us (8%)
  local copies, waits for them, and re-layouts  1.16 us (3%)
  between operations  1.06 us (3%)
    ppermute x12, starting transfers between devices, swap(): return lax.ppermute(value, axis, moves)  21 us
    pallas_call x3, Pallas kernels, call(): pl.pallas_call(kernel, out_shape=tuple((jax.ShapeDtypeStruct(shape, dtype...  5.5 us
    ppermute x12, waiting for transfers between devices, swap(): return lax.ppermute(value, axis, moves)  4.39 us
    convert_element_type x1, other arithmetic, local(): wide_tokens = lax.optimization_barrier(tokens.astype(full))  1.01 us
  transfers between devices with their start and end apart: 12, of which 8 were waited for; matrix products, arithmetic and copies ran while one was open for 6% of the time, Pallas kernels for 9%

profile of v5, /device:TPU:0, one launch (start us, length us, event | category | flops | bytes accessed | tf_op | source)
XLA Modules:
  0.0 36.1 jit_solution(7412839982897322937)
XLA Ops:
  0.6 0.0 copy-start.5
  0.6 0.0 copy-start.6
  0.7 0.0 copy-start
  0.7 0.0 copy-start.1
  0.7 0.0 copy-start.2
  0.7 0.0 copy-start.3
  0.7 0.0 copy-start.4
  0.7 1.0 %convert_element_type.100 = f32[8,16,384]{2,1,0:T(8,128)S(1)} convert(bf16[8,16,384]{2,1,0:T(8,128)(2,1)} %param.8) | non-fusion elementwise | flops 49152 | bytes 294912 | tf_op jit(solution)/shard_map/convert_element_type | solution.py:306
  1.8 0.7 %collective-permute-start.3 = (bf16[24,384]{1,0:T(8,128)(2,1)S(1)}, bf16[24,384]{1,0:T(8,128)(2,1)S(1)}, u32[]{:S(2)}, u32[]{:S(2)}) collective-permute-start(bf16[24,384]{1,0:T(8,128)(2,1)S(1)} %select_n.96), channel_id=1, source_target_pairs={{1,2},{2,1},{3,4},{4,3},{5,6},{6,5},{9,10},{10,9},{11,12},{12,11},... | collective-permute-start | bytes 55304 | tf_op jit(solution)/shard_map/r1_odd_columns/ppermute | solution.py:289
  2.6 0.7 %convert_bitcast_fusion = bf16[2]{0:T(256)(128)(2,1)S(1)} fusion(s32[1,2]{1,0:T(1,128)} %mask_ref.3), kind=kLoop, calls=%fused_computation.43 | loop fusion | flops 2 | bytes 12 | tf_op jit(solution)/shard_map/convert_element_type | solution.py:318
  3.2 0.1 broadcast_in_dim.21
  3.3 5.8 %collective-permute-start = (bf16[28,384]{1,0:T(8,128)(2,1)S(1)}, bf16[28,384]{1,0:T(8,128)(2,1)S(1)}, u32[]{:S(2)}, u32[]{:S(2)}) collective-permute-start(bf16[28,384]{1,0:T(8,128)(2,1)S(1)} %pad_maximum_fusion.7), channel_id=1, source_target_pairs={{0,1},{1,0},{2,3},{3,2},{4,5},{5,4},{6,7},{7,6},{8,9},{9,8},{10,11... | collective-permute-start | bytes 64520 | tf_op jit(solution)/shard_map/r1_low_columns/ppermute | solution.py:289
  9.1 0.7 %dynamic-slice_bitcast_fusion = s32[384,2]{0,1:T(2,128)S(1)} fusion(s32[2,2,384,2]{2,3,1,0:T(2,128)} %constant.57.clone, s32[]{:T(128)S(6)} %select_n.105, s32[]{:T(128)S(6)} %select_n.106), kind=kLoop, calls=%fused_computation.39 | loop fusion | bytes 6152 | tf_op jit(solution)/shard_map/squeeze | solution.py:102
  9.9 0.0 copy-done.5
  9.9 0.0 copy-done.6
  9.9 0.2 fusion.4.bias_ref
  10.1 0.0 collective-permute-done.3.odd_x_ref
  10.1 0.8 %collective-permute-done.low_x_ref = bf16[28,384]{1,0:T(8,128)(2,1)S(1)} collective-permute-done((bf16[28,384]{1,0:T(8,128)(2,1)S(1)}, bf16[28,384]{1,0:T(8,128)(2,1)S(1)}, u32[]{:S(2)}, u32[]{:S(2)}) %collective-permute-start) | collective-permute-done | bytes 21536 | tf_op jit(solution)/shard_map/r1_low_columns/ppermute | solution.py:289
  11.0 0.1 broadcast_select_fusion
  11.1 0.1 collective-permute-start.4
  11.2 2.0 %collective-permute-start.1 = (bf16[8,384]{1,0:T(8,128)(2,1)S(1)}, bf16[8,384]{1,0:T(8,128)(2,1)S(1)}, u32[]{:S(2)}, u32[]{:S(2)}) collective-permute-start(bf16[8,384]{1,0:T(8,128)(2,1)S(1)} %pad_maximum_fusion.10), channel_id=1, source_target_pairs={{0,2},{1,3},{2,0},{3,1},{4,6},{5,7},{6,4},{7,5},{8,10},{9,11},{10,... | collective-permute-start | bytes 18440 | tf_op jit(solution)/shard_map/r1_far_columns_2/ppermute | solution.py:289
  13.2 0.0 collective-permute-done.4.low_y_ref.low_ref
  13.3 1.4 %collective-permute-start.5 = (bf16[74,384]{1,0:T(8,128)(2,1)S(1)}, bf16[74,384]{1,0:T(8,128)(2,1)S(1)}, u32[]{:S(2)}, u32[]{:S(2)}) collective-permute-start(bf16[74,384]{1,0:T(8,128)(2,1)S(1)} %pad_maximum_fusion), channel_id=1, source_target_pairs={{0,24},{8,16},{16,8},{24,0},{1,25},{9,17},{17,9},{25,1},{2,26},{10... | collective-permute-start | bytes 170504 | tf_op jit(solution)/shard_map/r1_odd_rows/ppermute | solution.py:289
  14.6 0.3 collective-permute-done.1
  14.9 3.0 %collective-permute-start.2 = (bf16[16,384]{1,0:T(8,128)(2,1)S(1)}, bf16[16,384]{1,0:T(8,128)(2,1)S(1)}, u32[]{:S(2)}, u32[]{:S(2)}) collective-permute-start(bf16[16,384]{1,0:T(8,128)(2,1)S(1)} %pad_maximum_fusion.9.near_ref), channel_id=1, source_target_pairs={{0,4},{1,5},{2,6},{3,7},{4,0},{5,1},{6,2},{7,3},{8,12},{9,13},{10,... | collective-permute-start | bytes 36872 | tf_op jit(solution)/shard_map/r1_far_columns_4/ppermute | solution.py:289
  18.0 0.0 collective-permute-done.5.odd_y_ref.odd_ref
  18.0 0.0 copy-done
  18.0 0.0 copy-done.1
  18.0 0.0 copy-done.2
  18.0 0.0 copy-done.3
  18.0 0.0 copy-done.4
  18.0 1.6 %window.1 = (bf16[128,384]{1,0:T(8,128)(2,1)S(1)}, bf16[128,384]{1,0:T(8,128)(2,1)S(1)}, bf16[384,128]{1,0:T(8,128)(2,1)S(1)}, bf16[768,352]{1,0:T(8,128)(2,1)S(...) custom-call(s32[1,2]{1,0:T(1,128)S(1)} %copy-done.4, bf16[128,384]{1,0:T(8,128)(2,1)S(1)} %bitcast.12, ...), custom_call_target="tpu_custom_call" | custom-call | flops 415236096 | bytes 1723400 | tf_op jit(solution)/shard_map/window/pallas_call | solution.py:275
  19.6 0.1 collective-permute-done.2.far_ref
  19.6 2.4 %attention.1 = (bf16[256,384]{1,0:T(8,128)(2,1)S(1)}, bf16[128,768]{1,0:T(8,128)(2,1)S(1)}, bf16[384,128]{1,0:T(8,128)(2,1)S(1)}, bf16[384,128]{1,0:T(8,128)(2,1)S(1)}) custom-call(bf16[16,384]{1,0:T(8,128)(2,1)S(1)} %pad_maximum_fusion.9.near_ref, bf16[16,384]{1,0:T(8,128)(2,1)S(1)} %collective-permute-done.2.far_ref, ...), custom_call_target="tpu_custom_call" | custom-call | flops 490733568 | bytes 4024320 | tf_op jit(solution)/shard_map/attention/pallas_call | solution.py:275
  22.1 0.6 %collective-permute-start.7 = (bf16[70,384]{1,0:T(8,128)(2,1)S(1)}, bf16[70,384]{1,0:T(8,128)(2,1)S(1)}, u32[]{:S(2)}, u32[]{:S(2)}) collective-permute-start(bf16[70,384]{1,0:T(8,128)(2,1)S(1)} %pad_maximum_fusion.5), channel_id=1, source_target_pairs={{0,24},{8,16},{16,8},{24,0},{1,25},{9,17},{17,9},{25,1},{2,26},{10... | collective-permute-start | bytes 161288 | tf_op jit(solution)/shard_map/r2_odd_rows/ppermute | solution.py:289
  22.7 2.6 %collective-permute-start.6 = (bf16[8,384]{1,0:T(8,128)(2,1)S(1)}, bf16[8,384]{1,0:T(8,128)(2,1)S(1)}, u32[]{:S(2)}, u32[]{:S(2)}) collective-permute-start(bf16[8,384]{1,0:T(8,128)(2,1)S(1)} %slice.121), channel_id=1, source_target_pairs={{0,4},{1,5},{2,6},{3,7},{4,0},{5,1},{6,2},{7,3},{8,12},{9,13},{10,... | collective-permute-start | bytes 18440 | tf_op jit(solution)/shard_map/r2_far_columns_4/ppermute | solution.py:289
  25.3 1.0 %collective-permute-done.7 = bf16[70,384]{1,0:T(8,128)(2,1)S(1)} collective-permute-done((bf16[70,384]{1,0:T(8,128)(2,1)S(1)}, bf16[70,384]{1,0:T(8,128)(2,1)S(1)}, u32[]{:S(2)}, u32[]{:S(2)}) %collective-permute-start.7) | collective-permute-done | bytes 53792 | tf_op jit(solution)/shard_map/r2_odd_rows/ppermute | solution.py:289
  26.3 0.2 collective-permute-start.8
  26.5 0.7 %collective-permute-done.6 = bf16[8,384]{1,0:T(8,128)(2,1)S(1)} collective-permute-done((bf16[8,384]{1,0:T(8,128)(2,1)S(1)}, bf16[8,384]{1,0:T(8,128)(2,1)S(1)}, u32[]{:S(2)}, u32[]{:S(2)}) %collective-permute-start.6) | collective-permute-done | bytes 6176 | tf_op jit(solution)/shard_map/r2_far_columns_4/ppermute | solution.py:289
  27.2 0.4 %collective-permute-done.8 = bf16[68,384]{1,0:T(8,128)(2,1)S(1)} collective-permute-done((bf16[68,384]{1,0:T(8,128)(2,1)S(1)}, bf16[68,384]{1,0:T(8,128)(2,1)S(1)}, u32[]{:S(2)}, u32[]{:S(2)}) %collective-permute-start.8) | collective-permute-done | bytes 52256 | tf_op jit(solution)/shard_map/r2_low_rows/ppermute | solution.py:289
  27.8 2.0 %collective-permute-start.9 = (bf16[4,384]{1,0:T(4,128)(2,1)S(1)}, bf16[4,384]{1,0:T(4,128)(2,1)S(1)}, u32[]{:S(2)}, u32[]{:S(2)}) collective-permute-start(bf16[4,384]{1,0:T(4,128)(2,1)S(1)} %slice.129), channel_id=1, source_target_pairs={{0,2},{1,3},{2,0},{3,1},{4,6},{5,7},{6,4},{7,5},{8,10},{9,11},{10,... | collective-permute-start | bytes 9224 | tf_op jit(solution)/shard_map/r2_far_columns_2/ppermute | solution.py:289
  29.8 0.7 %collective-permute-start.11 = (bf16[24,384]{1,0:T(8,128)(2,1)S(1)}, bf16[24,384]{1,0:T(8,128)(2,1)S(1)}, u32[]{:S(2)}, u32[]{:S(2)}) collective-permute-start(bf16[24,384]{1,0:T(8,128)(2,1)S(1)} %get-tuple-element.44), channel_id=1, source_target_pairs={{1,2},{2,1},{3,4},{4,3},{5,6},{6,5},{9,10},{10,9},{11,12},{12,11},... | collective-permute-start | bytes 55304 | tf_op jit(solution)/shard_map/r2_odd_columns/ppermute | solution.py:289
  30.5 1.0 %collective-permute-done.9 = bf16[4,384]{1,0:T(4,128)(2,1)S(1)} collective-permute-done((bf16[4,384]{1,0:T(4,128)(2,1)S(1)}, bf16[4,384]{1,0:T(4,128)(2,1)S(1)}, u32[]{:S(2)}, u32[]{:S(2)}) %collective-permute-start.9) | collective-permute-done | bytes 3104 | tf_op jit(solution)/shard_map/r2_far_columns_2/ppermute | solution.py:289
  31.5 2.0 %collective-permute-start.10 = (bf16[26,384]{1,0:T(8,128)(2,1)S(1)}, bf16[26,384]{1,0:T(8,128)(2,1)S(1)}, u32[]{:S(2)}, u32[]{:S(2)}) collective-permute-start(bf16[26,384]{1,0:T(8,128)(2,1)S(1)} %pad_maximum_fusion.8), channel_id=1, source_target_pairs={{0,1},{1,0},{2,3},{3,2},{4,5},{5,4},{6,7},{7,6},{8,9},{9,8},{10,11... | collective-permute-start | bytes 59912 | tf_op jit(solution)/shard_map/r2_low_columns/ppermute | solution.py:289
  33.5 1.6 %final.1 = (bf16[128,384]{1,0:T(8,128)(2,1)}, f32[128,384]{1,0:T(8,128)S(1)}) custom-call(s32[1,2]{1,0:T(1,128)S(1)} %copy-done.4, bf16[128,384]{1,0:T(8,128)(2,1)S(1)} %bitcast.13, bf16[128,384]{1,0:T(8,128)(2,1)S(1)} %bitcast.15, bf16[384,128]{1,0:T(8,128)(2,1)S(1)} %get-tuple-element.33.att_ref, bf16[384,128]{1,0:T(8,128)(2,1)S(1)} %get-tuple-element.34.dq_ref, ...), custom_call_target="tpu_custom_call" | custom-call | flops 150994944 | bytes 1769480 | tf_op jit(solution)/shard_map/final/pallas_call | solution.py:275
  35.1 0.0 collective-permute-done.11
  35.2 0.2 collective-permute-done.10
  35.4 0.7 %add_convert_fusion = bf16[8,16,384]{2,1,0:T(8,128)(2,1)} fusion(f32[8,16,384]{2,1,0:T(8,128)S(1)} %select_add_fusion, f32[8,3,384]{2,1,0:T(4,128)S(1)} %reshape.88, f32[16,384]{1,0:T(8,128)S(1)} %broadcast_bitcast_fusion, pred[]{:T(512)S(6)} %not.3), kind=kLoop, calls=%fused_computation.4 | loop fusion | flops 196608 | bytes 356353 | tf_op jit(solution)/shard_map/convert_element_type | solution.py:442
  (50 shorter events, 0.7 us)
Async XLA Ops:
  0.6 9.2 %copy-start.5 = (s32[128]{0:T(128)S(1)}, s32[128]{0:T(128)}, u32[]{:S(2)}) copy-start(s32[128]{0:T(128)} %constant.83) | copy-start | bytes 1540
  0.6 9.2 %copy-start.6 = (s32[128]{0:T(128)S(1)}, s32[128]{0:T(128)}, u32[]{:S(2)}) copy-start(s32[128]{0:T(128)} %constant.84) | copy-start | bytes 1540
  0.7 17.3 %copy-start = (bf16[384,1152]{1,0:T(8,128)(2,1)S(1)}, bf16[384,1152]{1,0:T(8,128)(2,1)}, u32[]{:S(2)}) copy-start(bf16[384,1152]{1,0:T(8,128)(2,1)} %wqkv_ref.3) | copy-start | bytes 2654212
  0.7 17.3 %copy-start.1 = (bf16[384,384]{1,0:T(8,128)(2,1)S(1)}, bf16[384,384]{1,0:T(8,128)(2,1)}, u32[]{:S(2)}) copy-start(bf16[384,384]{1,0:T(8,128)(2,1)} %wout_ref.3) | copy-start | bytes 884740
  0.7 17.3 %copy-start.2 = (bf16[8,16,384]{2,1,0:T(8,128)(2,1)S(1)}, bf16[8,16,384]{2,1,0:T(8,128)(2,1)}, u32[]{:S(2)}) copy-start(bf16[8,16,384]{2,1,0:T(8,128)(2,1)} %param.8) | copy-start | bytes 294916
  0.7 17.3 %copy-start.3 = (bf16[8,16,384]{2,1,0:T(8,128)(2,1)S(1)}, bf16[8,16,384]{2,1,0:T(8,128)(2,1)}, u32[]{:S(2)}) copy-start(bf16[8,16,384]{2,1,0:T(8,128)(2,1)} %param.12) | copy-start | bytes 294916
  0.7 17.3 %copy-start.4 = (s32[1,2]{1,0:T(1,128)S(1)}, s32[1,2]{1,0:T(1,128)}, u32[]{:S(2)}) copy-start(s32[1,2]{1,0:T(1,128)} %mask_ref.3) | copy-start | bytes 28
  1.8 8.3 %collective-permute-start.3 = (bf16[24,384]{1,0:T(8,128)(2,1)S(1)}, bf16[24,384]{1,0:T(8,128)(2,1)S(1)}, u32[]{:S(2)}, u32[]{:S(2)}) collective-permute-start(bf16[24,384]{1,0:T(8,128)(2,1)S(1)} %select_n.96), channel_id=1, source_target_pairs={{1,2},{2,1},{3,4},{4,3},{5,6},{6,5},{9,10},{10,9},{11,12},{12,11},... | collective-permute-start | bytes 55304 | tf_op jit(solution)/shard_map/r1_odd_columns/ppermute | solution.py:289
  3.3 7.6 %collective-permute-start = (bf16[28,384]{1,0:T(8,128)(2,1)S(1)}, bf16[28,384]{1,0:T(8,128)(2,1)S(1)}, u32[]{:S(2)}, u32[]{:S(2)}) collective-permute-start(bf16[28,384]{1,0:T(8,128)(2,1)S(1)} %pad_maximum_fusion.7), channel_id=1, source_target_pairs={{0,1},{1,0},{2,3},{3,2},{4,5},{5,4},{6,7},{7,6},{8,9},{9,8},{10,11... | collective-permute-start | bytes 64520 | tf_op jit(solution)/shard_map/r1_low_columns/ppermute | solution.py:289
  11.1 2.2 %collective-permute-start.4 = (bf16[70,384]{1,0:T(8,128)(2,1)S(1)}, bf16[70,384]{1,0:T(8,128)(2,1)S(1)}, u32[]{:S(2)}, u32[]{:S(2)}) collective-permute-start(bf16[70,384]{1,0:T(8,128)(2,1)S(1)} %pad_maximum_fusion.4), channel_id=1, source_target_pairs={{0,8},{8,0},{16,24},{24,16},{1,9},{9,1},{17,25},{25,17},{2,10},{10... | collective-permute-start | bytes 161288 | tf_op jit(solution)/shard_map/r1_low_rows/ppermute | solution.py:289
  11.2 3.7 %collective-permute-start.1 = (bf16[8,384]{1,0:T(8,128)(2,1)S(1)}, bf16[8,384]{1,0:T(8,128)(2,1)S(1)}, u32[]{:S(2)}, u32[]{:S(2)}) collective-permute-start(bf16[8,384]{1,0:T(8,128)(2,1)S(1)} %pad_maximum_fusion.10), channel_id=1, source_target_pairs={{0,2},{1,3},{2,0},{3,1},{4,6},{5,7},{6,4},{7,5},{8,10},{9,11},{10,... | collective-permute-start | bytes 18440 | tf_op jit(solution)/shard_map/r1_far_columns_2/ppermute | solution.py:289
  13.3 4.7 %collective-permute-start.5 = (bf16[74,384]{1,0:T(8,128)(2,1)S(1)}, bf16[74,384]{1,0:T(8,128)(2,1)S(1)}, u32[]{:S(2)}, u32[]{:S(2)}) collective-permute-start(bf16[74,384]{1,0:T(8,128)(2,1)S(1)} %pad_maximum_fusion), channel_id=1, source_target_pairs={{0,24},{8,16},{16,8},{24,0},{1,25},{9,17},{17,9},{25,1},{2,26},{10... | collective-permute-start | bytes 170504 | tf_op jit(solution)/shard_map/r1_odd_rows/ppermute | solution.py:289
  14.9 4.7 %collective-permute-start.2 = (bf16[16,384]{1,0:T(8,128)(2,1)S(1)}, bf16[16,384]{1,0:T(8,128)(2,1)S(1)}, u32[]{:S(2)}, u32[]{:S(2)}) collective-permute-start(bf16[16,384]{1,0:T(8,128)(2,1)S(1)} %pad_maximum_fusion.9.near_ref), channel_id=1, source_target_pairs={{0,4},{1,5},{2,6},{3,7},{4,0},{5,1},{6,2},{7,3},{8,12},{9,13},{10,... | collective-permute-start | bytes 36872 | tf_op jit(solution)/shard_map/r1_far_columns_4/ppermute | solution.py:289
  22.1 4.2 %collective-permute-start.7 = (bf16[70,384]{1,0:T(8,128)(2,1)S(1)}, bf16[70,384]{1,0:T(8,128)(2,1)S(1)}, u32[]{:S(2)}, u32[]{:S(2)}) collective-permute-start(bf16[70,384]{1,0:T(8,128)(2,1)S(1)} %pad_maximum_fusion.5), channel_id=1, source_target_pairs={{0,24},{8,16},{16,8},{24,0},{1,25},{9,17},{17,9},{25,1},{2,26},{10... | collective-permute-start | bytes 161288 | tf_op jit(solution)/shard_map/r2_odd_rows/ppermute | solution.py:289
  22.7 4.5 %collective-permute-start.6 = (bf16[8,384]{1,0:T(8,128)(2,1)S(1)}, bf16[8,384]{1,0:T(8,128)(2,1)S(1)}, u32[]{:S(2)}, u32[]{:S(2)}) collective-permute-start(bf16[8,384]{1,0:T(8,128)(2,1)S(1)} %slice.121), channel_id=1, source_target_pairs={{0,4},{1,5},{2,6},{3,7},{4,0},{5,1},{6,2},{7,3},{8,12},{9,13},{10,... | collective-permute-start | bytes 18440 | tf_op jit(solution)/shard_map/r2_far_columns_4/ppermute | solution.py:289
  26.3 1.3 %collective-permute-start.8 = (bf16[68,384]{1,0:T(8,128)(2,1)S(1)}, bf16[68,384]{1,0:T(8,128)(2,1)S(1)}, u32[]{:S(2)}, u32[]{:S(2)}) collective-permute-start(bf16[68,384]{1,0:T(8,128)(2,1)S(1)} %pad_maximum_fusion.6), channel_id=1, source_target_pairs={{0,8},{8,0},{16,24},{24,16},{1,9},{9,1},{17,25},{25,17},{2,10},{10... | collective-permute-start | bytes 156680 | tf_op jit(solution)/shard_map/r2_low_rows/ppermute | solution.py:289
  27.8 3.7 %collective-permute-start.9 = (bf16[4,384]{1,0:T(4,128)(2,1)S(1)}, bf16[4,384]{1,0:T(4,128)(2,1)S(1)}, u32[]{:S(2)}, u32[]{:S(2)}) collective-permute-start(bf16[4,384]{1,0:T(4,128)(2,1)S(1)} %slice.129), channel_id=1, source_target_pairs={{0,2},{1,3},{2,0},{3,1},{4,6},{5,7},{6,4},{7,5},{8,10},{9,11},{10,... | collective-permute-start | bytes 9224 | tf_op jit(solution)/shard_map/r2_far_columns_2/ppermute | solution.py:289
  29.8 5.3 %collective-permute-start.11 = (bf16[24,384]{1,0:T(8,128)(2,1)S(1)}, bf16[24,384]{1,0:T(8,128)(2,1)S(1)}, u32[]{:S(2)}, u32[]{:S(2)}) collective-permute-start(bf16[24,384]{1,0:T(8,128)(2,1)S(1)} %get-tuple-element.44), channel_id=1, source_target_pairs={{1,2},{2,1},{3,4},{4,3},{5,6},{6,5},{9,10},{10,9},{11,12},{12,11},... | collective-permute-start | bytes 55304 | tf_op jit(solution)/shard_map/r2_odd_columns/ppermute | solution.py:289
  31.5 3.9 %collective-permute-start.10 = (bf16[26,384]{1,0:T(8,128)(2,1)S(1)}, bf16[26,384]{1,0:T(8,128)(2,1)S(1)}, u32[]{:S(2)}, u32[]{:S(2)}) collective-permute-start(bf16[26,384]{1,0:T(8,128)(2,1)S(1)} %pad_maximum_fusion.8), channel_id=1, source_target_pairs={{0,1},{1,0},{2,3},{3,2},{4,5},{5,4},{6,7},{7,6},{8,9},{9,8},{10,11... | collective-permute-start | bytes 59912 | tf_op jit(solution)/shard_map/r2_low_columns/ppermute | solution.py:289

commit v6 on v5

--- a/solution.py
+++ b/solution.py
@@ -123,6 +123,23 @@
         value = mask_ref[b // block_cols, b % block_cols].astype(jnp.float32)
         flag = jnp.where(block == b, value, flag)
     return flag
+
+
+def gather_kernel(rows, blocks, mask_ref, tokens_ref, sent_ref, mine_ref):
+    tokens = tokens_ref[...]
+    sent_ref[...] = tokens
+    shape = (blocks, rows.own)
+    line, token = lax.broadcasted_iota(jnp.int32, shape, 0), lax.broadcasted_iota(jnp.int32, shape, 1)
+    block_cols = rows.tile_cols // TISSUE_BLOCK
+    block = token // (rows.tile_cols * TISSUE_BLOCK) * block_cols + token % rows.tile_cols // TISSUE_BLOCK
+    pick = jnp.where(block == line, 1.0 / TISSUE_BLOCK, 0.0).astype(jnp.bfloat16)
+    sums = DOT(pick, tokens, NN)
+    row = lax.broadcasted_iota(jnp.int32, sums.shape, 0)
+    marks = jnp.zeros_like(sums)
+    for b in range(blocks):
+        r, c = b // block_cols, b % block_cols
+        marks = jnp.where(row == b, mask_ref[r : r + 1, c : c + 1].astype(jnp.float32), marks)
+    mine_ref[...] = jnp.concatenate([sums, marks], axis=0).astype(jnp.bfloat16)
 
 
 def two_heads(pair, own, query, d_att):
@@ -303,20 +320,17 @@
     macs = own * width * width
     bias = window_bias(rows, count_y, count_x)
 
-    wide_tokens = lax.optimization_barrier(tokens.astype(full))
-    sent_tokens = wide_tokens.astype(half)
+    sent_tokens, mine = call(
+        functools.partial(gather_kernel, rows, blocks), "gather", [((own, width), half), ((2 * blocks, width), half)],
+        [], 1, 0, block_mask, flat_tokens,
+    )
+    sent_tokens = sent_tokens.reshape(tile_rows, tile_cols, width)
 
     first = sent_tokens[:, :REACH].reshape(side, width)
     last = sent_tokens[:, tile_cols - REACH :].reshape(side, width)
     odd_send = jnp.where(even_x, first, last)
     odd_x = swap("r1_odd_columns", odd_send, "gx", pairs_odd(count_x, False))
-    tokens_later, _ = lax.optimization_barrier((wide_tokens, odd_send))
-    grouped = tokens_later.astype(full).reshape(
-        tile_rows // TISSUE_BLOCK, TISSUE_BLOCK, tile_cols // TISSUE_BLOCK, TISSUE_BLOCK, width
-    )
-    sums = (jnp.sum(grouped, axis=(1, 3)) / TISSUE_BLOCK).reshape(blocks, width).astype(half)
-    marks = jnp.broadcast_to(block_mask.reshape(blocks, 1), (blocks, width)).astype(half)
-    mine = jnp.concatenate([sums, marks], axis=0)
+    mine, _ = lax.optimization_barrier((mine, odd_send))
     low_x = swap("r1_low_columns",
         jnp.concatenate([jnp.where(even_x, last, first), mine], axis=0), "gx", pairs_low(count_x)
     )

time: 36.7 us -> 36.6 us (level)
  local copies, waits for them, and re-layouts: 1.16 us -> 2.7 us
  other arithmetic: 2.98 us -> 1.91 us
  waiting for transfers between devices: 4.39 us -> 3.76 us
    convert_element_type x4 -> x0, other arithmetic: 1.69 us -> none  [the longest x1 1.01 us: local(): wide_tokens = lax.optimization_barrier(tokens.astype(full))]
    unnamed x14, local copies, waits for them, and re-layouts: 0.04 us -> 1.65 us
    select_n x1, other arithmetic: 0.22 us -> 0.89 us  [window_bias(): return jnp.where(near & inside, 0.0, NEG_FILL).astype(jnp.float32)]
    ppermute x12, waiting for transfers between devices: 4.39 us -> 3.76 us  [swap(): return lax.ppermute(value, axis, moves)]
    pallas_call x3 -> x4, Pallas kernels: 5.5 us -> 5.64 us  [call(): pl.pallas_call(kernel, out_shape=tuple((jax.ShapeDtypeStruct(shape, dtype...]
  transfers between devices with their start and end apart: 12 -> 12, of which waited for: 8 -> 8; matrix products, arithmetic and copies ran while one was open for 6% -> 5% of each run, Pallas kernels for 9% -> 9%
where the time goes in v6:
time: 36.6 us; the launch traced here: 36 us
  starting transfers between devices  21 us (57%)
  Pallas kernels  5.64 us (15%)
  waiting for transfers between devices  3.76 us (10%)
  local copies, waits for them, and re-layouts  2.7 us (7%)
  other arithmetic  1.91 us (5%)
  between operations  0.99 us (3%)
    ppermute x12, starting transfers between devices, swap(): return lax.ppermute(value, axis, moves)  21 us
    pallas_call x4, Pallas kernels, call(): pl.pallas_call(kernel, out_shape=tuple((jax.ShapeDtypeStruct(shape, dtype...  5.64 us
    ppermute x12, waiting for transfers between devices, swap(): return lax.ppermute(value, axis, moves)  3.76 us
    unnamed x14, local copies, waits for them, and re-layouts  1.65 us
    select_n x1, other arithmetic, window_bias(): return jnp.where(near & inside, 0.0, NEG_FILL).astype(jnp.float32)  0.89 us
  transfers between devices with their start and end apart: 12, of which 8 were waited for; matrix products, arithmetic and copies ran while one was open for 5% of the time, Pallas kernels for 9%

profile of v6, /device:TPU:0, one launch (start us, length us, event | category | flops | bytes accessed | tf_op | source)
XLA Modules:
  0.0 36.0 jit_solution(16113247751704609633)
XLA Ops:
  0.6 0.0 copy-start.1
  0.6 0.0 copy-start
  0.7 0.0 copy-start.2
  0.7 1.0 %copy-done.2 = bf16[8,16,384]{2,1,0:T(8,128)(2,1)S(1)} copy-done((bf16[8,16,384]{2,1,0:T(8,128)(2,1)S(1)}, bf16[8,16,384]{2,1,0:T(8,128)(2,1)}, u32[]{:S(2)}) %copy-start.2) | copy-done | bytes 98328
  1.6 0.0 copy-start.5
  1.7 0.7 %copy-done.5 = s32[1,2]{1,0:T(1,128)S(1)} copy-done((s32[1,2]{1,0:T(1,128)S(1)}, s32[1,2]{1,0:T(1,128)}, u32[]{:S(2)}) %copy-start.5) | copy-done | bytes 32
  2.3 0.0 copy-start.3
  2.3 0.0 copy-start.4
  2.3 0.0 copy-start.6
  2.3 0.1 gather.1
  2.5 0.7 %collective-permute-start.3 = (bf16[24,384]{1,0:T(8,128)(2,1)S(1)}, bf16[24,384]{1,0:T(8,128)(2,1)S(1)}, u32[]{:S(2)}, u32[]{:S(2)}) collective-permute-start(bf16[24,384]{1,0:T(8,128)(2,1)S(1)} %select_n.96), channel_id=1, source_target_pairs={{1,2},{2,1},{3,4},{4,3},{5,6},{6,5},{9,10},{10,9},{11,12},{12,11},... | collective-permute-start | bytes 55304 | tf_op jit(solution)/shard_map/r1_odd_columns/ppermute | solution.py:306
  3.2 5.8 %collective-permute-start = (bf16[28,384]{1,0:T(8,128)(2,1)S(1)}, bf16[28,384]{1,0:T(8,128)(2,1)S(1)}, u32[]{:S(2)}, u32[]{:S(2)}) collective-permute-start(bf16[28,384]{1,0:T(8,128)(2,1)S(1)} %pad_maximum_fusion.7), channel_id=1, source_target_pairs={{0,1},{1,0},{2,3},{3,2},{4,5},{5,4},{6,7},{7,6},{8,9},{9,8},{10,11... | collective-permute-start | bytes 64520 | tf_op jit(solution)/shard_map/r1_low_columns/ppermute | solution.py:306
  9.0 0.7 %dynamic-slice_bitcast_fusion = s32[384,2]{0,1:T(2,128)S(1)} fusion(s32[2,2,384,2]{2,3,1,0:T(2,128)} %constant.55.clone, s32[]{:T(128)S(6)} %select_n.105, s32[]{:T(128)S(6)} %select_n.106), kind=kLoop, calls=%fused_computation.38 | loop fusion | bytes 6152 | tf_op jit(solution)/shard_map/squeeze | solution.py:102
  9.8 0.9 %fusion.4.bias_ref = f32[384,128]{1,0:T(8,128)S(1)} fusion(s32[128]{0:T(128)} %constant.82, s32[128]{0:T(128)} %constant.81, s32[384]{0:T(512)S(1)} %get-tuple-element.47, s32[384]{0:T(512)S(1)} %get-tuple-element.46, pred[384]{0:T(512)(128)(4,1)S(1)} %and_reduce_fusion), kind=kLoop, calls=%fused_computation.8 | loop fusion | flops 442368 | bytes 201088 | tf_op jit(solution)/shard_map/jit(_where)/select_n | solution.py:108
  10.7 0.0 collective-permute-done.3.odd_x_ref
  10.7 0.1 collective-permute-done.low_x_ref
  10.9 0.1 broadcast_select_fusion
  11.0 0.1 collective-permute-start.4
  11.1 2.0 %collective-permute-start.1 = (bf16[8,384]{1,0:T(8,128)(2,1)S(1)}, bf16[8,384]{1,0:T(8,128)(2,1)S(1)}, u32[]{:S(2)}, u32[]{:S(2)}) collective-permute-start(bf16[8,384]{1,0:T(8,128)(2,1)S(1)} %pad_maximum_fusion.10), channel_id=1, source_target_pairs={{0,2},{1,3},{2,0},{3,1},{4,6},{5,7},{6,4},{7,5},{8,10},{9,11},{10,... | collective-permute-start | bytes 18440 | tf_op jit(solution)/shard_map/r1_far_columns_2/ppermute | solution.py:306
  13.1 0.0 collective-permute-done.4.low_y_ref.low_ref
  13.2 1.4 %collective-permute-start.5 = (bf16[74,384]{1,0:T(8,128)(2,1)S(1)}, bf16[74,384]{1,0:T(8,128)(2,1)S(1)}, u32[]{:S(2)}, u32[]{:S(2)}) collective-permute-start(bf16[74,384]{1,0:T(8,128)(2,1)S(1)} %pad_maximum_fusion), channel_id=1, source_target_pairs={{0,24},{8,16},{16,8},{24,0},{1,25},{9,17},{17,9},{25,1},{2,26},{10... | collective-permute-start | bytes 170504 | tf_op jit(solution)/shard_map/r1_odd_rows/ppermute | solution.py:306
  14.5 0.3 collective-permute-done.1
  14.8 3.0 %collective-permute-start.2 = (bf16[16,384]{1,0:T(8,128)(2,1)S(1)}, bf16[16,384]{1,0:T(8,128)(2,1)S(1)}, u32[]{:S(2)}, u32[]{:S(2)}) collective-permute-start(bf16[16,384]{1,0:T(8,128)(2,1)S(1)} %pad_maximum_fusion.9.near_ref), channel_id=1, source_target_pairs={{0,4},{1,5},{2,6},{3,7},{4,0},{5,1},{6,2},{7,3},{8,12},{9,13},{10,... | collective-permute-start | bytes 36872 | tf_op jit(solution)/shard_map/r1_far_columns_4/ppermute | solution.py:306
  17.9 0.0 collective-permute-done.5.odd_y_ref.odd_ref
  17.9 0.0 copy-done.1
  17.9 0.0 copy-done
  17.9 0.0 copy-done.3
  17.9 0.0 copy-done.4
  17.9 0.0 copy-done.6
  17.9 1.6 %window.1 = (bf16[128,384]{1,0:T(8,128)(2,1)S(1)}, bf16[128,384]{1,0:T(8,128)(2,1)S(1)}, bf16[384,128]{1,0:T(8,128)(2,1)S(1)}, bf16[768,352]{1,0:T(8,128)(2,1)S(...) custom-call(s32[1,2]{1,0:T(1,128)S(1)} %copy-done.6, bf16[128,384]{1,0:T(8,128)(2,1)S(1)} %bitcast.10, ...), custom_call_target="tpu_custom_call" | custom-call | flops 415236096 | bytes 1723400 | tf_op jit(solution)/shard_map/window/pallas_call | solution.py:292
  19.4 0.1 collective-permute-done.2.far_ref
  19.5 2.4 %attention.1 = (bf16[256,384]{1,0:T(8,128)(2,1)S(1)}, bf16[128,768]{1,0:T(8,128)(2,1)S(1)}, bf16[384,128]{1,0:T(8,128)(2,1)S(1)}, bf16[384,128]{1,0:T(8,128)(2,1)S(1)}) custom-call(bf16[16,384]{1,0:T(8,128)(2,1)S(1)} %pad_maximum_fusion.9.near_ref, bf16[16,384]{1,0:T(8,128)(2,1)S(1)} %collective-permute-done.2.far_ref, ...), custom_call_target="tpu_custom_call" | custom-call | flops 490733568 | bytes 4024320 | tf_op jit(solution)/shard_map/attention/pallas_call | solution.py:292
  22.0 0.6 %collective-permute-start.7 = (bf16[70,384]{1,0:T(8,128)(2,1)S(1)}, bf16[70,384]{1,0:T(8,128)(2,1)S(1)}, u32[]{:S(2)}, u32[]{:S(2)}) collective-permute-start(bf16[70,384]{1,0:T(8,128)(2,1)S(1)} %pad_maximum_fusion.5), channel_id=1, source_target_pairs={{0,24},{8,16},{16,8},{24,0},{1,25},{9,17},{17,9},{25,1},{2,26},{10... | collective-permute-start | bytes 161288 | tf_op jit(solution)/shard_map/r2_odd_rows/ppermute | solution.py:306
  22.6 2.6 %collective-permute-start.6 = (bf16[8,384]{1,0:T(8,128)(2,1)S(1)}, bf16[8,384]{1,0:T(8,128)(2,1)S(1)}, u32[]{:S(2)}, u32[]{:S(2)}) collective-permute-start(bf16[8,384]{1,0:T(8,128)(2,1)S(1)} %slice.121), channel_id=1, source_target_pairs={{0,4},{1,5},{2,6},{3,7},{4,0},{5,1},{6,2},{7,3},{8,12},{9,13},{10,... | collective-permute-start | bytes 18440 | tf_op jit(solution)/shard_map/r2_far_columns_4/ppermute | solution.py:306
  25.1 1.0 %collective-permute-done.7 = bf16[70,384]{1,0:T(8,128)(2,1)S(1)} collective-permute-done((bf16[70,384]{1,0:T(8,128)(2,1)S(1)}, bf16[70,384]{1,0:T(8,128)(2,1)S(1)}, u32[]{:S(2)}, u32[]{:S(2)}) %collective-permute-start.7) | collective-permute-done | bytes 53792 | tf_op jit(solution)/shard_map/r2_odd_rows/ppermute | solution.py:306
  26.2 0.2 collective-permute-start.8
  26.4 0.7 %collective-permute-done.6 = bf16[8,384]{1,0:T(8,128)(2,1)S(1)} collective-permute-done((bf16[8,384]{1,0:T(8,128)(2,1)S(1)}, bf16[8,384]{1,0:T(8,128)(2,1)S(1)}, u32[]{:S(2)}, u32[]{:S(2)}) %collective-permute-start.6) | collective-permute-done | bytes 6176 | tf_op jit(solution)/shard_map/r2_far_columns_4/ppermute | solution.py:306
  27.1 0.4 %collective-permute-done.8 = bf16[68,384]{1,0:T(8,128)(2,1)S(1)} collective-permute-done((bf16[68,384]{1,0:T(8,128)(2,1)S(1)}, bf16[68,384]{1,0:T(8,128)(2,1)S(1)}, u32[]{:S(2)}, u32[]{:S(2)}) %collective-permute-start.8) | collective-permute-done | bytes 52256 | tf_op jit(solution)/shard_map/r2_low_rows/ppermute | solution.py:306
  27.7 2.0 %collective-permute-start.9 = (bf16[4,384]{1,0:T(4,128)(2,1)S(1)}, bf16[4,384]{1,0:T(4,128)(2,1)S(1)}, u32[]{:S(2)}, u32[]{:S(2)}) collective-permute-start(bf16[4,384]{1,0:T(4,128)(2,1)S(1)} %slice.129), channel_id=1, source_target_pairs={{0,2},{1,3},{2,0},{3,1},{4,6},{5,7},{6,4},{7,5},{8,10},{9,11},{10,... | collective-permute-start | bytes 9224 | tf_op jit(solution)/shard_map/r2_far_columns_2/ppermute | solution.py:306
  29.7 0.7 %collective-permute-start.11 = (bf16[24,384]{1,0:T(8,128)(2,1)S(1)}, bf16[24,384]{1,0:T(8,128)(2,1)S(1)}, u32[]{:S(2)}, u32[]{:S(2)}) collective-permute-start(bf16[24,384]{1,0:T(8,128)(2,1)S(1)} %get-tuple-element.48), channel_id=1, source_target_pairs={{1,2},{2,1},{3,4},{4,3},{5,6},{6,5},{9,10},{10,9},{11,12},{12,11},... | collective-permute-start | bytes 55304 | tf_op jit(solution)/shard_map/r2_odd_columns/ppermute | solution.py:306
  30.4 1.0 %collective-permute-done.9 = bf16[4,384]{1,0:T(4,128)(2,1)S(1)} collective-permute-done((bf16[4,384]{1,0:T(4,128)(2,1)S(1)}, bf16[4,384]{1,0:T(4,128)(2,1)S(1)}, u32[]{:S(2)}, u32[]{:S(2)}) %collective-permute-start.9) | collective-permute-done | bytes 3104 | tf_op jit(solution)/shard_map/r2_far_columns_2/ppermute | solution.py:306
  31.4 2.0 %collective-permute-start.10 = (bf16[26,384]{1,0:T(8,128)(2,1)S(1)}, bf16[26,384]{1,0:T(8,128)(2,1)S(1)}, u32[]{:S(2)}, u32[]{:S(2)}) collective-permute-start(bf16[26,384]{1,0:T(8,128)(2,1)S(1)} %pad_maximum_fusion.8), channel_id=1, source_target_pairs={{0,1},{1,0},{2,3},{3,2},{4,5},{5,4},{6,7},{7,6},{8,9},{9,8},{10,11... | collective-permute-start | bytes 59912 | tf_op jit(solution)/shard_map/r2_low_columns/ppermute | solution.py:306
  33.4 1.6 %final.1 = (bf16[128,384]{1,0:T(8,128)(2,1)}, f32[128,384]{1,0:T(8,128)S(1)}) custom-call(s32[1,2]{1,0:T(1,128)S(1)} %copy-done.6, bf16[128,384]{1,0:T(8,128)(2,1)S(1)} %bitcast.11, bf16[128,384]{1,0:T(8,128)(2,1)S(1)} %bitcast.13, bf16[384,128]{1,0:T(8,128)(2,1)S(1)} %get-tuple-element.37.att_ref, bf16[384,128]{1,0:T(8,128)(2,1)S(1)} %get-tuple-element.38.dq_ref, ...), custom_call_target="tpu_custom_call" | custom-call | flops 150994944 | bytes 1769480 | tf_op jit(solution)/shard_map/final/pallas_call | solution.py:292
  35.0 0.0 collective-permute-done.11
  35.1 0.2 collective-permute-done.10
  35.3 0.7 %add_convert_fusion = bf16[8,16,384]{2,1,0:T(8,128)(2,1)} fusion(f32[8,16,384]{2,1,0:T(8,128)S(1)} %select_add_fusion, f32[8,3,384]{2,1,0:T(4,128)S(1)} %reshape.81, f32[16,384]{1,0:T(8,128)S(1)} %broadcast_bitcast_fusion, pred[]{:T(512)S(6)} %not.3), kind=kLoop, calls=%fused_computation.4 | loop fusion | flops 196608 | bytes 356353 | tf_op jit(solution)/shard_map/convert_element_type | solution.py:456
  (46 shorter events, 0.6 us)
Async XLA Ops:
  0.6 17.2 %copy-start.1 = (bf16[384,384]{1,0:T(8,128)(2,1)S(1)}, bf16[384,384]{1,0:T(8,128)(2,1)}, u32[]{:S(2)}) copy-start(bf16[384,384]{1,0:T(8,128)(2,1)} %wout_ref.3) | copy-start | bytes 884740
  0.6 17.2 %copy-start = (bf16[384,1152]{1,0:T(8,128)(2,1)S(1)}, bf16[384,1152]{1,0:T(8,128)(2,1)}, u32[]{:S(2)}) copy-start(bf16[384,1152]{1,0:T(8,128)(2,1)} %wqkv_ref.3) | copy-start | bytes 2654212
  0.7 1.0 %copy-start.2 = (bf16[8,16,384]{2,1,0:T(8,128)(2,1)S(1)}, bf16[8,16,384]{2,1,0:T(8,128)(2,1)}, u32[]{:S(2)}) copy-start(bf16[8,16,384]{2,1,0:T(8,128)(2,1)} %param.8) | copy-start | bytes 294916
  1.6 0.7 %copy-start.5 = (s32[1,2]{1,0:T(1,128)S(1)}, s32[1,2]{1,0:T(1,128)}, u32[]{:S(2)}) copy-start(s32[1,2]{1,0:T(1,128)} %mask_ref.5) | copy-start | bytes 28
  2.3 15.6 %copy-start.3 = (bf16[8,16,384]{2,1,0:T(8,128)(2,1)S(1)}, bf16[8,16,384]{2,1,0:T(8,128)(2,1)}, u32[]{:S(2)}) copy-start(bf16[8,16,384]{2,1,0:T(8,128)(2,1)} %param.8) | copy-start | bytes 294916
  2.3 15.6 %copy-start.4 = (bf16[8,16,384]{2,1,0:T(8,128)(2,1)S(1)}, bf16[8,16,384]{2,1,0:T(8,128)(2,1)}, u32[]{:S(2)}) copy-start(bf16[8,16,384]{2,1,0:T(8,128)(2,1)} %param.12) | copy-start | bytes 294916
  2.3 15.6 %copy-start.6 = (s32[1,2]{1,0:T(1,128)S(1)}, s32[1,2]{1,0:T(1,128)}, u32[]{:S(2)}) copy-start(s32[1,2]{1,0:T(1,128)} %mask_ref.5) | copy-start | bytes 28
  2.5 8.2 %collective-permute-start.3 = (bf16[24,384]{1,0:T(8,128)(2,1)S(1)}, bf16[24,384]{1,0:T(8,128)(2,1)S(1)}, u32[]{:S(2)}, u32[]{:S(2)}) collective-permute-start(bf16[24,384]{1,0:T(8,128)(2,1)S(1)} %select_n.96), channel_id=1, source_target_pairs={{1,2},{2,1},{3,4},{4,3},{5,6},{6,5},{9,10},{10,9},{11,12},{12,11},... | collective-permute-start | bytes 55304 | tf_op jit(solution)/shard_map/r1_odd_columns/ppermute | solution.py:306
  3.2 7.6 %collective-permute-start = (bf16[28,384]{1,0:T(8,128)(2,1)S(1)}, bf16[28,384]{1,0:T(8,128)(2,1)S(1)}, u32[]{:S(2)}, u32[]{:S(2)}) collective-permute-start(bf16[28,384]{1,0:T(8,128)(2,1)S(1)} %pad_maximum_fusion.7), channel_id=1, source_target_pairs={{0,1},{1,0},{2,3},{3,2},{4,5},{5,4},{6,7},{7,6},{8,9},{9,8},{10,11... | collective-permute-start | bytes 64520 | tf_op jit(solution)/shard_map/r1_low_columns/ppermute | solution.py:306
  11.0 2.2 %collective-permute-start.4 = (bf16[70,384]{1,0:T(8,128)(2,1)S(1)}, bf16[70,384]{1,0:T(8,128)(2,1)S(1)}, u32[]{:S(2)}, u32[]{:S(2)}) collective-permute-start(bf16[70,384]{1,0:T(8,128)(2,1)S(1)} %pad_maximum_fusion.4), channel_id=1, source_target_pairs={{0,8},{8,0},{16,24},{24,16},{1,9},{9,1},{17,25},{25,17},{2,10},{10... | collective-permute-start | bytes 161288 | tf_op jit(solution)/shard_map/r1_low_rows/ppermute | solution.py:306
  11.1 3.7 %collective-permute-start.1 = (bf16[8,384]{1,0:T(8,128)(2,1)S(1)}, bf16[8,384]{1,0:T(8,128)(2,1)S(1)}, u32[]{:S(2)}, u32[]{:S(2)}) collective-permute-start(bf16[8,384]{1,0:T(8,128)(2,1)S(1)} %pad_maximum_fusion.10), channel_id=1, source_target_pairs={{0,2},{1,3},{2,0},{3,1},{4,6},{5,7},{6,4},{7,5},{8,10},{9,11},{10,... | collective-permute-start | bytes 18440 | tf_op jit(solution)/shard_map/r1_far_columns_2/ppermute | solution.py:306
  13.2 4.7 %collective-permute-start.5 = (bf16[74,384]{1,0:T(8,128)(2,1)S(1)}, bf16[74,384]{1,0:T(8,128)(2,1)S(1)}, u32[]{:S(2)}, u32[]{:S(2)}) collective-permute-start(bf16[74,384]{1,0:T(8,128)(2,1)S(1)} %pad_maximum_fusion), channel_id=1, source_target_pairs={{0,24},{8,16},{16,8},{24,0},{1,25},{9,17},{17,9},{25,1},{2,26},{10... | collective-permute-start | bytes 170504 | tf_op jit(solution)/shard_map/r1_odd_rows/ppermute | solution.py:306
  14.8 4.7 %collective-permute-start.2 = (bf16[16,384]{1,0:T(8,128)(2,1)S(1)}, bf16[16,384]{1,0:T(8,128)(2,1)S(1)}, u32[]{:S(2)}, u32[]{:S(2)}) collective-permute-start(bf16[16,384]{1,0:T(8,128)(2,1)S(1)} %pad_maximum_fusion.9.near_ref), channel_id=1, source_target_pairs={{0,4},{1,5},{2,6},{3,7},{4,0},{5,1},{6,2},{7,3},{8,12},{9,13},{10,... | collective-permute-start | bytes 36872 | tf_op jit(solution)/shard_map/r1_far_columns_4/ppermute | solution.py:306
  22.0 4.2 %collective-permute-start.7 = (bf16[70,384]{1,0:T(8,128)(2,1)S(1)}, bf16[70,384]{1,0:T(8,128)(2,1)S(1)}, u32[]{:S(2)}, u32[]{:S(2)}) collective-permute-start(bf16[70,384]{1,0:T(8,128)(2,1)S(1)} %pad_maximum_fusion.5), channel_id=1, source_target_pairs={{0,24},{8,16},{16,8},{24,0},{1,25},{9,17},{17,9},{25,1},{2,26},{10... | collective-permute-start | bytes 161288 | tf_op jit(solution)/shard_map/r2_odd_rows/ppermute | solution.py:306
  22.6 4.5 %collective-permute-start.6 = (bf16[8,384]{1,0:T(8,128)(2,1)S(1)}, bf16[8,384]{1,0:T(8,128)(2,1)S(1)}, u32[]{:S(2)}, u32[]{:S(2)}) collective-permute-start(bf16[8,384]{1,0:T(8,128)(2,1)S(1)} %slice.121), channel_id=1, source_target_pairs={{0,4},{1,5},{2,6},{3,7},{4,0},{5,1},{6,2},{7,3},{8,12},{9,13},{10,... | collective-permute-start | bytes 18440 | tf_op jit(solution)/shard_map/r2_far_columns_4/ppermute | solution.py:306
  26.2 1.3 %collective-permute-start.8 = (bf16[68,384]{1,0:T(8,128)(2,1)S(1)}, bf16[68,384]{1,0:T(8,128)(2,1)S(1)}, u32[]{:S(2)}, u32[]{:S(2)}) collective-permute-start(bf16[68,384]{1,0:T(8,128)(2,1)S(1)} %pad_maximum_fusion.6), channel_id=1, source_target_pairs={{0,8},{8,0},{16,24},{24,16},{1,9},{9,1},{17,25},{25,17},{2,10},{10... | collective-permute-start | bytes 156680 | tf_op jit(solution)/shard_map/r2_low_rows/ppermute | solution.py:306
  27.7 3.7 %collective-permute-start.9 = (bf16[4,384]{1,0:T(4,128)(2,1)S(1)}, bf16[4,384]{1,0:T(4,128)(2,1)S(1)}, u32[]{:S(2)}, u32[]{:S(2)}) collective-permute-start(bf16[4,384]{1,0:T(4,128)(2,1)S(1)} %slice.129), channel_id=1, source_target_pairs={{0,2},{1,3},{2,0},{3,1},{4,6},{5,7},{6,4},{7,5},{8,10},{9,11},{10,... | collective-permute-start | bytes 9224 | tf_op jit(solution)/shard_map/r2_far_columns_2/ppermute | solution.py:306
  29.7 5.3 %collective-permute-start.11 = (bf16[24,384]{1,0:T(8,128)(2,1)S(1)}, bf16[24,384]{1,0:T(8,128)(2,1)S(1)}, u32[]{:S(2)}, u32[]{:S(2)}) collective-permute-start(bf16[24,384]{1,0:T(8,128)(2,1)S(1)} %get-tuple-element.48), channel_id=1, source_target_pairs={{1,2},{2,1},{3,4},{4,3},{5,6},{6,5},{9,10},{10,9},{11,12},{12,11},... | collective-permute-start | bytes 55304 | tf_op jit(solution)/shard_map/r2_odd_columns/ppermute | solution.py:306
  31.4 3.9 %collective-permute-start.10 = (bf16[26,384]{1,0:T(8,128)(2,1)S(1)}, bf16[26,384]{1,0:T(8,128)(2,1)S(1)}, u32[]{:S(2)}, u32[]{:S(2)}) collective-permute-start(bf16[26,384]{1,0:T(8,128)(2,1)S(1)} %pad_maximum_fusion.8), channel_id=1, source_target_pairs={{0,1},{1,0},{2,3},{3,2},{4,5},{5,4},{6,7},{7,6},{8,9},{9,8},{10,11... | collective-permute-start | bytes 59912 | tf_op jit(solution)/shard_map/r2_low_columns/ppermute | solution.py:306
